TPU v7x, 128 devices: a whole 4x4x4 slice. The times are simulated.
128 devices in a mesh: tm: 32 (over x, z, core), panel: 4 (over y).
Axes of the slice: x: 4, y: 4, z: 4, core: 2. Of those that a mesh axis runs over, the one named last changes fastest.
Arguments:
- design: bfloat16 [8192, 7680], P('tm', 'panel'), may hold values from -6 to 6
- partials: bfloat16 [8192, 64], P('tm'), may hold values from -0.119628906 to 0.119628906
- observed: bfloat16 [8192], P('tm'), may hold values from -6 to 6
- arc_of_row: int32 [8192, 1], replicated, may hold values from 0 to 31, as said below
- autoreg: float32 [32], replicated, may hold values from -0.55 to 0.5
- movavg: float32 [32], replicated, may hold values from 0.3 to 0.9
Outputs:
- normal: float32 [7680, 7680], P('tm', 'panel')
- right_hand: float32 [7680], P('panel')
Inputs may be any that keep to these rules, and one draw needn't show every extreme that they name: arc_of_row never falls along the epochs and names every arc; arcs 2b and 2b + 1 together have 2 * 256 epochs, one of them 384 // 3 to 160 epochs and the other 352 to 384; one arc has exactly 384 epochs and its partner exactly 128, so that at most 12 rows of one device belong to one arc, and every device holds exactly 12 rows of the longest arc; arc a is held by index a of tm.
All inputs are finite; a program needn't handle non-finite values.
Results may differ from a plain program's by a relative error of at most 0.02.
Values may be sent and summed in bfloat16 or wider, within the bound.
A program may use at most 192 MiB of HBM per device.

v0:
```python
import jax
import jax.numpy as jnp
from jax import lax
from jax.sharding import PartitionSpec as P


def whiten_matrix(order_row, order_col, usable_row, usable_col, ar_value, ma_value):
    spacing = order_row[:, None] - order_col[None, :]
    lag_steps = jnp.maximum(spacing - 1, 0)
    parity = (lag_steps % 2).astype(jnp.float32)
    flip_sign = 1.0 - 2.0 * parity
    decayed = (
        -(ar_value + ma_value)
        * flip_sign
        * jnp.exp(lag_steps.astype(jnp.float32) * jnp.log(ma_value))
    )
    entry = jnp.where(spacing == 0, jnp.float32(1.0), decayed)
    allowed = usable_row[:, None] & usable_col[None, :] & (spacing >= 0)
    return jnp.where(allowed, entry, jnp.float32(0.0)).astype(jnp.bfloat16)


def eliminate(whitener, rows_design, rows_params, rows_obs, scale):
    white_design = jnp.dot(whitener, rows_design, preferred_element_type=jnp.float32)
    white_params = jnp.dot(whitener, rows_params, preferred_element_type=jnp.float32)
    white_obs = jnp.dot(whitener, rows_obs, preferred_element_type=jnp.float32)
    param_count = rows_params.shape[1]
    param_gram = jnp.dot(white_params.T, white_params, precision=lax.Precision.HIGHEST) + jnp.eye(
        param_count, dtype=jnp.float32
    )
    factor = jnp.linalg.cholesky(param_gram)
    basis = lax.linalg.triangular_solve(factor, white_params.T, left_side=True, lower=True)
    arc_terms = jnp.dot(basis, white_design, precision=lax.Precision.HIGHEST)
    arc_rhs = jnp.dot(basis, white_obs, precision=lax.Precision.HIGHEST)
    right_part = (
        jnp.dot(white_design.T, white_obs, precision=lax.Precision.HIGHEST)
        - jnp.dot(arc_terms.T, arc_rhs, precision=lax.Precision.HIGHEST)
    ) * scale
    return (white_design.astype(jnp.bfloat16), arc_terms.astype(jnp.bfloat16), right_part)


def body(design, partials, observed, arc_of_row, autoreg, movavg):
    tile_count = lax.axis_size("tm")
    device_index = lax.axis_index("tm")
    rows_dev = design.shape[0]
    panel_width = design.shape[1]
    param_count = partials.shape[1]
    capacity = 3 * rows_dev // 2 // tile_count
    slot_count = tile_count * capacity
    scale = 1.0 / (rows_dev * tile_count)
    arc_ids = arc_of_row[:, 0]
    epoch_table = arc_ids.reshape(rows_dev, tile_count)
    local_arcs = lax.dynamic_slice_in_dim(epoch_table, device_index, 1, 1)[:, 0]
    onehot = (local_arcs[:, None] == jnp.arange(tile_count, dtype=jnp.int32)[None, :]).astype(
        jnp.int32
    )
    earlier = jnp.cumsum(onehot, axis=0) - onehot
    within = jnp.sum(earlier * onehot, axis=1)
    target_slot = local_arcs * capacity + within
    source_row = (
        jnp.zeros((slot_count,), jnp.int32)
        .at[target_slot]
        .set(jnp.arange(1, rows_dev + 1, dtype=jnp.int32))
    )

    def pick_rows(values):
        padded = jnp.concatenate([jnp.zeros((1,) + values.shape[1:], values.dtype), values], axis=0)
        return jnp.take(padded, source_row, axis=0)

    send_design = pick_rows(design).reshape(tile_count, capacity, panel_width)
    send_params = pick_rows(partials).reshape(tile_count, capacity, param_count)
    send_obs = pick_rows(observed).reshape(tile_count, capacity)
    got_design, got_params, got_obs = (
        lax.all_to_all(send_design, "tm", split_axis=0, concat_axis=0, tiled=True),
        lax.all_to_all(send_params, "tm", split_axis=0, concat_axis=0, tiled=True),
        lax.all_to_all(send_obs, "tm", split_axis=0, concat_axis=0, tiled=True),
    )
    got_design = got_design.reshape(slot_count, panel_width)
    got_params = got_params.reshape(slot_count, param_count)
    got_obs = got_obs.reshape(slot_count)
    per_source = jnp.sum((epoch_table == device_index).astype(jnp.int32), axis=0)
    arc_start = jnp.sum((arc_ids < device_index).astype(jnp.int32))
    first_pos = jnp.mod(jnp.arange(tile_count, dtype=jnp.int32) - arc_start, tile_count)
    offset_in = jnp.arange(capacity, dtype=jnp.int32)
    order_pos = (first_pos[:, None] + offset_in[None, :] * tile_count).reshape(slot_count)
    usable = (offset_in[None, :] < per_source[:, None]).reshape(slot_count)
    whitener = whiten_matrix(
        order_pos, order_pos, usable, usable, autoreg[device_index], movavg[device_index]
    )
    design_bf, terms_bf, right_part = eliminate(whitener, got_design, got_params, got_obs, scale)
    right_hand = lax.psum(right_part, "tm")
    own_rows = jnp.concatenate([design_bf, terms_bf], axis=0)
    signed_rows = jnp.concatenate([design_bf, -terms_bf], axis=0)
    gathered = lax.all_gather(signed_rows, "panel", axis=1, tiled=True)
    product = lax.dot_general(
        gathered, own_rows, (((0,), (0,)), ((), ())), preferred_element_type=jnp.float32
    )
    normal = lax.psum_scatter(
        (product * scale).astype(jnp.bfloat16), "tm", scatter_dimension=0, tiled=True
    ).astype(jnp.float32)
    return (normal, right_hand)


def solution(mesh):
    in_specs = (P("tm", "panel"), P("tm", None), P("tm"), P(), P(), P())
    out_specs = (P("tm", "panel"), P("panel"))
    return jax.shard_map(body, mesh=mesh, in_specs=in_specs, out_specs=out_specs, check_vma=False)
```

profile of v0, /device:TPU:24, one launch (start us, length us, event | category | flops | bytes accessed | tf_op | source)
XLA Modules:
  0.0 332.1 jit_solution(6460968665628124426)
XLA Ops:
  7.2 1.0 copy.16
  8.1 0.5 broadcast.193
  8.7 2.1 fusion.33
  10.8 0.1 reshape_squeeze.3
  10.9 0.0 copy-start.1
  10.9 0.2 dynamic-slice_reduce_fusion
  11.1 0.6 reduce-window.6
  11.7 0.2 slice_reduce_fusion
  11.9 0.1 fusion.36
  12.0 0.1 copy.15
  12.2 0.2 fusion.31
  12.4 1.4 scatter_custom_fusion
  13.8 0.7 pad_maximum_fusion.1
  14.5 2.8 gather_fusion.2
  17.4 0.1 broadcast_in_dim.54
  17.5 1.4 gather_fusion.1
  19.0 0.1 broadcast_select_fusion.1
  19.2 0.8 reshape.233
  19.9 8.2 %all-to-all-start.1 = ((bf16[32,2,384]{2,1,0:T(2,128)(2,1)}), bf16[32,2,384]{2,1,0:T(2,128)(2,1)S(1)}, u32[]{:S(2)}, u32[]{:S(2)}) async-start(bf16[32,2,384]{2,1,0:T(2,128)(2,1)} %reshape.233), calls=%async_computation.1 | async-start | bytes 98304 | tf_op jit(solution)/shard_map/all_to_all | solution.py:74
  28.1 0.7 and_select_fusion
  28.8 0.2 concatenate.15
  29.0 2.5 gather_fusion
  31.5 0.4 gather.17
  31.9 1.6 broadcast_select_fusion
  33.5 0.1 broadcast_add_fusion
  33.5 0.1 convert_reduce_fusion
  33.6 1.9 all-to-all-done.1
  35.5 5.5 %all-to-all-start = ((bf16[32,12,1920]{2,1,0:T(8,128)(2,1)}), bf16[32,12,1920]{2,1,0:T(8,128)(2,1)S(1)}, u32[]{:S(2)}, u32[]{:S(2)}) async-start(bf16[32,12,1920]{2,1,0:T(8,128)(2,1)} %broadcast_select_fusion), calls=%async_computation | async-start | bytes 3932160 | tf_op jit(solution)/shard_map/all_to_all | solution.py:73
  41.0 0.2 all-gather.2.cloned.1.call-start
  41.3 0.1 iota_compare_fusion.5
  41.3 0.6 dynamic_slice.10
  42.6 0.6 dynamic_slice.9
  44.5 0.1 add.112
  44.6 0.1 lt.72
  44.7 0.1 reshape.234
  44.9 0.7 fusion.27
  45.7 0.2 fusion.69
  45.9 0.1 copy.17
  46.0 5.8 %cholesky.17 = f32[64,64]{1,0:T(8,128)S(1)} custom-call(f32[64,64]{1,0:T(8,128)S(1)} %fusion.40), custom_call_target="Cholesky" | custom-call | tf_op jit(solution)/shard_map/jit(cholesky)/cholesky | solution.py:30
  51.9 0.6 compare_reduce_fusion
  52.6 0.7 fusion.32
  53.2 4.9 %custom-call.6 = f32[1,64,64]{1,2,0:T(8,128)S(1)} custom-call(f32[1,64,64]{2,1,0:T(8,128)S(1)} %fusion.32), custom_call_target="InvertDiagBlocksLowerTriangular" | custom-call | tf_op jit(solution)/shard_map/triangular_solve | solution.py:31
  58.1 0.3 fusion.37
  58.4 10.1 %all-to-all-done = bf16[32,12,1920]{2,1,0:T(8,128)(2,1)S(1)} async-done(((bf16[32,12,1920]{2,1,0:T(8,128)(2,1)}), bf16[32,12,1920]{2,1,0:T(8,128)(2,1)S(1)}, u32[]{:S(2)}, u32[]{:S(2)}) %all-to-all-start) | async-done | bytes 1474592 | tf_op jit(solution)/shard_map/all_to_all | solution.py:73
  68.5 1.3 reshape.165
  69.8 2.7 fusion.68
  72.5 2.3 fusion.67
  74.9 1.3 pad_maximum_fusion
  76.2 0.0 all-gather.2.cloned.1.call-update
  76.2 0.0 reduce-scatter.4.cloned.1.call-start
  76.3 66.5 %all-gather.2.cloned.1.call-done = bf16[448,7680]{1,0:T(8,128)(2,1)} async-done(((bf16[448,1920]{1,0:T(8,128)(2,1)}), bf16[448,7680]{1,0:T(8,128)(2,1)}) %all-gather.2.cloned.1.call-update) | async-done | bytes 6881296 | tf_op jit(solution)/shard_map/all_gather | solution.py:93
  142.7 22.9 %multiply_convert_fusion = bf16[7680,1920]{1,0:T(8,128)(2,1)} fusion(bf16[448,7680]{1,0:T(8,128)(2,1)} %all-gather.2.cloned.1.call-done, bf16[64,1920]{1,0:T(8,128)(2,1)} %get-tuple-element.7, bf16[384,1920]{1,0:T(8,128)(2,1)} %copy-done), kind=kOutput, calls=%fused_computation.4 | convolution fusion | flops 13244989440 | bytes 38092800 | tf_op jit(solution)/shard_map/dot_general | solution.py:94
  165.6 0.0 reduce-scatter.4.cloned.1.call-update
  165.6 0.7 select_n.84
  166.3 14.8 %all_to_all.16 = bf16[32,1,12]{2,1,0:T(2,128)(2,1)S(1)} all-to-all(bf16[32,1,12]{2,1,0:T(2,128)(2,1)} %select_n.84), channel_id=1, replica_groups=mesh['tm'=32,'panel'=4] {'tm'}, dimensions={0} | all-to-all | bytes 1536 | tf_op jit(solution)/shard_map/all_to_all | solution.py:75
  181.1 0.7 reduce.12
  181.8 0.8 reshape.203
  182.6 1.5 convolution_bitcast_fusion
  184.0 0.2 convolution_bitcast_fusion.1
  184.2 0.4 convolution_reduce_fusion
  184.7 1.7 fusion.5
  186.3 66.6 %psum.7 = f32[1920]{0:T(1024)} all-reduce(f32[1920]{0:T(1024)S(1)} %subtract_multiply_fusion), channel_id=1, replica_groups=mesh['tm'=32,'panel'=4] {'tm'}, use_global_device_ids=true, to_apply=%region_9.10 | all-reduce | flops 1920 | bytes 15360 | tf_op jit(solution)/shard_map/psum | solution.py:90
  252.9 69.8 %reduce-scatter.4.cloned.1.call-done = bf16[240,1920]{1,0:T(8,128)(2,1)} async-done(((bf16[7680,1920]{1,0:T(8,128)(2,1)}), bf16[240,1920]{1,0:T(8,128)(2,1)}) %reduce-scatter.4.cloned.1.call-update) | async-done | bytes 921616
  322.8 2.5 convert_element_type.57
  (29 shorter events, 0.3 us)
Async XLA Ops:
  7.2 21.6 %copy-start.3 = (bf16[256,1920]{1,0:T(8,128)(2,1)S(1)}, bf16[256,1920]{1,0:T(8,128)(2,1)}, u32[]{:S(2)}) copy-start(bf16[256,1920]{1,0:T(8,128)(2,1)} %param.6) | copy-start | bytes 2949124
  10.9 2.9 copy-start.1
  19.9 15.6 %all-to-all-start.1 = ((bf16[32,2,384]{2,1,0:T(2,128)(2,1)}), bf16[32,2,384]{2,1,0:T(2,128)(2,1)S(1)}, u32[]{:S(2)}, u32[]{:S(2)}) async-start(bf16[32,2,384]{2,1,0:T(2,128)(2,1)} %reshape.233), calls=%async_computation.1 | async-start | bytes 98304 | tf_op jit(solution)/shard_map/all_to_all | solution.py:74
  31.9 1.7 copy-start.2
  33.6 7.7 %copy-start.6 = (f32[32]{0:T(128)S(1)}, f32[32]{0:T(128)}, u32[]{:S(2)}) copy-start(f32[32]{0:T(128)} %param.11) | copy-start | bytes 388
  33.6 9.0 %copy-start.7 = (f32[32]{0:T(128)S(1)}, f32[32]{0:T(128)}, u32[]{:S(2)}) copy-start(f32[32]{0:T(128)} %param.10) | copy-start | bytes 388
  35.5 33.0 %all-to-all-start = ((bf16[32,12,1920]{2,1,0:T(8,128)(2,1)}), bf16[32,12,1920]{2,1,0:T(8,128)(2,1)S(1)}, u32[]{:S(2)}, u32[]{:S(2)}) async-start(bf16[32,12,1920]{2,1,0:T(8,128)(2,1)} %broadcast_select_fusion), calls=%async_computation | async-start | bytes 3932160 | tf_op jit(solution)/shard_map/all_to_all | solution.py:73
  41.0 101.7 %all-gather.2.cloned.1.call-start = ((), (), s32[]{:S(2)}) async-start(), calls=%async_computation.4 | async-start | bytes 8601600 | tf_op jit(solution)/shard_map/all_gather | solution.py:93
  44.6 25.2 %copy-start.4 = (s32[384]{0:T(512)}, s32[384]{0:T(512)S(1)}, u32[]{:S(2)}) copy-start(s32[384]{0:T(512)S(1)} %add.112) | copy-start | bytes 4612
  44.7 25.0 %copy-start.5 = (pred[384]{0:T(512)(128)(4,1)}, pred[384]{0:T(512)(128)(4,1)S(1)}, u32[]{:S(2)}) copy-start(pred[384]{0:T(512)(128)(4,1)S(1)} %lt.72) | copy-start | bytes 1156
  72.5 2.4 copy-start
  76.2 246.6 %reduce-scatter.4.cloned.1.call-start = ((), (), s32[]{:S(2)}) async-start(), calls=%async_computation.5 | async-start | bytes 30412800
Sparse Core Ops, SparseCore 0:
  76.3 66.3 all-gather.1
  165.7 156.9 reduce-scatter.3
where the time goes:
time: 333 us; the launch traced here: 332 us
  waiting for transfers between devices  148 us (44%)
  blocking collectives  81.4 us (24%)
  matrix products  33 us (10%)
  other arithmetic  23 us (7%)
  between operations  16.4 us (5%)
  local copies, waits for them, and re-layouts  16.2 us (5%)
  starting transfers between devices  13.9 us (4%)
    unnamed x3, waiting for transfers between devices  69.9 us
    psum x1, blocking collectives, body(): right_hand = lax.psum(right_part, 'tm')  66.6 us
    all_gather x1, waiting for transfers between devices, body(): gathered = lax.all_gather(signed_rows, 'panel', axis=1, tiled=True)  66.5 us
    dot_general x1, matrix products, body(): lax.dot_general(gathered, own_rows, (((0,), (0,)), ((), ())), preferred_e...  22.9 us
    all_to_all x1, blocking collectives, body(): lax.all_to_all(send_obs, 'tm', split_axis=0, concat_axis=0, tiled=True)  14.8 us
    all_to_all x1, waiting for transfers between devices, body(): lax.all_to_all(send_design, 'tm', split_axis=0, concat_axis=0, tiled=True)  10.1 us
    all_to_all x1, starting transfers between devices, body(): lax.all_to_all(send_params, 'tm', split_axis=0, concat_axis=0, tiled=True)  8.16 us
    gather x5, local copies, waits for them, and re-layouts, pick_rows(): return jnp.take(padded, source_row, axis=0)  7.16 us
  transfers between devices with their start and end apart: 4, of which 4 were waited for; matrix products, arithmetic and copies ran while one was open for 8% of the time, Pallas kernels for 0%

commit v1 on v0

--- a/solution.py
+++ b/solution.py
@@ -1,7 +1,9 @@
 import jax
 import jax.numpy as jnp
 from jax import lax
-from jax.sharding import PartitionSpec as P
+from jax.sharding import Mesh, PartitionSpec as P
+
+TM = ("tmc", "core")
 
 
 def whiten_matrix(order_row, order_col, usable_row, usable_col, ar_value, ma_value):
@@ -39,8 +41,10 @@
 
 
 def body(design, partials, observed, arc_of_row, autoreg, movavg):
-    tile_count = lax.axis_size("tm")
-    device_index = lax.axis_index("tm")
+    chip_count = lax.axis_size("tmc")
+    core_count = lax.axis_size("core")
+    tile_count = chip_count * core_count
+    device_index = lax.axis_index("tmc") * core_count + lax.axis_index("core")
     rows_dev = design.shape[0]
     panel_width = design.shape[1]
     param_count = partials.shape[1]
@@ -70,9 +74,9 @@
     send_params = pick_rows(partials).reshape(tile_count, capacity, param_count)
     send_obs = pick_rows(observed).reshape(tile_count, capacity)
     got_design, got_params, got_obs = (
-        lax.all_to_all(send_design, "tm", split_axis=0, concat_axis=0, tiled=True),
-        lax.all_to_all(send_params, "tm", split_axis=0, concat_axis=0, tiled=True),
-        lax.all_to_all(send_obs, "tm", split_axis=0, concat_axis=0, tiled=True),
+        lax.all_to_all(send_design, TM, split_axis=0, concat_axis=0, tiled=True),
+        lax.all_to_all(send_params, TM, split_axis=0, concat_axis=0, tiled=True),
+        lax.all_to_all(send_obs, TM, split_axis=0, concat_axis=0, tiled=True),
     )
     got_design = got_design.reshape(slot_count, panel_width)
     got_params = got_params.reshape(slot_count, param_count)
@@ -87,20 +91,33 @@
         order_pos, order_pos, usable, usable, autoreg[device_index], movavg[device_index]
     )
     design_bf, terms_bf, right_part = eliminate(whitener, got_design, got_params, got_obs, scale)
-    right_hand = lax.psum(right_part, "tm")
+    right_hand = lax.psum(right_part, TM)
     own_rows = jnp.concatenate([design_bf, terms_bf], axis=0)
     signed_rows = jnp.concatenate([design_bf, -terms_bf], axis=0)
     gathered = lax.all_gather(signed_rows, "panel", axis=1, tiled=True)
+    coeff_count = gathered.shape[1]
+    block_rows = coeff_count // tile_count
+    gathered = (
+        gathered.reshape(-1, chip_count, core_count, block_rows)
+        .transpose(0, 2, 1, 3)
+        .reshape(-1, coeff_count)
+    )
     product = lax.dot_general(
         gathered, own_rows, (((0,), (0,)), ((), ())), preferred_element_type=jnp.float32
     )
-    normal = lax.psum_scatter(
-        (product * scale).astype(jnp.bfloat16), "tm", scatter_dimension=0, tiled=True
-    ).astype(jnp.float32)
+    partial = (product * scale).astype(jnp.bfloat16)
+    partial = lax.psum_scatter(partial, "core", scatter_dimension=0, tiled=True)
+    normal = lax.psum_scatter(partial, "tmc", scatter_dimension=0, tiled=True).astype(
+        jnp.float32
+    )
     return (normal, right_hand)
 
 
 def solution(mesh):
-    in_specs = (P("tm", "panel"), P("tm", None), P("tm"), P(), P(), P())
-    out_specs = (P("tm", "panel"), P("panel"))
-    return jax.shard_map(body, mesh=mesh, in_specs=in_specs, out_specs=out_specs, check_vma=False)
+    chips = mesh.devices.shape[0] // 2
+    split = Mesh(
+        mesh.devices.reshape(chips, 2, mesh.devices.shape[1]), ("tmc", "core", "panel")
+    )
+    in_specs = (P(TM, "panel"), P(TM, None), P(TM), P(), P(), P())
+    out_specs = (P(TM, "panel"), P("panel"))
+    return jax.shard_map(body, mesh=split, in_specs=in_specs, out_specs=out_specs, check_vma=False)

time: 333 us -> 384 us (1.15)
  local copies, waits for them, and re-layouts: 16.2 us -> 68.1 us
    reshape x0 -> x3, local copies, waits for them, and re-layouts: none -> 51.9 us  [the longest x2 37.6 us: body(): gathered.reshape(-1, chip_count, core_count, block_rows)]
    unnamed x3 -> x4, waiting for transfers between devices: 69.9 us -> 22.5 us
    reduce_scatter x0 -> x1, waiting for transfers between devices: none -> 45.5 us  [body(): partial = lax.psum_scatter(partial, 'core', scatter_dimension=0, tiled=True)]
  transfers between devices with their start and end apart: 4 -> 5, of which waited for: 4 -> 5; matrix products, arithmetic and copies ran while one was open for 8% -> 7% of each run, Pallas kernels for 0% -> 0%
where the time goes in v1:
time: 384 us; the launch traced here: 382 us
  waiting for transfers between devices  146 us (38%)
  blocking collectives  81.6 us (21%)
  local copies, waits for them, and re-layouts  68.1 us (18%)
  matrix products  33 us (9%)
  other arithmetic  23 us (6%)
  between operations  16.1 us (4%)
  starting transfers between devices  14.2 us (4%)
    psum x1, blocking collectives, body(): right_hand = lax.psum(right_part, TM)  67.2 us
    all_gather x1, waiting for transfers between devices, body(): gathered = lax.all_gather(signed_rows, 'panel', axis=1, tiled=True)  66.2 us
    reduce_scatter x1, waiting for transfers between devices, body(): partial = lax.psum_scatter(partial, 'core', scatter_dimension=0, tiled=True)  45.5 us
    reshape x2, local copies, waits for them, and re-layouts, body(): gathered.reshape(-1, chip_count, core_count, block_rows)  37.6 us
    dot_general x1, matrix products, body(): lax.dot_general(gathered, own_rows, (((0,), (0,)), ((), ())), preferred_e...  22.9 us
    unnamed x4, waiting for transfers between devices  22.5 us
    all_to_all x1, blocking collectives, body(): lax.all_to_all(send_obs, TM, split_axis=0, concat_axis=0, tiled=True)  14.4 us
    reshape x1, local copies, waits for them, and re-layouts, body(): gathered = gathered.reshape(-1, chip_count, core_count, block_rows).trans...  14.3 us
  transfers between devices with their start and end apart: 5, of which 5 were waited for; matrix products, arithmetic and copies ran while one was open for 7% of the time, Pallas kernels for 0%

profile of v1, /device:TPU:24, one launch (start us, length us, event | category | flops | bytes accessed | tf_op | source)
XLA Modules:
  0.0 382.2 jit_solution(10395129118387624693)
XLA Ops:
  7.2 1.0 copy.17
  8.2 0.5 broadcast.193
  8.7 2.1 fusion.33
  10.8 0.1 reshape_squeeze.3
  10.9 0.2 dynamic-slice_reduce_fusion
  11.1 0.6 reduce-window.6
  11.7 0.2 slice_reduce_fusion
  11.9 0.1 fusion.36
  12.0 0.1 copy.16
  12.2 0.2 fusion.31
  12.4 1.4 scatter_custom_fusion
  13.8 0.7 pad_maximum_fusion.1
  14.6 2.8 gather_fusion.2
  17.4 0.1 broadcast_in_dim.54
  17.5 1.4 gather_fusion.1
  19.0 0.1 broadcast_select_fusion.1
  19.2 0.8 reshape.241
  19.9 8.2 %all-to-all-start.1 = ((bf16[32,2,384]{2,1,0:T(2,128)(2,1)}), bf16[32,2,384]{2,1,0:T(2,128)(2,1)S(1)}, u32[]{:S(2)}, u32[]{:S(2)}) async-start(bf16[32,2,384]{2,1,0:T(2,128)(2,1)} %reshape.241), calls=%async_computation.1 | async-start | bytes 98304 | tf_op jit(solution)/shard_map/all_to_all | solution.py:78
  28.1 0.7 and_select_fusion
  28.8 0.2 concatenate.15
  29.0 2.5 gather_fusion
  31.5 0.4 gather.17
  31.9 1.6 broadcast_select_fusion
  33.5 0.1 broadcast_add_fusion
  33.6 1.9 all-to-all-done.1
  35.6 5.5 %all-to-all-start = ((bf16[32,12,1920]{2,1,0:T(8,128)(2,1)}), bf16[32,12,1920]{2,1,0:T(8,128)(2,1)S(1)}, u32[]{:S(2)}, u32[]{:S(2)}) async-start(bf16[32,12,1920]{2,1,0:T(8,128)(2,1)} %broadcast_select_fusion), calls=%async_computation | async-start | bytes 3932160 | tf_op jit(solution)/shard_map/all_to_all | solution.py:77
  41.0 0.2 all-gather.2.cloned.1.call-start
  41.3 0.1 iota_compare_fusion.5
  41.3 0.6 dynamic_slice.10
  42.6 0.6 dynamic_slice.9
  44.5 0.1 add.118
  44.6 0.1 lt.72
  44.8 0.1 reshape.242
  44.9 0.7 fusion.27
  45.7 0.2 fusion.69
  45.9 0.1 copy.18
  46.0 5.8 %cholesky.17 = f32[64,64]{1,0:T(8,128)S(1)} custom-call(f32[64,64]{1,0:T(8,128)S(1)} %fusion.40), custom_call_target="Cholesky" | custom-call | tf_op jit(solution)/shard_map/jit(cholesky)/cholesky | solution.py:32
  51.9 0.6 compare_reduce_fusion
  52.6 0.7 fusion.32
  53.2 4.9 %custom-call.6 = f32[1,64,64]{1,2,0:T(8,128)S(1)} custom-call(f32[1,64,64]{2,1,0:T(8,128)S(1)} %fusion.32), custom_call_target="InvertDiagBlocksLowerTriangular" | custom-call | tf_op jit(solution)/shard_map/triangular_solve | solution.py:33
  58.1 0.3 fusion.37
  58.4 10.1 %all-to-all-done = bf16[32,12,1920]{2,1,0:T(8,128)(2,1)S(1)} async-done(((bf16[32,12,1920]{2,1,0:T(8,128)(2,1)}), bf16[32,12,1920]{2,1,0:T(8,128)(2,1)S(1)}, u32[]{:S(2)}, u32[]{:S(2)}) %all-to-all-start) | async-done | bytes 1474592 | tf_op jit(solution)/shard_map/all_to_all | solution.py:77
  68.5 1.3 reshape.171
  69.8 2.7 fusion.68
  72.5 2.3 fusion.67
  74.9 1.3 pad_maximum_fusion
  76.2 0.3 reduce-scatter.5.cloned.1.call-start
  76.5 66.2 %all-gather.2.cloned.1.call-done = bf16[448,7680]{1,0:T(8,128)(2,1)} async-done(((bf16[448,1920]{1,0:T(8,128)(2,1)}), bf16[448,7680]{1,0:T(8,128)(2,1)}) %all-gather.2.cloned.1.call-update) | async-done | bytes 6881296 | tf_op jit(solution)/shard_map/all_gather | solution.py:97
  142.7 29.3 %reshape.173 = bf16[448,16,2,240]{3,2,1,0:T(2,128)(2,1)} reshape(bf16[448,7680]{1,0:T(8,128)(2,1)} %all-gather.2.cloned.1.call-done) | data formatting | bytes 13762560 | tf_op jit(solution)/shard_map/reshape | solution.py:101
  172.0 8.3 %copy.24 = bf16[448,16,2,240]{3,1,2,0:T(8,128)(2,1)} copy(bf16[448,16,2,240]{3,2,1,0:T(2,128)(2,1)} %reshape.173) | data formatting | bytes 13762560 | tf_op jit(solution)/shard_map/reshape | solution.py:101
  180.3 14.3 %reshape.174 = bf16[448,7680]{1,0:T(8,128)(2,1)} reshape(bf16[448,2,16,240]{3,2,1,0:T(8,128)(2,1)} %bitcast.68) | data formatting | bytes 13762560 | tf_op jit(solution)/shard_map/reshape | solution.py:103
  194.6 22.9 %multiply_convert_fusion = bf16[7680,1920]{1,0:T(8,128)(2,1)} fusion(bf16[448,7680]{1,0:T(8,128)(2,1)} %reshape.174, bf16[64,1920]{1,0:T(8,128)(2,1)} %get-tuple-element.7, bf16[384,1920]{1,0:T(8,128)(2,1)} %copy-done), kind=kOutput, calls=%fused_computation.4 | convolution fusion | flops 13244989440 | bytes 38092800 | tf_op jit(solution)/shard_map/dot_general | solution.py:105
  217.6 45.5 %reduce-scatter.5.cloned.1.call-done = bf16[3840,1920]{1,0:T(8,128)(2,1)} async-done(((bf16[7680,1920]{1,0:T(8,128)(2,1)}), bf16[3840,1920]{1,0:T(8,128)(2,1)}) %reduce-scatter.5.cloned.1.call-update) | async-done | bytes 14745616 | tf_op jit(solution)/shard_map/reduce_scatter | solution.py:109
  263.1 0.7 select_n.84
  263.9 14.4 %all_to_all.16 = bf16[32,1,12]{2,1,0:T(2,128)(2,1)S(1)} all-to-all(bf16[32,1,12]{2,1,0:T(2,128)(2,1)} %select_n.84), channel_id=1, replica_groups=mesh['tmc'=16,'core'=2,'panel'=4] {'tmc','core'}, dimensions={0} | all-to-all | bytes 1536 | tf_op jit(solution)/shard_map/all_to_all | solution.py:79
  278.2 0.7 reduce.12
  278.9 0.8 reshape.211
  279.7 1.4 convolution_bitcast_fusion
  281.1 0.2 convolution_bitcast_fusion.1
  281.3 0.4 convolution_reduce_fusion
  281.8 1.7 fusion.5
  283.5 67.2 %psum.7 = f32[1920]{0:T(1024)} all-reduce(f32[1920]{0:T(1024)S(1)} %subtract_multiply_fusion), channel_id=1, replica_groups=mesh['tmc'=16,'core'=2,'panel'=4] {'tmc','core'}, use_global_device_ids=true, to_apply=%region_10.11 | all-reduce | flops 1920 | bytes 15360 | tf_op jit(solution)/shard_map/psum | solution.py:94
  350.7 22.5 %reduce-scatter.7.cloned.1.call-done = bf16[240,1920]{1,0:T(8,128)(2,1)} async-done(((bf16[3840,1920]{1,0:T(8,128)(2,1)}), bf16[240,1920]{1,0:T(8,128)(2,1)}) %reduce-scatter.7.cloned.1.call-update) | async-done | bytes 921616
  373.1 2.5 convert_element_type.57
  (35 shorter events, 0.4 us)
Async XLA Ops:
  7.2 21.6 %copy-start.3 = (bf16[256,1920]{1,0:T(8,128)(2,1)S(1)}, bf16[256,1920]{1,0:T(8,128)(2,1)}, u32[]{:S(2)}) copy-start(bf16[256,1920]{1,0:T(8,128)(2,1)} %param.6) | copy-start | bytes 2949124
  10.9 2.9 copy-start.1
  19.9 15.6 %all-to-all-start.1 = ((bf16[32,2,384]{2,1,0:T(2,128)(2,1)}), bf16[32,2,384]{2,1,0:T(2,128)(2,1)S(1)}, u32[]{:S(2)}, u32[]{:S(2)}) async-start(bf16[32,2,384]{2,1,0:T(2,128)(2,1)} %reshape.241), calls=%async_computation.1 | async-start | bytes 98304 | tf_op jit(solution)/shard_map/all_to_all | solution.py:78
  31.9 1.7 copy-start.2
  33.6 7.7 %copy-start.6 = (f32[32]{0:T(128)S(1)}, f32[32]{0:T(128)}, u32[]{:S(2)}) copy-start(f32[32]{0:T(128)} %param.11) | copy-start | bytes 388
  33.6 9.0 %copy-start.7 = (f32[32]{0:T(128)S(1)}, f32[32]{0:T(128)}, u32[]{:S(2)}) copy-start(f32[32]{0:T(128)} %param.10) | copy-start | bytes 388
  35.6 33.0 %all-to-all-start = ((bf16[32,12,1920]{2,1,0:T(8,128)(2,1)}), bf16[32,12,1920]{2,1,0:T(8,128)(2,1)S(1)}, u32[]{:S(2)}, u32[]{:S(2)}) async-start(bf16[32,12,1920]{2,1,0:T(8,128)(2,1)} %broadcast_select_fusion), calls=%async_computation | async-start | bytes 3932160 | tf_op jit(solution)/shard_map/all_to_all | solution.py:77
  41.0 101.7 %all-gather.2.cloned.1.call-start = ((), (), s32[]{:S(2)}) async-start(), calls=%async_computation.5 | async-start | bytes 8601600 | tf_op jit(solution)/shard_map/all_gather | solution.py:97
  44.6 25.2 %copy-start.4 = (s32[384]{0:T(512)}, s32[384]{0:T(512)S(1)}, u32[]{:S(2)}) copy-start(s32[384]{0:T(512)S(1)} %add.118) | copy-start | bytes 4612
  44.7 25.0 %copy-start.5 = (pred[384]{0:T(512)(128)(4,1)}, pred[384]{0:T(512)(128)(4,1)S(1)}, u32[]{:S(2)}) copy-start(pred[384]{0:T(512)(128)(4,1)S(1)} %lt.72) | copy-start | bytes 1156
  72.5 2.4 copy-start
  76.2 186.9 %reduce-scatter.5.cloned.1.call-start = ((), (), s32[]{:S(2)}) async-start(), calls=%async_computation.6 | async-start | bytes 44236800 | tf_op jit(solution)/shard_map/reduce_scatter | solution.py:109
  217.5 155.6 %reduce-scatter.7.cloned.1.call-start = ((), (), s32[]{:S(2)}) async-start(), calls=%async_computation.7 | async-start | bytes 15667200
Sparse Core Ops, SparseCore 0:
  76.3 66.3 all-gather.1
  217.7 45.4 reduce-scatter.4
  266.6 106.5 reduce-scatter.6

commit v2 on v0

--- a/solution.py
+++ b/solution.py
@@ -36,6 +36,16 @@
         - jnp.dot(arc_terms.T, arc_rhs, precision=lax.Precision.HIGHEST)
     ) * scale
     return (white_design.astype(jnp.bfloat16), arc_terms.astype(jnp.bfloat16), right_part)
+
+
+def mirror_pairs(tile_count, panel_count, offset):
+    group = tile_count // panel_count
+    pairs = []
+    for u in range(tile_count):
+        for q in range(panel_count):
+            target = group * q + (u % group + offset) % group
+            pairs.append((u * panel_count + q, target * panel_count + u // group))
+    return pairs
 
 
 def body(design, partials, observed, arc_of_row, autoreg, movavg):
@@ -91,12 +101,38 @@
     own_rows = jnp.concatenate([design_bf, terms_bf], axis=0)
     signed_rows = jnp.concatenate([design_bf, -terms_bf], axis=0)
     gathered = lax.all_gather(signed_rows, "panel", axis=1, tiled=True)
-    product = lax.dot_general(
-        gathered, own_rows, (((0,), (0,)), ((), ())), preferred_element_type=jnp.float32
+    panel_count = lax.axis_size("panel")
+    panel_index = lax.axis_index("panel")
+    group = tile_count // panel_count
+    width = panel_width // group
+    kept = group // 2 + 1
+    row_count = gathered.shape[0]
+    doubled = jnp.concatenate([own_rows, own_rows[:, : (kept - 1) * width]], axis=1)
+    windows = jnp.stack(
+        [doubled[:, k * width : (k + kept) * width] for k in range(group)]
     )
-    normal = lax.psum_scatter(
-        (product * scale).astype(jnp.bfloat16), "tm", scatter_dimension=0, tiled=True
-    ).astype(jnp.float32)
+    row_tiles = gathered.reshape(row_count, panel_count, group, width)
+    pieces = []
+    for r in range(panel_count):
+        block = lax.dot_general(
+            row_tiles[:, r], windows, (((0,), (1,)), ((1,), (0,))),
+            preferred_element_type=jnp.float32,
+        )
+        pieces.append((block * scale).astype(jnp.bfloat16))
+    stacked = jnp.concatenate(pieces, axis=0).reshape(tile_count * width, kept * width)
+    reduced = lax.psum_scatter(stacked, "tm", scatter_dimension=0, tiled=True).astype(
+        jnp.float32
+    )
+    tiles = [reduced[:, s * width : (s + 1) * width] for s in range(kept)]
+    for s in range(kept, group):
+        mirror = group - s
+        sent = reduced[:, mirror * width : (mirror + 1) * width].T
+        tiles.append(lax.ppermute(sent, ("tm", "panel"), mirror_pairs(tile_count, panel_count, group - s)))
+    by_offset = jnp.stack(tiles, axis=0)
+    by_offset = jnp.concatenate([by_offset, by_offset], axis=0)
+    start = (group - device_index % group) % group
+    ordered = lax.dynamic_slice_in_dim(by_offset, start, group, 0)
+    normal = ordered.transpose(1, 0, 2).reshape(width, group * width)
     return (normal, right_hand)
 
 

time: 333 us -> 395 us (1.19); the launches traced: 332 us -> 390 us
  local copies, waits for them, and re-layouts: 16.2 us -> 51.7 us
  other arithmetic: 23 us -> 49.8 us
  starting transfers between devices: 13.9 us -> 30 us
  blocking collectives: 81.4 us -> 66.9 us
  waiting for transfers between devices: 148 us -> 134 us
  matrix products: 33 us -> 40.3 us
    unnamed x3 -> x2, waiting for transfers between devices: 69.9 us -> 0.03 us
    reduce_scatter x0 -> x1, waiting for transfers between devices: none -> 38.8 us  [body(): lax.psum_scatter(stacked, 'tm', scatter_dimension=0, tiled=True)]
    ppermute x0 -> x3, waiting for transfers between devices: none -> 30.8 us  [body(): lax.ppermute(sent, ('tm', 'panel'), mirror_pairs(tile_count, panel_count,...]
    concatenate x0 -> x2, other arithmetic: none -> 23.6 us  [the longest x1 15 us: body(): jnp.concatenate(pieces, axis=0).reshape(tile_count * width, kept * width)]
    reshape x0 -> x2, local copies, waits for them, and re-layouts: none -> 21 us  [the longest x1 18.8 us: body(): row_tiles = gathered.reshape(row_count, panel_count, group, width)]
    all_gather x1, waiting for transfers between devices: 66.5 us -> 45.5 us  [body(): gathered = lax.all_gather(signed_rows, 'panel', axis=1, tiled=True)]
    all_to_all x1 -> x0, blocking collectives: 14.8 us -> none  [body(): lax.all_to_all(send_obs, 'tm', split_axis=0, concat_axis=0, tiled=True)]
    dot_general x1 -> x4, matrix products: 22.9 us -> 32.2 us  [body(): lax.dot_general(row_tiles[:, r], windows, (((0,), (1,)), ((1,), (0,))), p...]
  transfers between devices with their start and end apart: 4 -> 8, of which waited for: 4 -> 6; matrix products, arithmetic and copies ran while one was open for 8% -> 12% of each run, Pallas kernels for 0% -> 0%
where the time goes in v2:
time: 395 us; the launch traced here: 390 us
  waiting for transfers between devices  134 us (34%)
  blocking collectives  66.9 us (17%)
  local copies, waits for them, and re-layouts  51.7 us (13%)
  other arithmetic  49.8 us (13%)
  matrix products  40.3 us (10%)
  starting transfers between devices  30 us (8%)
  between operations  16.9 us (4%)
    psum x1, blocking collectives, body(): right_hand = lax.psum(right_part, 'tm')  66.9 us
    all_gather x1, waiting for transfers between devices, body(): gathered = lax.all_gather(signed_rows, 'panel', axis=1, tiled=True)  45.5 us
    reduce_scatter x1, waiting for transfers between devices, body(): lax.psum_scatter(stacked, 'tm', scatter_dimension=0, tiled=True)  38.8 us
    dot_general x4, matrix products, body(): lax.dot_general(row_tiles[:, r], windows, (((0,), (1,)), ((1,), (0,))), p...  32.2 us
    ppermute x3, waiting for transfers between devices, body(): lax.ppermute(sent, ('tm', 'panel'), mirror_pairs(tile_count, panel_count,...  30.8 us
    reshape x1, local copies, waits for them, and re-layouts, body(): row_tiles = gathered.reshape(row_count, panel_count, group, width)  18.8 us
    concatenate x1, other arithmetic, body(): jnp.concatenate(pieces, axis=0).reshape(tile_count * width, kept * width)  15 us
    all_to_all x1, waiting for transfers between devices, body(): lax.all_to_all(send_design, 'tm', split_axis=0, concat_axis=0, tiled=True)  9.96 us
  transfers between devices with their start and end apart: 8, of which 6 were waited for; matrix products, arithmetic and copies ran while one was open for 12% of the time, Pallas kernels for 0%

profile of v2, /device:TPU:24, one launch (start us, length us, event | category | flops | bytes accessed | tf_op | source)
XLA Modules:
  0.0 389.7 jit_solution(11471922817907603062)
XLA Ops:
  7.2 1.0 copy.44
  8.1 0.5 broadcast.203
  8.7 2.1 fusion.51
  11.1 0.6 reduce-window.6
  12.4 1.4 scatter_custom_fusion
  13.8 0.7 pad_maximum_fusion.3
  14.5 2.8 gather_fusion.2
  17.5 1.4 gather_fusion.1
  19.2 0.8 reshape.244
  19.9 8.2 %all-to-all-start.1 = ((bf16[32,2,384]{2,1,0:T(2,128)(2,1)}), bf16[32,2,384]{2,1,0:T(2,128)(2,1)S(1)}, u32[]{:S(2)}, u32[]{:S(2)}) async-start(bf16[32,2,384]{2,1,0:T(2,128)(2,1)} %reshape.244), calls=%async_computation.1 | async-start | bytes 98304 | tf_op jit(solution)/shard_map/all_to_all | solution.py:84
  28.1 0.7 and_select_fusion
  29.0 2.5 gather_fusion
  31.5 0.4 gather.17
  31.9 1.6 broadcast_select_fusion
  33.6 1.9 all-to-all-done.1
  35.5 5.5 %all-to-all-start = ((bf16[32,12,1920]{2,1,0:T(8,128)(2,1)}), bf16[32,12,1920]{2,1,0:T(8,128)(2,1)S(1)}, u32[]{:S(2)}, u32[]{:S(2)}) async-start(bf16[32,12,1920]{2,1,0:T(8,128)(2,1)} %broadcast_select_fusion), calls=%async_computation | async-start | bytes 3932160 | tf_op jit(solution)/shard_map/all_to_all | solution.py:83
  41.4 0.6 dynamic_slice.13
  42.7 0.6 dynamic_slice.12
  45.0 0.7 fusion.41
  46.1 5.8 %cholesky.17 = f32[64,64]{1,0:T(8,128)S(1)} custom-call(f32[64,64]{1,0:T(8,128)S(1)} %fusion.58), custom_call_target="Cholesky" | custom-call | tf_op jit(solution)/shard_map/jit(cholesky)/cholesky | solution.py:30
  52.0 0.6 compare_reduce_fusion
  52.7 0.7 fusion.50
  53.3 4.9 %custom-call.6 = f32[1,64,64]{1,2,0:T(8,128)S(1)} custom-call(f32[1,64,64]{2,1,0:T(8,128)S(1)} %fusion.50), custom_call_target="InvertDiagBlocksLowerTriangular" | custom-call | tf_op jit(solution)/shard_map/triangular_solve | solution.py:31
  58.5 10.0 %all-to-all-done = bf16[32,12,1920]{2,1,0:T(8,128)(2,1)S(1)} async-done(((bf16[32,12,1920]{2,1,0:T(8,128)(2,1)}), bf16[32,12,1920]{2,1,0:T(8,128)(2,1)S(1)}, u32[]{:S(2)}, u32[]{:S(2)}) %all-to-all-start) | async-done | bytes 1474592 | tf_op jit(solution)/shard_map/all_to_all | solution.py:83
  68.5 0.4 reshape.174
  68.9 1.4 fusion.87
  70.3 1.6 copy-done
  71.9 1.7 fusion.84
  73.5 1.3 pad_maximum_fusion.2
  74.9 0.6 reduce-scatter.2.cloned.1.call-start
  75.4 1.1 fusion.8
  76.5 1.5 fusion.11
  78.1 1.5 fusion.14
  79.6 1.5 fusion.5
  81.0 8.7 %fusion.2 = bf16[448,2880]{1,0:T(8,128)(2,1)S(1)} fusion(bf16[64,1920]{1,0:T(8,128)(2,1)S(1)} %get-tuple-element.7, bf16[384,1920]{1,0:T(8,128)(2,1)S(1)} %get-tuple-element.15), kind=kLoop, calls=%fused_computation.16 | loop fusion | flops 10321920 | bytes 4300800 | tf_op jit(solution)/shard_map/concatenate | solution.py:110
  89.7 1.5 fusion.18
  91.3 1.5 fusion.17
  92.8 1.5 fusion.16
  94.3 1.6 fusion.15
  95.9 45.5 %all-gather.2.cloned.1.call-done = bf16[448,7680]{1,0:T(8,128)(2,1)} async-done(((bf16[448,1920]{1,0:T(8,128)(2,1)}), bf16[448,7680]{1,0:T(8,128)(2,1)}) %all-gather.2.cloned.1.call-update) | async-done | bytes 6881296 | tf_op jit(solution)/shard_map/all_gather | solution.py:103
  141.4 18.8 %reshape.176 = bf16[448,4,8,240]{3,2,1,0:T(8,128)(2,1)} reshape(bf16[448,7680]{1,0:T(8,128)(2,1)} %all-gather.2.cloned.1.call-done) | data formatting | bytes 13762560 | tf_op jit(solution)/shard_map/reshape | solution.py:114
  160.2 3.7 fusion.85
  163.9 6.4 %multiply_convert_fusion = bf16[8,240,1200]{2,1,0:T(8,128)(2,1)S(1)} fusion(bf16[8,448,1200]{2,1,0:T(8,128)(2,1)} %fusion.15, bf16[448,1,8,240]{3,2,1,0:T(8,128)(2,1)S(1)} %get-tuple-element.11), kind=kOutput, calls=%fused_computation.5 | convolution fusion | flops 2068992000 | bytes 14929920 | tf_op jit(solution)/shard_map/dot_general | solution.py:117
  170.3 8.6 %multiply_convert_fusion.1 = bf16[8,240,1200]{2,1,0:T(8,128)(2,1)} fusion(bf16[8,448,1200]{2,1,0:T(8,128)(2,1)} %fusion.15, bf16[448,1,8,240]{3,2,1,0:T(8,128)(2,1)S(1)} %get-tuple-element.9), kind=kOutput, calls=%fused_computation.6 | convolution fusion | flops 2068992000 | bytes 14929920 | tf_op jit(solution)/shard_map/dot_general | solution.py:117
  178.9 8.6 %multiply_convert_fusion.2 = bf16[8,240,1200]{2,1,0:T(8,128)(2,1)} fusion(bf16[8,448,1200]{2,1,0:T(8,128)(2,1)} %fusion.15, bf16[448,1,8,240]{3,2,1,0:T(8,128)(2,1)S(1)} %get-tuple-element.10), kind=kOutput, calls=%fused_computation.7 | convolution fusion | flops 2068992000 | bytes 14929920 | tf_op jit(solution)/shard_map/dot_general | solution.py:117
  187.5 8.6 %multiply_convert_fusion.3 = bf16[8,240,1200]{2,1,0:T(8,128)(2,1)} fusion(bf16[8,448,1200]{2,1,0:T(8,128)(2,1)} %fusion.15, bf16[448,1,8,240]{3,2,1,0:T(8,128)(2,1)S(1)} %get-tuple-element.8), kind=kOutput, calls=%fused_computation.8 | convolution fusion | flops 2068992000 | bytes 14929920 | tf_op jit(solution)/shard_map/dot_general | solution.py:117
  196.1 15.0 %pad_maximum_fusion = bf16[32,240,1200]{2,1,0:T(8,128)(2,1)} fusion(bf16[8,240,1200]{2,1,0:T(8,128)(2,1)S(1)} %multiply_convert_fusion, bf16[8,240,1200]{2,1,0:T(8,128)(2,1)} %multiply_convert_fusion.1, bf16[8,240,1200]{2,1,0:T(8,128)(2,1)} %multiply_convert_fusion.2, bf16[8,240,1200]{2,1,0:T(8,128)(2,1)} %multiply_convert_fusion.3), kind=kLoop, calls=%fused_computation.4 | loop fusion | flops 27648000 | bytes 36864000 | tf_op jit(solution)/shard_map/concatenate | solution.py:122
  211.1 0.7 select_n.100
  211.8 7.6 %all-to-all-start.2 = ((bf16[32,1,12]{2,1,0:T(2,128)(2,1)}), bf16[32,1,12]{2,1,0:T(2,128)(2,1)S(1)}, u32[]{:S(2)}, u32[]{:S(2)}) async-start(bf16[32,1,12]{2,1,0:T(2,128)(2,1)} %select_n.100), calls=%async_computation.3 | async-start | bytes 32768 | tf_op jit(solution)/shard_map/all_to_all | solution.py:85
  219.5 7.3 %all-to-all-done.2 = bf16[32,1,12]{2,1,0:T(2,128)(2,1)S(1)} async-done(((bf16[32,1,12]{2,1,0:T(2,128)(2,1)}), bf16[32,1,12]{2,1,0:T(2,128)(2,1)S(1)}, u32[]{:S(2)}, u32[]{:S(2)}) %all-to-all-start.2) | async-done | bytes 800 | tf_op jit(solution)/shard_map/all_to_all | solution.py:85
  226.7 0.7 reduce.12
  227.4 0.8 reshape.215
  228.2 1.4 convolution_bitcast_fusion
  229.8 0.4 convolution_reduce_fusion
  230.3 1.7 fusion.19
  232.0 66.9 %psum.7 = f32[1920]{0:T(1024)} all-reduce(f32[1920]{0:T(1024)S(1)} %subtract_multiply_fusion), channel_id=1, replica_groups=mesh['tm'=32,'panel'=4] {'tm'}, use_global_device_ids=true, to_apply=%region_9.10 | all-reduce | flops 1920 | bytes 15360 | tf_op jit(solution)/shard_map/psum | solution.py:100
  298.8 38.8 %reduce-scatter.2.cloned.1.call-done = bf16[240,1200]{1,0:T(8,128)(2,1)} async-done(((bf16[7680,1200]{1,0:T(8,128)(2,1)}), bf16[240,1200]{1,0:T(8,128)(2,1)}) %reduce-scatter.2.cloned.1.call-update) | async-done | bytes 576016 | tf_op jit(solution)/shard_map/reduce_scatter | solution.py:123
  337.6 1.3 fusion.86
  339.8 0.9 collective-permute-start.2
  340.6 3.6 collective-permute-start.1
  344.2 3.4 collective-permute-start
  347.9 30.8 %collective-permute-done = f32[240,240]{1,0:T(8,128)S(1)} collective-permute-done((f32[240,240]{1,0:T(8,128)S(1)}, f32[240,240]{1,0:T(8,128)S(1)}, u32[]{:S(2)}, u32[]{:S(2)}) %collective-permute-start) | collective-permute-done | bytes 230432 | tf_op jit(solution)/shard_map/ppermute | solution.py:130
  379.2 1.1 copy.59
  380.4 2.2 reshape.178
  (81 shorter events, 4.8 us)
Async XLA Ops:
  7.2 21.6 %copy-start.5 = (bf16[256,1920]{1,0:T(8,128)(2,1)S(1)}, bf16[256,1920]{1,0:T(8,128)(2,1)}, u32[]{:S(2)}) copy-start(bf16[256,1920]{1,0:T(8,128)(2,1)} %param.6) | copy-start | bytes 2949124
  10.9 2.9 copy-start.3
  19.9 15.6 %all-to-all-start.1 = ((bf16[32,2,384]{2,1,0:T(2,128)(2,1)}), bf16[32,2,384]{2,1,0:T(2,128)(2,1)S(1)}, u32[]{:S(2)}, u32[]{:S(2)}) async-start(bf16[32,2,384]{2,1,0:T(2,128)(2,1)} %reshape.244), calls=%async_computation.1 | async-start | bytes 98304 | tf_op jit(solution)/shard_map/all_to_all | solution.py:84
  31.9 1.7 copy-start.4
  31.9 9.5 %copy-start.8 = (f32[32]{0:T(128)S(1)}, f32[32]{0:T(128)}, u32[]{:S(2)}) copy-start(f32[32]{0:T(128)} %param.11) | copy-start | bytes 388
  31.9 10.8 %copy-start.9 = (f32[32]{0:T(128)S(1)}, f32[32]{0:T(128)}, u32[]{:S(2)}) copy-start(f32[32]{0:T(128)} %param.10) | copy-start | bytes 388
  35.5 33.0 %all-to-all-start = ((bf16[32,12,1920]{2,1,0:T(8,128)(2,1)}), bf16[32,12,1920]{2,1,0:T(8,128)(2,1)S(1)}, u32[]{:S(2)}, u32[]{:S(2)}) async-start(bf16[32,12,1920]{2,1,0:T(8,128)(2,1)} %broadcast_select_fusion), calls=%async_computation | async-start | bytes 3932160 | tf_op jit(solution)/shard_map/all_to_all | solution.py:83
  41.0 100.3 %all-gather.2.cloned.1.call-start = ((), (), s32[]{:S(2)}) async-start(), calls=%async_computation.4 | async-start | bytes 8601600 | tf_op jit(solution)/shard_map/all_gather | solution.py:103
  44.7 24.1 %copy-start.6 = (s32[384]{0:T(512)}, s32[384]{0:T(512)S(1)}, u32[]{:S(2)}) copy-start(s32[384]{0:T(512)S(1)} %add.122) | copy-start | bytes 4612
  44.8 24.0 %copy-start.7 = (pred[384]{0:T(512)(128)(4,1)}, pred[384]{0:T(512)(128)(4,1)S(1)}, u32[]{:S(2)}) copy-start(pred[384]{0:T(512)(128)(4,1)S(1)} %lt.85) | copy-start | bytes 1156
  70.3 1.6 copy-start
  74.9 262.8 %reduce-scatter.2.cloned.1.call-start = ((), (), s32[]{:S(2)}) async-start(), calls=%async_computation.5 | async-start | bytes 20275200 | tf_op jit(solution)/shard_map/reduce_scatter | solution.py:123
  211.1 19.2 %copy-start.1 = (f32[384,1920]{1,0:T(8,128)S(1)}, f32[384,1920]{1,0:T(8,128)}, u32[]{:S(2)}) copy-start(f32[384,1920]{1,0:T(8,128)} %copy-done) | copy-start | bytes 8847364
  211.8 14.9 %all-to-all-start.2 = ((bf16[32,1,12]{2,1,0:T(2,128)(2,1)}), bf16[32,1,12]{2,1,0:T(2,128)(2,1)S(1)}, u32[]{:S(2)}, u32[]{:S(2)}) async-start(bf16[32,1,12]{2,1,0:T(2,128)(2,1)} %select_n.100), calls=%async_computation.3 | async-start | bytes 32768 | tf_op jit(solution)/shard_map/all_to_all | solution.py:85
  337.6 10.0 %copy-start.2 = (bf16[240,1200]{1,0:T(8,128)(2,1)S(1)}, bf16[240,1200]{1,0:T(8,128)(2,1)}, u32[]{:S(2)}) copy-start(bf16[240,1200]{1,0:T(8,128)(2,1)} %reduce-scatter.2.cloned.1.call-done) | copy-start | bytes 1728004
  339.8 39.0 %collective-permute-start.2 = (f32[240,240]{1,0:T(8,128)S(1)}, f32[240,240]{1,0:T(8,128)S(1)}, u32[]{:S(2)}, u32[]{:S(2)}) collective-permute-start(f32[240,240]{1,0:T(8,128)S(1)} %bitcast.141), channel_id=1, source_target_pairs={{0,4},{1,36},{2,68},{3,100},{4,8},{5,40},{6,72},{7,104},{8,12},{9,... | collective-permute-start | bytes 691208 | tf_op jit(solution)/shard_map/ppermute | solution.py:130
  340.6 38.1 %collective-permute-start.1 = (f32[240,240]{1,0:T(8,128)S(1)}, f32[240,240]{1,0:T(8,128)S(1)}, u32[]{:S(2)}, u32[]{:S(2)}) collective-permute-start(f32[240,240]{1,0:T(8,128)S(1)} %bitcast.143), channel_id=1, source_target_pairs={{0,8},{1,40},{2,72},{3,104},{4,12},{5,44},{6,76},{7,108},{8,16},{9... | collective-permute-start | bytes 691208 | tf_op jit(solution)/shard_map/ppermute | solution.py:130
  344.2 34.4 %collective-permute-start = (f32[240,240]{1,0:T(8,128)S(1)}, f32[240,240]{1,0:T(8,128)S(1)}, u32[]{:S(2)}, u32[]{:S(2)}) collective-permute-start(f32[240,240]{1,0:T(8,128)S(1)} %bitcast.145), channel_id=1, source_target_pairs={{0,12},{1,44},{2,76},{3,108},{4,16},{5,48},{6,80},{7,112},{8,20},{... | collective-permute-start | bytes 691208 | tf_op jit(solution)/shard_map/ppermute | solution.py:130
Sparse Core Ops, SparseCore 0:
  75.0 66.3 all-gather.1
  211.2 126.3 reduce-scatter.1

commit v3 on v2

--- a/solution.py
+++ b/solution.py
@@ -1,6 +1,9 @@
+import functools
+
 import jax
 import jax.numpy as jnp
 from jax import lax
+from jax.experimental import pallas as pl
 from jax.sharding import PartitionSpec as P
 
 
@@ -36,6 +39,39 @@
         - jnp.dot(arc_terms.T, arc_rhs, precision=lax.Precision.HIGHEST)
     ) * scale
     return (white_design.astype(jnp.bfloat16), arc_terms.astype(jnp.bfloat16), right_part)
+
+
+def window_kernel(group, width, kept, scale, rows_ref, cols_ref, rider_ref, out_ref):
+    tile = pl.program_id(0)
+    start = pl.multiple_of((tile % group) * width, 16)
+    window = cols_ref[pl.ds(start, kept * width), :]
+    product = lax.dot_general(
+        rows_ref[...], window, (((1,), (1,)), ((), ())), preferred_element_type=jnp.float32
+    )
+    out_ref[:width, :] = (product * scale).astype(out_ref.dtype)
+    out_ref[width:, :] = rider_ref[...]
+
+
+def window_products(rows, cols, riders, group, width, kept, scale):
+    tile_count = rows.shape[0] // width
+    depth = rows.shape[1]
+    chunk = width + riders.shape[0]
+    return pl.pallas_call(
+        functools.partial(window_kernel, group, width, kept, scale),
+        out_shape=jax.ShapeDtypeStruct((tile_count * chunk, kept * width), jnp.bfloat16),
+        grid=(tile_count,),
+        in_specs=[
+            pl.BlockSpec((width, depth), lambda t: (t, 0)),
+            pl.BlockSpec(cols.shape, lambda t: (0, 0)),
+            pl.BlockSpec(riders.shape, lambda t: (0, 0)),
+        ],
+        out_specs=pl.BlockSpec((chunk, kept * width), lambda t: (t, 0)),
+        cost_estimate=pl.CostEstimate(
+            flops=2 * tile_count * width * kept * width * depth,
+            bytes_accessed=2 * (rows.size + cols.size + tile_count * chunk * kept * width),
+            transcendentals=0,
+        ),
+    )(rows, cols, riders)
 
 
 def mirror_pairs(tile_count, panel_count, offset):
@@ -97,32 +133,23 @@
         order_pos, order_pos, usable, usable, autoreg[device_index], movavg[device_index]
     )
     design_bf, terms_bf, right_part = eliminate(whitener, got_design, got_params, got_obs, scale)
-    right_hand = lax.psum(right_part, "tm")
-    own_rows = jnp.concatenate([design_bf, terms_bf], axis=0)
-    signed_rows = jnp.concatenate([design_bf, -terms_bf], axis=0)
-    gathered = lax.all_gather(signed_rows, "panel", axis=1, tiled=True)
+    own_rows = jnp.concatenate([design_bf, terms_bf], axis=0).T
+    signed_rows = jnp.concatenate([design_bf, -terms_bf], axis=0).T
+    gathered = lax.all_gather(signed_rows, "panel", axis=0, tiled=True)
     panel_count = lax.axis_size("panel")
-    panel_index = lax.axis_index("panel")
     group = tile_count // panel_count
     width = panel_width // group
     kept = group // 2 + 1
-    row_count = gathered.shape[0]
-    doubled = jnp.concatenate([own_rows, own_rows[:, : (kept - 1) * width]], axis=1)
-    windows = jnp.stack(
-        [doubled[:, k * width : (k + kept) * width] for k in range(group)]
-    )
-    row_tiles = gathered.reshape(row_count, panel_count, group, width)
-    pieces = []
-    for r in range(panel_count):
-        block = lax.dot_general(
-            row_tiles[:, r], windows, (((0,), (1,)), ((1,), (0,))),
-            preferred_element_type=jnp.float32,
-        )
-        pieces.append((block * scale).astype(jnp.bfloat16))
-    stacked = jnp.concatenate(pieces, axis=0).reshape(tile_count * width, kept * width)
-    reduced = lax.psum_scatter(stacked, "tm", scatter_dimension=0, tiled=True).astype(
+    doubled = jnp.concatenate([own_rows, own_rows[: (kept - 1) * width]], axis=0)
+    spare = 8
+    riders = jnp.zeros((spare * kept * width,), jnp.float32).at[: right_part.shape[0]].set(right_part)
+    riders = riders.reshape(spare, kept * width).astype(jnp.bfloat16)
+    stacked = window_products(gathered, doubled, riders, group, width, kept, scale)
+    summed = lax.psum_scatter(stacked, "tm", scatter_dimension=0, tiled=True).astype(
         jnp.float32
     )
+    reduced = summed[:width]
+    right_hand = summed[width:].reshape(-1)[: right_part.shape[0]]
     tiles = [reduced[:, s * width : (s + 1) * width] for s in range(kept)]
     for s in range(kept, group):
         mirror = group - s

time: 395 us -> 379 us (0.959)
  waiting for transfers between devices: 134 us -> 232 us
  blocking collectives: 66.9 us -> 11.1 us
  matrix products: 40.3 us -> 9.42 us
  Pallas kernels: 0 us -> 30.1 us
  local copies, waits for them, and re-layouts: 51.7 us -> 28.4 us
  other arithmetic: 49.8 us -> 27.8 us
  starting transfers between devices: 30 us -> 21.8 us
    reduce_scatter x1, waiting for transfers between devices: 38.8 us -> 137 us  [body(): lax.psum_scatter(stacked, 'tm', scatter_dimension=0, tiled=True)]
    psum x1 -> x0, blocking collectives: 66.9 us -> none  [body(): right_hand = lax.psum(right_part, 'tm')]
    dot_general x4 -> x0, matrix products: 32.2 us -> none  [body(): lax.dot_general(row_tiles[:, r], windows, (((0,), (1,)), ((1,), (0,))), p...]
    pallas_call x0 -> x1, Pallas kernels: none -> 30.1 us  [window_products(): pl.pallas_call(functools.partial(window_kernel, group, width, kept, scale...]
    concatenate x3 -> x1, other arithmetic: 25 us -> 3.63 us  [body(): doubled = jnp.concatenate([own_rows, own_rows[:(kept - 1) * width]], axis=0)]
    reshape x1, local copies, waits for them, and re-layouts: 18.8 us -> 0.09 us  [body(): right_hand = summed[width:].reshape(-1)[:right_part.shape[0]]]
    all_to_all x0 -> x1, blocking collectives: none -> 11.1 us  [body(): lax.all_to_all(send_obs, 'tm', split_axis=0, concat_axis=0, tiled=True)]
    all_to_all x1 -> x0, starting transfers between devices: 7.6 us -> none  [body(): lax.all_to_all(send_obs, 'tm', split_axis=0, concat_axis=0, tiled=True)]
  transfers between devices with their start and end apart: 8 -> 7, of which waited for: 6 -> 5; matrix products, arithmetic and copies ran while one was open for 12% -> 9% of each run, Pallas kernels for 0% -> 0%
where the time goes in v3:
time: 379 us; the launch traced here: 377 us
  waiting for transfers between devices  232 us (61%)
  Pallas kernels  30.1 us (8%)
  local copies, waits for them, and re-layouts  28.4 us (7%)
  other arithmetic  27.8 us (7%)
  starting transfers between devices  21.8 us (6%)
  between operations  16.6 us (4%)
  blocking collectives  11.1 us (3%)
  matrix products  9.42 us (2%)
    reduce_scatter x1, waiting for transfers between devices, body(): lax.psum_scatter(stacked, 'tm', scatter_dimension=0, tiled=True)  137 us
    all_gather x1, waiting for transfers between devices, body(): gathered = lax.all_gather(signed_rows, 'panel', axis=0, tiled=True)  52.1 us
    ppermute x3, waiting for transfers between devices, body(): lax.ppermute(sent, ('tm', 'panel'), mirror_pairs(tile_count, panel_count,...  31.2 us
    pallas_call x1, Pallas kernels, window_products(): pl.pallas_call(functools.partial(window_kernel, group, width, kept, scale...  30.1 us
    all_to_all x1, blocking collectives, body(): lax.all_to_all(send_obs, 'tm', split_axis=0, concat_axis=0, tiled=True)  11.1 us
    all_to_all x1, waiting for transfers between devices, body(): lax.all_to_all(send_design, 'tm', split_axis=0, concat_axis=0, tiled=True)  10.1 us
    all_to_all x1, starting transfers between devices, body(): lax.all_to_all(send_params, 'tm', split_axis=0, concat_axis=0, tiled=True)  8.16 us
    ppermute x3, starting transfers between devices, body(): lax.ppermute(sent, ('tm', 'panel'), mirror_pairs(tile_count, panel_count,...  7.89 us
  transfers between devices with their start and end apart: 7, of which 5 were waited for; matrix products, arithmetic and copies ran while one was open for 9% of the time, Pallas kernels for 0%

profile of v3, /device:TPU:24, one launch (start us, length us, event | category | flops | bytes accessed | tf_op | source)
XLA Modules:
  0.0 377.5 jit_solution(1464243182687743627)
XLA Ops:
  7.2 1.0 copy.40
  8.1 0.5 broadcast.212
  8.7 2.1 fusion.36
  10.9 0.2 dynamic-slice_reduce_fusion
  11.1 0.6 reduce-window.6
  11.7 0.2 slice_reduce_fusion
  12.0 0.1 copy.38
  12.2 0.2 fusion.34
  12.4 1.4 scatter_custom_fusion
  13.8 0.7 pad_maximum_fusion.3
  14.5 2.8 gather_fusion.2
  17.5 1.4 gather_fusion.1
  19.0 0.1 broadcast_select_fusion.1
  19.2 0.8 reshape.264
  19.9 8.2 %all-to-all-start.1 = ((bf16[32,2,384]{2,1,0:T(2,128)(2,1)}), bf16[32,2,384]{2,1,0:T(2,128)(2,1)S(1)}, u32[]{:S(2)}, u32[]{:S(2)}) async-start(bf16[32,2,384]{2,1,0:T(2,128)(2,1)} %reshape.264), calls=%async_computation.1 | async-start | bytes 98304 | tf_op jit(solution)/shard_map/all_to_all | solution.py:120
  28.1 0.7 and_select_fusion
  28.8 0.2 concatenate.24
  29.0 2.5 gather_fusion
  31.5 0.4 gather.17
  31.9 1.6 broadcast_select_fusion
  33.6 1.9 all-to-all-done.1
  35.5 5.5 %all-to-all-start = ((bf16[32,12,1920]{2,1,0:T(8,128)(2,1)}), bf16[32,12,1920]{2,1,0:T(8,128)(2,1)S(1)}, u32[]{:S(2)}, u32[]{:S(2)}) async-start(bf16[32,12,1920]{2,1,0:T(8,128)(2,1)} %broadcast_select_fusion), calls=%async_computation | async-start | bytes 3932160 | tf_op jit(solution)/shard_map/all_to_all | solution.py:119
  41.0 0.2 all-gather.2.cloned.1.call-start
  41.3 0.6 dynamic_slice.13
  42.6 0.6 dynamic_slice.12
  44.9 0.7 fusion.26
  45.7 0.2 fusion.70
  46.0 5.8 %cholesky.17 = f32[64,64]{1,0:T(8,128)S(1)} custom-call(f32[64,64]{1,0:T(8,128)S(1)} %fusion.43), custom_call_target="Cholesky" | custom-call | tf_op jit(solution)/shard_map/jit(cholesky)/cholesky | solution.py:33
  51.9 0.6 compare_reduce_fusion
  52.6 0.7 fusion.35
  53.2 4.9 %custom-call.6 = f32[1,64,64]{1,2,0:T(8,128)S(1)} custom-call(f32[1,64,64]{2,1,0:T(8,128)S(1)} %fusion.35), custom_call_target="InvertDiagBlocksLowerTriangular" | custom-call | tf_op jit(solution)/shard_map/triangular_solve | solution.py:34
  58.1 0.3 fusion.40
  58.4 10.1 %all-to-all-done = bf16[32,12,1920]{2,1,0:T(8,128)(2,1)S(1)} async-done(((bf16[32,12,1920]{2,1,0:T(8,128)(2,1)}), bf16[32,12,1920]{2,1,0:T(8,128)(2,1)S(1)}, u32[]{:S(2)}, u32[]{:S(2)}) %all-to-all-start) | async-done | bytes 1474592 | tf_op jit(solution)/shard_map/all_to_all | solution.py:119
  68.5 1.3 reshape.195
  69.8 2.7 fusion.28
  72.5 1.7 copy.39
  74.2 1.6 fusion.71
  75.9 1.0 copy.42
  76.9 1.1 neg.11
  78.0 3.8 %fusion.3 = (bf16[1920,448]{1,0:T(8,128)(2,1)}, bf16[1920,448]{1,0:T(8,128)(2,1)}) fusion(bf16[384,1920]{0,1:T(8,128)(2,1)} %copy.39, bf16[64,1920]{0,1:T(8,128)(2,1)} %copy.42, bf16[64,1920]{0,1:T(8,128)(2,1)S(1)} %neg.11), kind=kLoop, calls=%fused_computation.10 | loop fusion | flops 6021120 | bytes 5406720 | tf_op jit(solution)/shard_map/transpose | solution.py:136
  81.9 0.7 select_n.100
  82.6 11.1 %all_to_all.16 = bf16[32,1,12]{2,1,0:T(2,128)(2,1)S(1)} all-to-all(bf16[32,1,12]{2,1,0:T(2,128)(2,1)} %select_n.100), channel_id=1, replica_groups=mesh['tm'=32,'panel'=4] {'tm'}, dimensions={0} | all-to-all | bytes 1536 | tf_op jit(solution)/shard_map/all_to_all | solution.py:121
  93.7 0.7 reduce.14
  94.4 0.8 reshape.235
  95.2 1.5 convolution_bitcast_fusion
  96.6 0.2 convolution_bitcast_fusion.1
  96.8 0.4 convolution_reduce_fusion
  97.3 1.7 fusion.4
  99.0 0.7 convert_element_type.56.rider_ref
  99.7 1.3 slice.77
  101.0 3.6 pad_maximum_fusion.cols_ref
  104.6 52.1 %all-gather.2.cloned.1.call-done.rows_ref = bf16[7680,448]{1,0:T(8,128)(2,1)} async-done(((bf16[1920,448]{1,0:T(8,128)(2,1)}), bf16[7680,448]{1,0:T(8,128)(2,1)}) %all-gather.2.cloned.1.call-update) | async-done | bytes 6881296 | tf_op jit(solution)/shard_map/all_gather | solution.py:138
  156.7 30.1 %shard_map.77 = bf16[7936,1200]{1,0:T(8,128)(2,1)} custom-call(bf16[7680,448]{1,0:T(8,128)(2,1)} %all-gather.2.cloned.1.call-done.rows_ref, bf16[2880,448]{1,0:T(8,128)(2,1)} %pad_maximum_fusion.cols_ref, bf16[8,1200]{1,0:T(8,128)(2,1)} %convert_element_type.56.rider_ref), custom_call_target="tpu_custom_call" | custom-call | flops 8257536000 | bytes 28508160 | tf_op jit(solution)/shard_map/pallas_call | solution.py:59
  186.9 136.9 %reduce-scatter.2.cloned.1.call-done = bf16[248,1200]{1,0:T(8,128)(2,1)} async-done(((bf16[7936,1200]{1,0:T(8,128)(2,1)}), bf16[248,1200]{1,0:T(8,128)(2,1)}) %reduce-scatter.2.cloned.1.call-update) | async-done | bytes 595216 | tf_op jit(solution)/shard_map/reduce_scatter | solution.py:148
  323.7 0.8 slice.83
  324.6 0.6 slice.84
  325.2 1.3 fusion.69
  327.3 1.2 collective-permute-start.2
  328.6 3.6 collective-permute-start.1
  332.1 3.1 collective-permute-start
  335.5 31.2 %collective-permute-done = f32[240,240]{1,0:T(8,128)S(1)} collective-permute-done((f32[240,240]{1,0:T(8,128)S(1)}, f32[240,240]{1,0:T(8,128)S(1)}, u32[]{:S(2)}, u32[]{:S(2)}) %collective-permute-start) | collective-permute-done | bytes 230432 | tf_op jit(solution)/shard_map/ppermute | solution.py:157
  367.1 0.1 dynamic-slice_bitcast_fusion
  367.3 1.1 copy.53
  368.4 2.2 reshape.198
  (70 shorter events, 2.7 us)
Async XLA Ops:
  7.2 21.6 %copy-start.3 = (bf16[256,1920]{1,0:T(8,128)(2,1)S(1)}, bf16[256,1920]{1,0:T(8,128)(2,1)}, u32[]{:S(2)}) copy-start(bf16[256,1920]{1,0:T(8,128)(2,1)} %param.8) | copy-start | bytes 2949124
  10.9 2.9 copy-start.1
  19.9 15.6 %all-to-all-start.1 = ((bf16[32,2,384]{2,1,0:T(2,128)(2,1)}), bf16[32,2,384]{2,1,0:T(2,128)(2,1)S(1)}, u32[]{:S(2)}, u32[]{:S(2)}) async-start(bf16[32,2,384]{2,1,0:T(2,128)(2,1)} %reshape.264), calls=%async_computation.1 | async-start | bytes 98304 | tf_op jit(solution)/shard_map/all_to_all | solution.py:120
  31.9 1.7 copy-start.2
  31.9 9.4 %copy-start.6 = (f32[32]{0:T(128)S(1)}, f32[32]{0:T(128)}, u32[]{:S(2)}) copy-start(f32[32]{0:T(128)} %param.13) | copy-start | bytes 388
  31.9 10.7 %copy-start.7 = (f32[32]{0:T(128)S(1)}, f32[32]{0:T(128)}, u32[]{:S(2)}) copy-start(f32[32]{0:T(128)} %param.12) | copy-start | bytes 388
  35.5 33.0 %all-to-all-start = ((bf16[32,12,1920]{2,1,0:T(8,128)(2,1)}), bf16[32,12,1920]{2,1,0:T(8,128)(2,1)S(1)}, u32[]{:S(2)}, u32[]{:S(2)}) async-start(bf16[32,12,1920]{2,1,0:T(8,128)(2,1)} %broadcast_select_fusion), calls=%async_computation | async-start | bytes 3932160 | tf_op jit(solution)/shard_map/all_to_all | solution.py:119
  41.0 115.6 %all-gather.2.cloned.1.call-start = ((), (), s32[]{:S(2)}) async-start(), calls=%async_computation.4 | async-start | bytes 9830400 | tf_op jit(solution)/shard_map/all_gather | solution.py:138
  44.6 25.2 %copy-start.4 = (s32[384]{0:T(512)}, s32[384]{0:T(512)S(1)}, u32[]{:S(2)}) copy-start(s32[384]{0:T(512)S(1)} %add.124) | copy-start | bytes 4612
  44.7 25.0 %copy-start.5 = (pred[384]{0:T(512)(128)(4,1)}, pred[384]{0:T(512)(128)(4,1)S(1)}, u32[]{:S(2)}) copy-start(pred[384]{0:T(512)(128)(4,1)S(1)} %lt.85) | copy-start | bytes 1156
  81.8 241.9 %reduce-scatter.2.cloned.1.call-start = ((), (), s32[]{:S(2)}) async-start(), calls=%async_computation.5 | async-start | bytes 20951040 | tf_op jit(solution)/shard_map/reduce_scatter | solution.py:148
  323.7 11.5 %copy-start = (bf16[248,1200]{1,0:T(8,128)(2,1)S(1)}, bf16[248,1200]{1,0:T(8,128)(2,1)}, u32[]{:S(2)}) copy-start(bf16[248,1200]{1,0:T(8,128)(2,1)} %reduce-scatter.2.cloned.1.call-done) | copy-start | bytes 1785604
  327.3 39.4 %collective-permute-start.2 = (f32[240,240]{1,0:T(8,128)S(1)}, f32[240,240]{1,0:T(8,128)S(1)}, u32[]{:S(2)}, u32[]{:S(2)}) collective-permute-start(f32[240,240]{1,0:T(8,128)S(1)} %bitcast.95), channel_id=1, source_target_pairs={{0,4},{1,36},{2,68},{3,100},{4,8},{5,40},{6,72},{7,104},{8,12},{9,... | collective-permute-start | bytes 691208 | tf_op jit(solution)/shard_map/ppermute | solution.py:157
  328.6 38.2 %collective-permute-start.1 = (f32[240,240]{1,0:T(8,128)S(1)}, f32[240,240]{1,0:T(8,128)S(1)}, u32[]{:S(2)}, u32[]{:S(2)}) collective-permute-start(f32[240,240]{1,0:T(8,128)S(1)} %bitcast.97), channel_id=1, source_target_pairs={{0,8},{1,40},{2,72},{3,104},{4,12},{5,44},{6,76},{7,108},{8,16},{9... | collective-permute-start | bytes 691208 | tf_op jit(solution)/shard_map/ppermute | solution.py:157
  332.1 34.6 %collective-permute-start = (f32[240,240]{1,0:T(8,128)S(1)}, f32[240,240]{1,0:T(8,128)S(1)}, u32[]{:S(2)}, u32[]{:S(2)}) collective-permute-start(f32[240,240]{1,0:T(8,128)S(1)} %bitcast.99), channel_id=1, source_target_pairs={{0,12},{1,44},{2,76},{3,108},{4,16},{5,48},{6,80},{7,112},{8,20},{... | collective-permute-start | bytes 691208 | tf_op jit(solution)/shard_map/ppermute | solution.py:157
Sparse Core Ops, SparseCore 0:
  82.0 74.6 all-gather.1
  186.9 136.7 reduce-scatter.1

commit v4 on v1

--- a/solution.py
+++ b/solution.py
@@ -43,8 +43,9 @@
 def body(design, partials, observed, arc_of_row, autoreg, movavg):
     chip_count = lax.axis_size("tmc")
     core_count = lax.axis_size("core")
+    core_index = lax.axis_index("core")
     tile_count = chip_count * core_count
-    device_index = lax.axis_index("tmc") * core_count + lax.axis_index("core")
+    device_index = lax.axis_index("tmc") * core_count + core_index
     rows_dev = design.shape[0]
     panel_width = design.shape[1]
     param_count = partials.shape[1]
@@ -93,23 +94,23 @@
     design_bf, terms_bf, right_part = eliminate(whitener, got_design, got_params, got_obs, scale)
     right_hand = lax.psum(right_part, TM)
     own_rows = jnp.concatenate([design_bf, terms_bf], axis=0)
-    signed_rows = jnp.concatenate([design_bf, -terms_bf], axis=0)
-    gathered = lax.all_gather(signed_rows, "panel", axis=1, tiled=True)
-    coeff_count = gathered.shape[1]
-    block_rows = coeff_count // tile_count
-    gathered = (
-        gathered.reshape(-1, chip_count, core_count, block_rows)
-        .transpose(0, 2, 1, 3)
-        .reshape(-1, coeff_count)
+    signed_rows = jnp.concatenate([design_bf, -terms_bf], axis=0).T
+    gathered = lax.all_gather(signed_rows, "panel", axis=0, tiled=True)
+    block_rows = gathered.shape[0] // tile_count
+    by_core = gathered.reshape(chip_count, core_count, block_rows, gathered.shape[1])
+    swap = [(0, 1), (1, 0)]
+    kept_rows = lax.dynamic_index_in_dim(by_core, core_index, 1, keepdims=False)
+    given_rows = lax.dynamic_index_in_dim(by_core, 1 - core_index, 1, keepdims=False)
+    got_rows = lax.ppermute(given_rows, "core", swap)
+    got_cols = lax.ppermute(own_rows, "core", swap)
+    row_side = jnp.concatenate([kept_rows, got_rows], axis=2).reshape(
+        chip_count * block_rows, -1
     )
-    product = lax.dot_general(
-        gathered, own_rows, (((0,), (0,)), ((), ())), preferred_element_type=jnp.float32
-    )
-    partial = (product * scale).astype(jnp.bfloat16)
-    partial = lax.psum_scatter(partial, "core", scatter_dimension=0, tiled=True)
-    normal = lax.psum_scatter(partial, "tmc", scatter_dimension=0, tiled=True).astype(
-        jnp.float32
-    )
+    col_side = jnp.concatenate([own_rows, got_cols], axis=0)
+    product = jnp.dot(row_side, col_side, preferred_element_type=jnp.float32)
+    normal = lax.psum_scatter(
+        (product * scale).astype(jnp.bfloat16), "tmc", scatter_dimension=0, tiled=True
+    ).astype(jnp.float32)
     return (normal, right_hand)
 
 

time: 384 us -> 379 us (0.987)
  waiting for transfers between devices: 146 us -> 97.7 us
  local copies, waits for them, and re-layouts: 68.1 us -> 112 us
    reduce_scatter x1 -> x0, waiting for transfers between devices: 45.5 us -> none  [body(): partial = lax.psum_scatter(partial, 'core', scatter_dimension=0, tiled=True)]
    dynamic_slice x0 -> x1, local copies, waits for them, and re-layouts: none -> 35 us  [body(): kept_rows = lax.dynamic_index_in_dim(by_core, core_index, 1, keepdims=False)]
    reshape x3 -> x1, local copies, waits for them, and re-layouts: 51.9 us -> 29.2 us  [body(): gathered.reshape(chip_count, core_count, block_rows, gathered.shape[1])]
    concatenate x0 -> x2, local copies, waits for them, and re-layouts: none -> 16.1 us  [body(): jnp.concatenate([kept_rows, got_rows], axis=2)]
    unnamed x20 -> x23, local copies, waits for them, and re-layouts: 2.4 us -> 12 us
    ppermute x0 -> x1, local copies, waits for them, and re-layouts: none -> 5.92 us  [body(): got_rows = lax.ppermute(given_rows, 'core', swap)]
    unnamed x4 -> x3, waiting for transfers between devices: 22.5 us -> 19.5 us
  transfers between devices with their start and end apart: 5 -> 6, of which waited for: 5 -> 4; matrix products, arithmetic and copies ran while one was open for 7% -> 13% of each run, Pallas kernels for 0% -> 0%
where the time goes in v4:
time: 379 us; the launch traced here: 378 us
  local copies, waits for them, and re-layouts  112 us (30%)
  waiting for transfers between devices  97.7 us (26%)
  blocking collectives  82 us (22%)
  matrix products  31.1 us (8%)
  other arithmetic  23.7 us (6%)
  between operations  16.4 us (4%)
  starting transfers between devices  14.6 us (4%)
    psum x1, blocking collectives, body(): right_hand = lax.psum(right_part, TM)  67.2 us
    all_gather x1, waiting for transfers between devices, body(): gathered = lax.all_gather(signed_rows, 'panel', axis=0, tiled=True)  66.2 us
    dynamic_slice x1, local copies, waits for them, and re-layouts, body(): kept_rows = lax.dynamic_index_in_dim(by_core, core_index, 1, keepdims=False)  35 us
    reshape x1, local copies, waits for them, and re-layouts, body(): gathered.reshape(chip_count, core_count, block_rows, gathered.shape[1])  29.2 us
    dot_general x1, matrix products, body(): product = jnp.dot(row_side, col_side, preferred_element_type=jnp.float32)  21.7 us
    unnamed x3, waiting for transfers between devices  19.5 us
    concatenate x2, local copies, waits for them, and re-layouts, body(): jnp.concatenate([kept_rows, got_rows], axis=2)  16.1 us
    all_to_all x1, blocking collectives, body(): lax.all_to_all(send_obs, TM, split_axis=0, concat_axis=0, tiled=True)  14.8 us
  transfers between devices with their start and end apart: 6, of which 4 were waited for; matrix products, arithmetic and copies ran while one was open for 13% of the time, Pallas kernels for 0%

profile of v4, /device:TPU:24, one launch (start us, length us, event | category | flops | bytes accessed | tf_op | source)
XLA Modules:
  0.0 377.6 jit_solution(7968733083437564356)
XLA Ops:
  7.2 1.0 copy.19
  8.1 0.5 broadcast.194
  8.7 2.1 fusion.38
  10.9 0.2 dynamic-slice_reduce_fusion.1
  11.1 0.6 reduce-window.6
  11.7 0.2 slice_reduce_fusion
  11.9 0.1 fusion.41
  12.0 0.1 copy.18
  12.2 0.2 fusion.36
  12.4 1.4 scatter_custom_fusion
  13.8 0.7 pad_maximum_fusion.1
  14.5 2.8 gather_fusion.2
  17.4 0.1 broadcast_in_dim.54
  17.5 1.4 gather_fusion.1
  19.0 0.1 broadcast_select_fusion.1
  19.2 0.8 reshape.243
  19.9 8.2 %all-to-all-start.1 = ((bf16[32,2,384]{2,1,0:T(2,128)(2,1)}), bf16[32,2,384]{2,1,0:T(2,128)(2,1)S(1)}, u32[]{:S(2)}, u32[]{:S(2)}) async-start(bf16[32,2,384]{2,1,0:T(2,128)(2,1)} %reshape.243), calls=%async_computation.1 | async-start | bytes 98304 | tf_op jit(solution)/shard_map/all_to_all | solution.py:79
  28.1 0.7 and_select_fusion
  28.8 0.2 concatenate.27
  29.0 2.5 gather_fusion
  31.5 0.4 gather.17
  31.9 1.6 broadcast_select_fusion
  33.6 1.9 all-to-all-done.1
  35.6 5.5 %all-to-all-start = ((bf16[32,12,1920]{2,1,0:T(8,128)(2,1)}), bf16[32,12,1920]{2,1,0:T(8,128)(2,1)S(1)}, u32[]{:S(2)}, u32[]{:S(2)}) async-start(bf16[32,12,1920]{2,1,0:T(8,128)(2,1)} %broadcast_select_fusion), calls=%async_computation | async-start | bytes 3932160 | tf_op jit(solution)/shard_map/all_to_all | solution.py:78
  41.0 0.2 all-gather.2.cloned.1.call-start
  41.4 0.6 dynamic_slice.17
  42.6 0.6 dynamic_slice.16
  44.5 0.1 add.124
  44.6 0.1 lt.79
  44.8 0.1 reshape.244
  44.9 0.7 fusion.32
  45.7 0.2 fusion.74
  46.1 5.8 %cholesky.17 = f32[64,64]{1,0:T(8,128)S(1)} custom-call(f32[64,64]{1,0:T(8,128)S(1)} %fusion.45), custom_call_target="Cholesky" | custom-call | tf_op jit(solution)/shard_map/jit(cholesky)/cholesky | solution.py:32
  51.9 0.6 compare_reduce_fusion
  52.6 0.7 fusion.37
  53.2 4.9 %custom-call.6 = f32[1,64,64]{1,2,0:T(8,128)S(1)} custom-call(f32[1,64,64]{2,1,0:T(8,128)S(1)} %fusion.37), custom_call_target="InvertDiagBlocksLowerTriangular" | custom-call | tf_op jit(solution)/shard_map/triangular_solve | solution.py:33
  58.1 0.3 fusion.42
  58.4 10.1 %all-to-all-done = bf16[32,12,1920]{2,1,0:T(8,128)(2,1)S(1)} async-done(((bf16[32,12,1920]{2,1,0:T(8,128)(2,1)}), bf16[32,12,1920]{2,1,0:T(8,128)(2,1)S(1)}, u32[]{:S(2)}, u32[]{:S(2)}) %all-to-all-start) | async-done | bytes 1474592 | tf_op jit(solution)/shard_map/all_to_all | solution.py:78
  68.5 1.3 reshape.172
  69.8 2.7 fusion.73
  72.5 1.7 fusion.72
  74.2 0.7 copy-done.4
  74.9 2.0 pad_maximum_fusion
  76.9 0.3 reduce-scatter.4.cloned.1.call-start
  77.2 66.2 %all-gather.2.cloned.1.call-done = bf16[7680,448]{0,1:T(8,128)(2,1)} async-done(((bf16[1920,448]{0,1:T(8,128)(2,1)}), bf16[7680,448]{0,1:T(8,128)(2,1)}) %all-gather.2.cloned.1.call-update) | async-done | bytes 6881296 | tf_op jit(solution)/shard_map/all_gather | solution.py:98
  143.4 29.2 %reshape.174 = bf16[16,2,240,448]{2,1,0,3:T(2,128)(2,1)} reshape(bf16[7680,448]{0,1:T(8,128)(2,1)} %all-gather.2.cloned.1.call-done) | data formatting | bytes 13762560 | tf_op jit(solution)/shard_map/reshape | solution.py:100
  172.7 35.0 %dynamic-slice_reduce_fusion = (bf16[16,240,448]{1,0,2:T(8,128)(2,1)}, bf16[16,1,240,448]{2,1,0,3:T(2,128)(2,1)}) fusion(bf16[16,2,240,448]{2,1,0,3:T(2,128)(2,1)} %reshape.174, s32[]{:T(128)S(6)} %select_n.89, s32[]{:T(128)S(6)} %select_n.90), kind=kLoop, calls=%fused_computation.5 | loop fusion | bytes 13762568 | tf_op jit(solution)/shard_map/jit(dynamic_index_in_dim)/dynamic_slice | solution.py:102
  207.7 8.9 %copy.30 = bf16[16,1,240,448]{2,3,1,0:T(8,128)(2,1)} copy(bf16[16,1,240,448]{2,1,0,3:T(2,128)(2,1)} %get-tuple-element.9) | data formatting | bytes 6881280
  216.6 0.5 collective-permute-start.1
  217.1 8.1 %concatenate.30 = bf16[3840,448]{0,1:T(8,128)(2,1)} reshape(bf16[16,240,448]{1,0,2:T(8,128)(2,1)} %get-tuple-element.8) | data formatting | bytes 6881280 | tf_op jit(solution)/shard_map/concatenate | solution.py:106
  225.2 5.9 %copy.23 = bf16[16,240,448]{1,0,2:T(8,128)(2,1)} copy(bf16[16,240,448]{1,2,0:T(8,128)(2,1)} %collective-permute-done) | data formatting | bytes 6881280 | tf_op jit(solution)/shard_map/ppermute | solution.py:104
  231.1 8.1 %concatenate.31 = bf16[3840,448]{0,1:T(8,128)(2,1)} reshape(bf16[16,240,448]{1,0,2:T(8,128)(2,1)} %copy.23) | data formatting | bytes 6881280 | tf_op jit(solution)/shard_map/concatenate | solution.py:106
  239.2 21.7 %multiply_convert_fusion = bf16[3840,1920]{1,0:T(8,128)(2,1)} fusion(bf16[3840,448]{0,1:T(8,128)(2,1)} %concatenate.31, bf16[3840,448]{0,1:T(8,128)(2,1)} %concatenate.30, bf16[448,1920]{1,0:T(8,128)(2,1)} %collective-permute-done.1, bf16[64,1920]{1,0:T(8,128)(2,1)} %copy-done.4, bf16[384,1920]{1,0:T(8,128)(2,1)} %copy-done), kind=kOutput, calls=%fused_computation.4 | convolution fusion | flops 13250887680 | bytes 25067520 | tf_op jit(solution)/shard_map/dot_general | solution.py:110
  260.9 0.7 select_n.93
  261.6 14.8 %all_to_all.16 = bf16[32,1,12]{2,1,0:T(2,128)(2,1)S(1)} all-to-all(bf16[32,1,12]{2,1,0:T(2,128)(2,1)} %select_n.93), channel_id=1, replica_groups=mesh['tmc'=16,'core'=2,'panel'=4] {'tmc','core'}, dimensions={0} | all-to-all | bytes 1536 | tf_op jit(solution)/shard_map/all_to_all | solution.py:80
  276.4 0.7 reduce.12
  277.1 0.8 reshape.211
  277.9 1.5 convolution_bitcast_fusion
  279.3 0.2 convolution_bitcast_fusion.1
  279.5 0.4 convolution_reduce_fusion
  280.0 1.7 fusion.10
  281.6 67.2 %psum.7 = f32[1920]{0:T(1024)} all-reduce(f32[1920]{0:T(1024)S(1)} %subtract_multiply_fusion), channel_id=1, replica_groups=mesh['tmc'=16,'core'=2,'panel'=4] {'tmc','core'}, use_global_device_ids=true, to_apply=%region_9.10 | all-reduce | flops 1920 | bytes 15360 | tf_op jit(solution)/shard_map/psum | solution.py:95
  348.8 19.4 %reduce-scatter.4.cloned.1.call-done = bf16[240,1920]{1,0:T(8,128)(2,1)} async-done(((bf16[3840,1920]{1,0:T(8,128)(2,1)}), bf16[240,1920]{1,0:T(8,128)(2,1)}) %reduce-scatter.4.cloned.1.call-update) | async-done | bytes 921616
  368.3 2.5 convert_element_type.57
  (41 shorter events, 0.7 us)
Async XLA Ops:
  7.2 21.6 %copy-start.3 = (bf16[256,1920]{1,0:T(8,128)(2,1)S(1)}, bf16[256,1920]{1,0:T(8,128)(2,1)}, u32[]{:S(2)}) copy-start(bf16[256,1920]{1,0:T(8,128)(2,1)} %param.6) | copy-start | bytes 2949124
  10.9 2.9 copy-start.1
  19.9 15.7 %all-to-all-start.1 = ((bf16[32,2,384]{2,1,0:T(2,128)(2,1)}), bf16[32,2,384]{2,1,0:T(2,128)(2,1)S(1)}, u32[]{:S(2)}, u32[]{:S(2)}) async-start(bf16[32,2,384]{2,1,0:T(2,128)(2,1)} %reshape.243), calls=%async_computation.1 | async-start | bytes 98304 | tf_op jit(solution)/shard_map/all_to_all | solution.py:79
  31.9 1.7 copy-start.2
  31.9 9.4 %copy-start.7 = (f32[32]{0:T(128)S(1)}, f32[32]{0:T(128)}, u32[]{:S(2)}) copy-start(f32[32]{0:T(128)} %param.11) | copy-start | bytes 388
  31.9 10.7 %copy-start.8 = (f32[32]{0:T(128)S(1)}, f32[32]{0:T(128)}, u32[]{:S(2)}) copy-start(f32[32]{0:T(128)} %param.10) | copy-start | bytes 388
  35.6 33.0 %all-to-all-start = ((bf16[32,12,1920]{2,1,0:T(8,128)(2,1)}), bf16[32,12,1920]{2,1,0:T(8,128)(2,1)S(1)}, u32[]{:S(2)}, u32[]{:S(2)}) async-start(bf16[32,12,1920]{2,1,0:T(8,128)(2,1)} %broadcast_select_fusion), calls=%async_computation | async-start | bytes 3932160 | tf_op jit(solution)/shard_map/all_to_all | solution.py:78
  41.0 102.4 %all-gather.2.cloned.1.call-start = ((), (), s32[]{:S(2)}) async-start(), calls=%async_computation.4 | async-start | bytes 8601600 | tf_op jit(solution)/shard_map/all_gather | solution.py:98
  44.6 25.2 %copy-start.5 = (s32[384]{0:T(512)}, s32[384]{0:T(512)S(1)}, u32[]{:S(2)}) copy-start(s32[384]{0:T(512)S(1)} %add.124) | copy-start | bytes 4612
  44.8 25.0 %copy-start.6 = (pred[384]{0:T(512)(128)(4,1)}, pred[384]{0:T(512)(128)(4,1)S(1)}, u32[]{:S(2)}) copy-start(pred[384]{0:T(512)(128)(4,1)S(1)} %lt.79) | copy-start | bytes 1156
  72.5 4.4 %copy-start = (bf16[384,1920]{1,0:T(8,128)(2,1)}, bf16[384,1920]{1,0:T(8,128)(2,1)S(1)}, u32[]{:S(2)}) copy-start(bf16[384,1920]{1,0:T(8,128)(2,1)S(1)} %get-tuple-element.13) | copy-start | bytes 4423684
  74.2 0.7 copy-start.4
  76.9 291.4 %reduce-scatter.4.cloned.1.call-start = ((), (), s32[]{:S(2)}) async-start(), calls=%async_computation.5 | async-start | bytes 15667200
  216.6 8.6 %collective-permute-start = (bf16[16,240,448]{1,2,0:T(8,128)(2,1)}, bf16[16,240,448]{1,2,0:T(8,128)(2,1)}, u32[]{:S(2)}, u32[]{:S(2)}) collective-permute-start(bf16[16,240,448]{1,2,0:T(8,128)(2,1)} %bitcast.71), channel_id=1, source_target_pairs={{0,4},{4,0},{1,5},{5,1},{2,6},{6,2},{3,7},{7,3},{8,12},{12,8},{9,1... | collective-permute-start | bytes 10321928 | tf_op jit(solution)/shard_map/ppermute | solution.py:104
  216.6 22.5 %collective-permute-start.1 = (bf16[448,1920]{1,0:T(8,128)(2,1)}, bf16[448,1920]{1,0:T(8,128)(2,1)}, u32[]{:S(2)}, u32[]{:S(2)}) collective-permute-start(bf16[448,1920]{1,0:T(8,128)(2,1)} %get-tuple-element.10), channel_id=1, source_target_pairs={{0,4},{4,0},{1,5},{5,1},{2,6},{6,2},{3,7},{7,3},{8,12},{12,8},{9,1... | collective-permute-start | bytes 5160968 | tf_op jit(solution)/shard_map/ppermute | solution.py:105
Sparse Core Ops, SparseCore 0:
  77.0 66.3 all-gather.1
  261.0 107.1 reduce-scatter.3

commit v5 on v4

--- a/solution.py
+++ b/solution.py
@@ -94,23 +94,33 @@
     design_bf, terms_bf, right_part = eliminate(whitener, got_design, got_params, got_obs, scale)
     right_hand = lax.psum(right_part, TM)
     own_rows = jnp.concatenate([design_bf, terms_bf], axis=0)
-    signed_rows = jnp.concatenate([design_bf, -terms_bf], axis=0).T
-    gathered = lax.all_gather(signed_rows, "panel", axis=0, tiled=True)
-    block_rows = gathered.shape[0] // tile_count
-    by_core = gathered.reshape(chip_count, core_count, block_rows, gathered.shape[1])
+    signed_rows = jnp.concatenate([design_bf, -terms_bf], axis=0)
+    gathered = lax.all_gather(signed_rows, "panel", axis=1, tiled=True)
+    gathered, right_hand = lax.optimization_barrier((gathered, right_hand))
     swap = [(0, 1), (1, 0)]
-    kept_rows = lax.dynamic_index_in_dim(by_core, core_index, 1, keepdims=False)
-    given_rows = lax.dynamic_index_in_dim(by_core, 1 - core_index, 1, keepdims=False)
-    got_rows = lax.ppermute(given_rows, "core", swap)
+    half = panel_width // core_count
+    got_rows = lax.ppermute(gathered, "core", swap)
     got_cols = lax.ppermute(own_rows, "core", swap)
-    row_side = jnp.concatenate([kept_rows, got_rows], axis=2).reshape(
-        chip_count * block_rows, -1
+    row_side = jnp.concatenate([gathered, got_rows], axis=0)
+    col_side = lax.dynamic_slice_in_dim(
+        jnp.concatenate([own_rows, got_cols], axis=0), core_index * half, half, 1
     )
-    col_side = jnp.concatenate([own_rows, got_cols], axis=0)
-    product = jnp.dot(row_side, col_side, preferred_element_type=jnp.float32)
-    normal = lax.psum_scatter(
+    product = lax.dot_general(
+        row_side, col_side, (((0,), (0,)), ((), ())), preferred_element_type=jnp.float32
+    )
+    pair = lax.psum_scatter(
         (product * scale).astype(jnp.bfloat16), "tmc", scatter_dimension=0, tiled=True
     ).astype(jnp.float32)
+    block_rows = pair.shape[0] // core_count
+    by_core = pair.reshape(core_count, block_rows, half)
+    mine = lax.dynamic_index_in_dim(by_core, core_index, 0, keepdims=False)
+    given = lax.dynamic_index_in_dim(by_core, 1 - core_index, 0, keepdims=False)
+    got = lax.ppermute(given, "core", swap)
+    normal = jnp.where(
+        core_index == 0,
+        jnp.concatenate([mine, got], axis=1),
+        jnp.concatenate([got, mine], axis=1),
+    )
     return (normal, right_hand)
 
 

time: 379 us -> 311 us (0.82)
  local copies, waits for them, and re-layouts: 112 us -> 15.5 us
  waiting for transfers between devices: 97.7 us -> 130 us
  blocking collectives: 82 us -> 76.6 us
    reduce_scatter x0 -> x1, waiting for transfers between devices: none -> 102 us  [body(): lax.psum_scatter((product * scale).astype(jnp.bfloat16), 'tmc', scatter_d...]
    all_gather x1, waiting for transfers between devices: 66.2 us -> 0.01 us  [body(): gathered = lax.all_gather(signed_rows, 'panel', axis=1, tiled=True)]
    dynamic_slice x1 -> x0, local copies, waits for them, and re-layouts: 35 us -> none  [body(): kept_rows = lax.dynamic_index_in_dim(by_core, core_index, 1, keepdims=False)]
    reshape x1 -> x0, local copies, waits for them, and re-layouts: 29.2 us -> none  [body(): gathered.reshape(chip_count, core_count, block_rows, gathered.shape[1])]
    unnamed x3 -> x2, waiting for transfers between devices: 19.5 us -> 0.03 us
    concatenate x2 -> x0, local copies, waits for them, and re-layouts: 16.1 us -> none  [body(): jnp.concatenate([kept_rows, got_rows], axis=2)]
    ppermute x1, waiting for transfers between devices: 0.01 us -> 10.5 us  [body(): got_cols = lax.ppermute(own_rows, 'core', swap)]
    unnamed x23 -> x24, local copies, waits for them, and re-layouts: 12 us -> 1.56 us
  transfers between devices with their start and end apart: 6 -> 7, of which waited for: 4 -> 6; matrix products, arithmetic and copies ran while one was open for 13% -> 9% of each run, Pallas kernels for 0% -> 0%
where the time goes in v5:
time: 311 us; the launch traced here: 309 us
  waiting for transfers between devices  130 us (42%)
  blocking collectives  76.6 us (25%)
  matrix products  32.1 us (10%)
  other arithmetic  24.4 us (8%)
  between operations  16.4 us (5%)
  local copies, waits for them, and re-layouts  15.5 us (5%)
  starting transfers between devices  14.5 us (5%)
    reduce_scatter x1, waiting for transfers between devices, body(): lax.psum_scatter((product * scale).astype(jnp.bfloat16), 'tmc', scatter_d...  102 us
    psum x1, blocking collectives, body(): right_hand = lax.psum(right_part, TM)  65.5 us
    dot_general x1, matrix products, body(): lax.dot_general(row_side, col_side, (((0,), (0,)), ((), ())), preferred_e...  22.7 us
    all_to_all x1, blocking collectives, body(): lax.all_to_all(send_obs, TM, split_axis=0, concat_axis=0, tiled=True)  11.1 us
    ppermute x1, waiting for transfers between devices, body(): got_cols = lax.ppermute(own_rows, 'core', swap)  10.5 us
    all_to_all x1, waiting for transfers between devices, body(): lax.all_to_all(send_design, TM, split_axis=0, concat_axis=0, tiled=True)  10.1 us
    all_to_all x1, starting transfers between devices, body(): lax.all_to_all(send_params, TM, split_axis=0, concat_axis=0, tiled=True)  8.16 us
    gather x5, local copies, waits for them, and re-layouts, pick_rows(): return jnp.take(padded, source_row, axis=0)  7.16 us
  transfers between devices with their start and end apart: 7, of which 6 were waited for; matrix products, arithmetic and copies ran while one was open for 9% of the time, Pallas kernels for 0%

profile of v5, /device:TPU:24, one launch (start us, length us, event | category | flops | bytes accessed | tf_op | source)
XLA Modules:
  0.0 309.4 jit_solution(12412613966868585761)
XLA Ops:
  7.2 0.5 broadcast.193
  7.7 2.1 fusion.36
  9.9 0.1 reshape_squeeze.3
  10.0 0.2 dynamic-slice_reduce_fusion
  10.2 0.6 reduce-window.6
  10.8 0.2 slice_reduce_fusion
  11.0 0.1 fusion.39
  11.1 0.1 copy.15
  11.2 0.2 fusion.34
  11.4 1.4 scatter_custom_fusion
  12.9 0.7 pad_maximum_fusion.2
  13.6 2.8 gather_fusion.2
  16.4 0.1 broadcast_in_dim.54
  16.6 0.1 copy.16
  16.7 1.4 gather_fusion.1
  18.2 0.1 broadcast_select_fusion.1
  18.3 0.8 reshape.242
  19.1 8.2 %all-to-all-start.1 = ((bf16[32,2,384]{2,1,0:T(2,128)(2,1)}), bf16[32,2,384]{2,1,0:T(2,128)(2,1)S(1)}, u32[]{:S(2)}, u32[]{:S(2)}) async-start(bf16[32,2,384]{2,1,0:T(2,128)(2,1)} %reshape.242), calls=%async_computation.1 | async-start | bytes 98304 | tf_op jit(solution)/shard_map/all_to_all | solution.py:79
  27.3 0.2 concatenate.28
  27.5 2.5 gather_fusion
  30.0 0.4 gather.17
  30.4 1.6 broadcast_select_fusion
  32.0 0.7 and_select_fusion
  32.8 1.9 all-to-all-done.1
  34.7 5.5 %all-to-all-start = ((bf16[32,12,1920]{2,1,0:T(8,128)(2,1)}), bf16[32,12,1920]{2,1,0:T(8,128)(2,1)S(1)}, u32[]{:S(2)}, u32[]{:S(2)}) async-start(bf16[32,12,1920]{2,1,0:T(8,128)(2,1)} %broadcast_select_fusion), calls=%async_computation | async-start | bytes 3932160 | tf_op jit(solution)/shard_map/all_to_all | solution.py:78
  40.2 0.2 all-gather.2.cloned.1.call-start
  40.4 0.1 iota_compare_fusion.5
  40.5 0.6 dynamic_slice.20
  41.1 0.6 dynamic_slice.19
  43.7 0.1 lt.82
  43.8 0.1 add.127
  43.9 0.1 reshape.243
  44.1 0.7 fusion.30
  44.8 0.2 fusion.73
  45.1 0.1 copy.17
  45.2 5.8 %cholesky.17 = f32[64,64]{1,0:T(8,128)S(1)} custom-call(f32[64,64]{1,0:T(8,128)S(1)} %fusion.43), custom_call_target="Cholesky" | custom-call | tf_op jit(solution)/shard_map/jit(cholesky)/cholesky | solution.py:32
  51.1 0.6 compare_reduce_fusion
  51.7 0.7 fusion.35
  52.4 4.9 %custom-call.6 = f32[1,64,64]{1,2,0:T(8,128)S(1)} custom-call(f32[1,64,64]{2,1,0:T(8,128)S(1)} %fusion.35), custom_call_target="InvertDiagBlocksLowerTriangular" | custom-call | tf_op jit(solution)/shard_map/triangular_solve | solution.py:33
  57.3 0.3 fusion.40
  57.6 10.1 %all-to-all-done = bf16[32,12,1920]{2,1,0:T(8,128)(2,1)S(1)} async-done(((bf16[32,12,1920]{2,1,0:T(8,128)(2,1)}), bf16[32,12,1920]{2,1,0:T(8,128)(2,1)S(1)}, u32[]{:S(2)}, u32[]{:S(2)}) %all-to-all-start) | async-done | bytes 1474592 | tf_op jit(solution)/shard_map/all_to_all | solution.py:78
  67.7 1.3 reshape.171
  69.0 2.7 fusion.72
  71.7 1.7 fusion.71
  73.4 2.0 pad_maximum_fusion.1
  75.5 0.7 select_n.107
  76.2 11.1 %all_to_all.16 = bf16[32,1,12]{2,1,0:T(2,128)(2,1)S(1)} all-to-all(bf16[32,1,12]{2,1,0:T(2,128)(2,1)} %select_n.107), channel_id=1, replica_groups=mesh['tmc'=16,'core'=2,'panel'=4] {'tmc','core'}, dimensions={0} | all-to-all | bytes 1536 | tf_op jit(solution)/shard_map/all_to_all | solution.py:80
  87.3 0.7 reduce.12
  88.0 0.8 reshape.213
  88.8 1.4 convolution_bitcast_fusion
  90.2 0.2 convolution_bitcast_fusion.1
  90.4 0.4 convolution_reduce_fusion
  90.9 1.7 fusion.8
  92.5 65.5 %psum.7 = f32[1920]{0:T(1024)} all-reduce(f32[1920]{0:T(1024)S(1)} %subtract_multiply_fusion), channel_id=1, replica_groups=mesh['tmc'=16,'core'=2,'panel'=4] {'tmc','core'}, use_global_device_ids=true, to_apply=%region_8.9 | all-reduce | flops 1920 | bytes 15360 | tf_op jit(solution)/shard_map/psum | solution.py:95
  158.0 0.5 collective-permute-start.1
  158.5 10.5 %collective-permute-done.1 = bf16[448,1920]{1,0:T(8,128)(2,1)S(1)} collective-permute-done((bf16[448,1920]{1,0:T(8,128)(2,1)}, bf16[448,1920]{1,0:T(8,128)(2,1)S(1)}, u32[]{:S(2)}, u32[]{:S(2)}) %collective-permute-start.1) | collective-permute-done | bytes 1720352 | tf_op jit(solution)/shard_map/ppermute | solution.py:103
  169.0 2.8 collective-permute-done
  171.8 22.7 %multiply_convert_fusion = bf16[7680,960]{1,0:T(8,128)(2,1)} fusion(bf16[448,7680]{1,0:T(8,128)(2,1)} %collective-permute-done, bf16[448,7680]{1,0:T(8,128)(2,1)} %all-gather.2.cloned.1.call-done, s32[]{:T(128)S(6)} %select_n.103, bf16[384,1920]{1,0:T(8,128)(2,1)} %copy-done, bf16[64,1920]{1,0:T(8,128)(2,1)} %copy-done.4, ...), kind=kOutput, calls=%fused_computation.4 | convolution fusion | flops 13259489280 | bytes 31948804 | tf_op jit(solution)/shard_map/dot_general | solution.py:108
  194.5 102.0 %reduce-scatter.2.cloned.1.call-done = bf16[480,960]{1,0:T(8,128)(2,1)} async-done(((bf16[7680,960]{1,0:T(8,128)(2,1)}), bf16[480,960]{1,0:T(8,128)(2,1)}) %reduce-scatter.2.cloned.1.call-update) | async-done | bytes 921616 | tf_op jit(solution)/shard_map/reduce_scatter | solution.py:111
  296.5 1.4 convert.1
  297.9 0.1 dynamic-slice_bitcast_fusion.1
  298.1 0.1 collective-permute-start.2
  298.1 2.5 collective-permute-done.2
  300.7 1.8 maximum_select_fusion
  (41 shorter events, 0.5 us)
Async XLA Ops:
  7.2 9.4 %copy-start.5 = (bf16[256,64]{0,1:T(8,128)(2,1)S(1)}, bf16[256,64]{0,1:T(8,128)(2,1)}, u32[]{:S(2)}) copy-start(bf16[256,64]{0,1:T(8,128)(2,1)} %param.7) | copy-start | bytes 98308
  7.2 20.1 %copy-start.3 = (bf16[256,1920]{1,0:T(8,128)(2,1)S(1)}, bf16[256,1920]{1,0:T(8,128)(2,1)}, u32[]{:S(2)}) copy-start(bf16[256,1920]{1,0:T(8,128)(2,1)} %param.6) | copy-start | bytes 2949124
  9.9 2.9 copy-start.1
  19.1 15.6 %all-to-all-start.1 = ((bf16[32,2,384]{2,1,0:T(2,128)(2,1)}), bf16[32,2,384]{2,1,0:T(2,128)(2,1)S(1)}, u32[]{:S(2)}, u32[]{:S(2)}) async-start(bf16[32,2,384]{2,1,0:T(2,128)(2,1)} %reshape.242), calls=%async_computation.1 | async-start | bytes 98304 | tf_op jit(solution)/shard_map/all_to_all | solution.py:79
  30.4 2.3 copy-start.2
  32.8 7.7 %copy-start.8 = (f32[32]{0:T(128)S(1)}, f32[32]{0:T(128)}, u32[]{:S(2)}) copy-start(f32[32]{0:T(128)} %param.11) | copy-start | bytes 388
  32.8 8.3 %copy-start.9 = (f32[32]{0:T(128)S(1)}, f32[32]{0:T(128)}, u32[]{:S(2)}) copy-start(f32[32]{0:T(128)} %param.10) | copy-start | bytes 388
  34.7 33.0 %all-to-all-start = ((bf16[32,12,1920]{2,1,0:T(8,128)(2,1)}), bf16[32,12,1920]{2,1,0:T(8,128)(2,1)S(1)}, u32[]{:S(2)}, u32[]{:S(2)}) async-start(bf16[32,12,1920]{2,1,0:T(8,128)(2,1)} %broadcast_select_fusion), calls=%async_computation | async-start | bytes 3932160 | tf_op jit(solution)/shard_map/all_to_all | solution.py:78
  40.2 117.8 %all-gather.2.cloned.1.call-start = ((), (), s32[]{:S(2)}) async-start(), calls=%async_computation.4 | async-start | bytes 8601600 | tf_op jit(solution)/shard_map/all_gather | solution.py:98
  43.8 25.2 %copy-start.7 = (pred[384]{0:T(512)(128)(4,1)}, pred[384]{0:T(512)(128)(4,1)S(1)}, u32[]{:S(2)}) copy-start(pred[384]{0:T(512)(128)(4,1)S(1)} %lt.82) | copy-start | bytes 1156
  43.9 25.1 %copy-start.6 = (s32[384]{0:T(512)}, s32[384]{0:T(512)S(1)}, u32[]{:S(2)}) copy-start(s32[384]{0:T(512)S(1)} %add.127) | copy-start | bytes 4612
  71.7 1.7 copy-start
  73.4 2.0 copy-start.4
  75.4 221.0 %reduce-scatter.2.cloned.1.call-start = ((), (), s32[]{:S(2)}) async-start(), calls=%async_computation.5 | async-start | bytes 16711680 | tf_op jit(solution)/shard_map/reduce_scatter | solution.py:111
  158.0 13.8 %collective-permute-start = (bf16[448,7680]{1,0:T(8,128)(2,1)}, bf16[448,7680]{1,0:T(8,128)(2,1)}, u32[]{:S(2)}, u32[]{:S(2)}) collective-permute-start(bf16[448,7680]{1,0:T(8,128)(2,1)} %all-gather.2.cloned.1.call-done), channel_id=1, source_target_pairs={{0,4},{4,0},{1,5},{5,1},{2,6},{6,2},{3,7},{7,3},{8,12},{12,8},{9,1... | collective-permute-start | bytes 20643848 | tf_op jit(solution)/shard_map/ppermute | solution.py:102
  158.0 11.0 %collective-permute-start.1 = (bf16[448,1920]{1,0:T(8,128)(2,1)}, bf16[448,1920]{1,0:T(8,128)(2,1)S(1)}, u32[]{:S(2)}, u32[]{:S(2)}) collective-permute-start(bf16[448,1920]{1,0:T(8,128)(2,1)} %get-tuple-element.14), channel_id=1, source_target_pairs={{0,4},{4,0},{1,5},{5,1},{2,6},{6,2},{3,7},{7,3},{8,12},{12,8},{9,1... | collective-permute-start | bytes 5160968 | tf_op jit(solution)/shard_map/ppermute | solution.py:103
  298.1 2.6 collective-permute-start.2
Sparse Core Ops, SparseCore 0:
  75.6 66.3 all-gather.1
  194.6 101.8 reduce-scatter.1

commit v6 on v5

--- a/solution.py
+++ b/solution.py
@@ -72,16 +72,16 @@
         return jnp.take(padded, source_row, axis=0)
 
     send_design = pick_rows(design).reshape(tile_count, capacity, panel_width)
-    send_params = pick_rows(partials).reshape(tile_count, capacity, param_count)
-    send_obs = pick_rows(observed).reshape(tile_count, capacity)
-    got_design, got_params, got_obs = (
+    with_obs = jnp.concatenate([partials, observed[:, None]], axis=1)
+    send_params = pick_rows(with_obs).reshape(tile_count, capacity, param_count + 1)
+    got_design, got_params = (
         lax.all_to_all(send_design, TM, split_axis=0, concat_axis=0, tiled=True),
         lax.all_to_all(send_params, TM, split_axis=0, concat_axis=0, tiled=True),
-        lax.all_to_all(send_obs, TM, split_axis=0, concat_axis=0, tiled=True),
     )
     got_design = got_design.reshape(slot_count, panel_width)
-    got_params = got_params.reshape(slot_count, param_count)
-    got_obs = got_obs.reshape(slot_count)
+    got_params = got_params.reshape(slot_count, param_count + 1)
+    got_obs = got_params[:, param_count]
+    got_params = got_params[:, :param_count]
     per_source = jnp.sum((epoch_table == device_index).astype(jnp.int32), axis=0)
     arc_start = jnp.sum((arc_ids < device_index).astype(jnp.int32))
     first_pos = jnp.mod(jnp.arange(tile_count, dtype=jnp.int32) - arc_start, tile_count)
@@ -92,12 +92,12 @@
         order_pos, order_pos, usable, usable, autoreg[device_index], movavg[device_index]
     )
     design_bf, terms_bf, right_part = eliminate(whitener, got_design, got_params, got_obs, scale)
-    right_hand = lax.psum(right_part, TM)
+    swap = [(0, 1), (1, 0)]
+    right_hand = lax.psum(right_part + lax.ppermute(right_part, "core", swap), "tmc")
     own_rows = jnp.concatenate([design_bf, terms_bf], axis=0)
     signed_rows = jnp.concatenate([design_bf, -terms_bf], axis=0)
     gathered = lax.all_gather(signed_rows, "panel", axis=1, tiled=True)
     gathered, right_hand = lax.optimization_barrier((gathered, right_hand))
-    swap = [(0, 1), (1, 0)]
     half = panel_width // core_count
     got_rows = lax.ppermute(gathered, "core", swap)
     got_cols = lax.ppermute(own_rows, "core", swap)

time: 311 us -> 299 us (0.961)
  blocking collectives: 76.6 us -> 38 us
  waiting for transfers between devices: 130 us -> 160 us
    psum x1, blocking collectives: 65.5 us -> 38 us  [body(): lax.psum(right_part + lax.ppermute(right_part, 'core', swap), 'tmc')]
    all_gather x1, waiting for transfers between devices: 0.01 us -> 23.1 us  [body(): gathered = lax.all_gather(signed_rows, 'panel', axis=1, tiled=True)]
    all_to_all x1 -> x0, blocking collectives: 11.1 us -> none  [body(): lax.all_to_all(send_obs, TM, split_axis=0, concat_axis=0, tiled=True)]
    reduce_scatter x1, waiting for transfers between devices: 102 us -> 108 us  [body(): lax.psum_scatter((product * scale).astype(jnp.bfloat16), 'tmc', scatter_d...]
    gather x5 -> x4, local copies, waits for them, and re-layouts: 7.16 us -> 4.36 us  [pick_rows(): return jnp.take(padded, source_row, axis=0)]
  transfers between devices with their start and end apart: 7 -> 8, of which waited for: 6 -> 8; matrix products, arithmetic and copies ran while one was open for 9% -> 8% of each run, Pallas kernels for 0% -> 0%
where the time goes in v6:
time: 299 us; the launch traced here: 297 us
  waiting for transfers between devices  160 us (54%)
  blocking collectives  38 us (13%)
  matrix products  31.3 us (10%)
  other arithmetic  23.1 us (8%)
  between operations  16.4 us (5%)
  starting transfers between devices  14.5 us (5%)
  local copies, waits for them, and re-layouts  13.8 us (5%)
    reduce_scatter x1, waiting for transfers between devices, body(): lax.psum_scatter((product * scale).astype(jnp.bfloat16), 'tmc', scatter_d...  108 us
    psum x1, blocking collectives, body(): lax.psum(right_part + lax.ppermute(right_part, 'core', swap), 'tmc')  38 us
    all_gather x1, waiting for transfers between devices, body(): gathered = lax.all_gather(signed_rows, 'panel', axis=1, tiled=True)  23.1 us
    dot_general x1, matrix products, body(): lax.dot_general(row_side, col_side, (((0,), (0,)), ((), ())), preferred_e...  22.7 us
    ppermute x1, waiting for transfers between devices, body(): got_cols = lax.ppermute(own_rows, 'core', swap)  10.5 us
    all_to_all x1, waiting for transfers between devices, body(): lax.all_to_all(send_design, TM, split_axis=0, concat_axis=0, tiled=True)  10.1 us
    all_to_all x1, starting transfers between devices, body(): lax.all_to_all(send_params, TM, split_axis=0, concat_axis=0, tiled=True)  8.16 us
    another operation x3, other arithmetic, eliminate(): factor = jnp.linalg.cholesky(param_gram)  6.51 us
  transfers between devices with their start and end apart: 8, of which 8 were waited for; matrix products, arithmetic and copies ran while one was open for 8% of the time, Pallas kernels for 0%

profile of v6, /device:TPU:24, one launch (start us, length us, event | category | flops | bytes accessed | tf_op | source)
XLA Modules:
  0.0 297.4 jit_solution(12270109158446470053)
XLA Ops:
  7.2 0.5 broadcast.187
  7.7 2.1 fusion.75
  9.8 0.1 reshape_squeeze.3
  9.9 0.2 dynamic-slice_reduce_fusion
  10.1 0.6 reduce-window.6
  10.7 0.2 slice_reduce_fusion.1
  11.0 0.1 fusion.43
  11.1 0.1 copy.11
  11.2 0.2 fusion.36
  11.4 1.4 scatter_custom_fusion
  12.9 0.1 broadcast_in_dim.51
  13.0 0.8 broadcast_in_dim.58
  13.7 0.9 copy.12
  14.6 0.1 fusion.38
  14.7 1.4 gather_fusion.1
  16.2 0.1 broadcast_select_fusion.1
  16.4 0.8 reshape.203
  17.2 8.2 %all-to-all-start.1 = ((bf16[32,2,390]{2,1,0:T(2,128)(2,1)}), bf16[32,2,390]{2,1,0:T(2,128)(2,1)S(1)}, u32[]{:S(2)}, u32[]{:S(2)}) async-start(bf16[32,2,390]{2,1,0:T(2,128)(2,1)} %reshape.203), calls=%async_computation.1 | async-start | bytes 131072 | tf_op jit(solution)/shard_map/all_to_all | solution.py:79
  25.4 0.2 concatenate.28
  25.6 2.5 gather_fusion
  28.1 0.4 gather.13
  28.5 1.6 broadcast_select_fusion
  30.1 0.7 and_select_fusion
  30.9 2.0 all-to-all-done.1
  32.9 5.4 %all-to-all-start = ((bf16[32,12,1920]{2,1,0:T(8,128)(2,1)}), bf16[32,12,1920]{2,1,0:T(8,128)(2,1)S(1)}, u32[]{:S(2)}, u32[]{:S(2)}) async-start(bf16[32,12,1920]{2,1,0:T(8,128)(2,1)} %broadcast_select_fusion), calls=%async_computation | async-start | bytes 3932160 | tf_op jit(solution)/shard_map/all_to_all | solution.py:78
  38.3 0.2 all-gather.2.cloned.1.call-start
  38.5 0.1 iota_compare_fusion.6
  38.6 0.6 dynamic_slice.20
  39.2 0.6 dynamic_slice.19
  41.7 0.1 lt.78
  41.9 0.1 add.126
  42.0 0.2 reshape.204
  42.2 0.7 fusion.30
  42.9 0.2 fusion.78
  43.2 0.1 copy.14
  43.3 5.8 %cholesky.17 = f32[64,64]{1,0:T(8,128)S(1)} custom-call(f32[64,64]{1,0:T(8,128)S(1)} %fusion.47), custom_call_target="Cholesky" | custom-call | tf_op jit(solution)/shard_map/jit(cholesky)/cholesky | solution.py:32
  49.2 0.6 compare_reduce_fusion
  49.8 0.7 fusion.39
  50.5 4.9 %custom-call.6 = f32[1,64,64]{1,2,0:T(8,128)S(1)} custom-call(f32[1,64,64]{2,1,0:T(8,128)S(1)} %fusion.39), custom_call_target="InvertDiagBlocksLowerTriangular" | custom-call | tf_op jit(solution)/shard_map/triangular_solve | solution.py:33
  55.4 0.3 fusion.44
  55.7 10.1 %all-to-all-done = bf16[32,12,1920]{2,1,0:T(8,128)(2,1)S(1)} async-done(((bf16[32,12,1920]{2,1,0:T(8,128)(2,1)}), bf16[32,12,1920]{2,1,0:T(8,128)(2,1)S(1)}, u32[]{:S(2)}, u32[]{:S(2)}) %all-to-all-start) | async-done | bytes 1474592 | tf_op jit(solution)/shard_map/all_to_all | solution.py:78
  65.8 1.3 reshape.142
  67.0 2.7 fusion.77
  69.8 1.7 fusion.76
  71.4 2.0 pad_maximum_fusion.1
  73.5 1.1 slice_reduce_fusion
  74.6 0.7 convolution_bitcast_fusion
  75.3 0.2 convolution_bitcast_fusion.1
  75.5 0.4 convolution_reduce_fusion
  76.0 1.7 fusion.8
  77.6 0.1 collective-permute-start
  77.7 1.2 collective-permute-done
  78.9 38.0 %psum.7 = f32[1920]{0:T(1024)} all-reduce(f32[1920]{0:T(1024)S(1)} %add.140), channel_id=1, replica_groups=mesh['tmc'=16,'core'=2,'panel'=4] {'tmc'}, use_global_device_ids=true, to_apply=%region_8.9 | all-reduce | flops 1920 | bytes 15360 | tf_op jit(solution)/shard_map/psum | solution.py:96
  116.9 23.1 %all-gather.2.cloned.1.call-done = bf16[448,7680]{1,0:T(8,128)(2,1)} async-done(((bf16[448,1920]{1,0:T(8,128)(2,1)}), bf16[448,7680]{1,0:T(8,128)(2,1)}) %all-gather.2.cloned.1.call-update) | async-done | bytes 6881296 | tf_op jit(solution)/shard_map/all_gather | solution.py:99
  140.0 0.5 collective-permute-start.2
  140.5 10.5 %collective-permute-done.2 = bf16[448,1920]{1,0:T(8,128)(2,1)S(1)} collective-permute-done((bf16[448,1920]{1,0:T(8,128)(2,1)}, bf16[448,1920]{1,0:T(8,128)(2,1)S(1)}, u32[]{:S(2)}, u32[]{:S(2)}) %collective-permute-start.2) | collective-permute-done | bytes 1720352 | tf_op jit(solution)/shard_map/ppermute | solution.py:103
  151.0 2.8 collective-permute-done.1
  153.8 22.7 %multiply_convert_fusion = bf16[7680,960]{1,0:T(8,128)(2,1)} fusion(bf16[448,7680]{1,0:T(8,128)(2,1)} %collective-permute-done.1, bf16[448,7680]{1,0:T(8,128)(2,1)} %all-gather.2.cloned.1.call-done, s32[]{:T(128)S(6)} %select_n.84, bf16[384,1920]{1,0:T(8,128)(2,1)} %copy-done, bf16[64,1920]{1,0:T(8,128)(2,1)} %copy-done.4, ...), kind=kOutput, calls=%fused_computation.3 | convolution fusion | flops 13259489280 | bytes 31948804 | tf_op jit(solution)/shard_map/dot_general | solution.py:108
  176.5 108.0 %reduce-scatter.2.cloned.1.call-done = bf16[480,960]{1,0:T(8,128)(2,1)} async-done(((bf16[7680,960]{1,0:T(8,128)(2,1)}), bf16[480,960]{1,0:T(8,128)(2,1)}) %reduce-scatter.2.cloned.1.call-update) | async-done | bytes 921616 | tf_op jit(solution)/shard_map/reduce_scatter | solution.py:111
  284.5 1.4 convert.1
  285.9 0.1 dynamic-slice_bitcast_fusion.1
  286.1 0.1 collective-permute-start.3
  286.2 2.5 collective-permute-done.3
  288.7 1.8 maximum_select_fusion
  (37 shorter events, 0.5 us)
Async XLA Ops:
  7.2 18.2 %copy-start.3 = (bf16[256,1920]{1,0:T(8,128)(2,1)S(1)}, bf16[256,1920]{1,0:T(8,128)(2,1)}, u32[]{:S(2)}) copy-start(bf16[256,1920]{1,0:T(8,128)(2,1)} %param.6) | copy-start | bytes 2949124
  9.9 3.8 %copy-start.1 = (s32[256,32]{1,0:T(8,128)}, s32[256,32]{1,0:T(8,128)S(1)}, u32[]{:S(2)}) copy-start(s32[256,32]{1,0:T(8,128)S(1)} %reshape_squeeze.3) | copy-start | bytes 98308
  17.2 15.7 %all-to-all-start.1 = ((bf16[32,2,390]{2,1,0:T(2,128)(2,1)}), bf16[32,2,390]{2,1,0:T(2,128)(2,1)S(1)}, u32[]{:S(2)}, u32[]{:S(2)}) async-start(bf16[32,2,390]{2,1,0:T(2,128)(2,1)} %reshape.203), calls=%async_computation.1 | async-start | bytes 131072 | tf_op jit(solution)/shard_map/all_to_all | solution.py:79
  28.5 2.3 copy-start.2
  30.8 7.7 %copy-start.6 = (f32[32]{0:T(128)S(1)}, f32[32]{0:T(128)}, u32[]{:S(2)}) copy-start(f32[32]{0:T(128)} %param.11) | copy-start | bytes 388
  30.9 8.3 %copy-start.7 = (f32[32]{0:T(128)S(1)}, f32[32]{0:T(128)}, u32[]{:S(2)}) copy-start(f32[32]{0:T(128)} %param.10) | copy-start | bytes 388
  32.9 32.9 %all-to-all-start = ((bf16[32,12,1920]{2,1,0:T(8,128)(2,1)}), bf16[32,12,1920]{2,1,0:T(8,128)(2,1)S(1)}, u32[]{:S(2)}, u32[]{:S(2)}) async-start(bf16[32,12,1920]{2,1,0:T(8,128)(2,1)} %broadcast_select_fusion), calls=%async_computation | async-start | bytes 3932160 | tf_op jit(solution)/shard_map/all_to_all | solution.py:78
  38.3 101.7 %all-gather.2.cloned.1.call-start = ((), (), s32[]{:S(2)}) async-start(), calls=%async_computation.3 | async-start | bytes 8601600 | tf_op jit(solution)/shard_map/all_gather | solution.py:99
  42.2 7.0 %copy-start.5 = (bf16[384,65]{1,0:T(8,128)(2,1)}, bf16[384,65]{1,0:T(8,128)(2,1)S(1)}, u32[]{:S(2)}) copy-start(bf16[384,65]{1,0:T(8,128)(2,1)S(1)} %reshape.143) | copy-start | bytes 149764
  69.8 1.7 copy-start
  71.4 2.0 copy-start.4
  73.5 211.0 %reduce-scatter.2.cloned.1.call-start = ((), (), s32[]{:S(2)}) async-start(), calls=%async_computation.4 | async-start | bytes 16711680 | tf_op jit(solution)/shard_map/reduce_scatter | solution.py:111
  77.6 1.3 collective-permute-start
  140.0 13.8 %collective-permute-start.1 = (bf16[448,7680]{1,0:T(8,128)(2,1)}, bf16[448,7680]{1,0:T(8,128)(2,1)}, u32[]{:S(2)}, u32[]{:S(2)}) collective-permute-start(bf16[448,7680]{1,0:T(8,128)(2,1)} %all-gather.2.cloned.1.call-done), channel_id=1, source_target_pairs={{0,4},{4,0},{1,5},{5,1},{2,6},{6,2},{3,7},{7,3},{8,12},{12,8},{9,1... | collective-permute-start | bytes 20643848 | tf_op jit(solution)/shard_map/ppermute | solution.py:102
  140.0 11.0 %collective-permute-start.2 = (bf16[448,1920]{1,0:T(8,128)(2,1)}, bf16[448,1920]{1,0:T(8,128)(2,1)S(1)}, u32[]{:S(2)}, u32[]{:S(2)}) collective-permute-start(bf16[448,1920]{1,0:T(8,128)(2,1)} %get-tuple-element.12), channel_id=1, source_target_pairs={{0,4},{4,0},{1,5},{5,1},{2,6},{6,2},{3,7},{7,3},{8,12},{12,8},{9,1... | collective-permute-start | bytes 5160968 | tf_op jit(solution)/shard_map/ppermute | solution.py:103
  286.1 2.6 collective-permute-start.3
Sparse Core Ops, SparseCore 0:
  73.6 66.3 all-gather.1
  176.6 107.8 reduce-scatter.1

commit v7 on v6

--- a/solution.py
+++ b/solution.py
@@ -88,14 +88,21 @@
     offset_in = jnp.arange(capacity, dtype=jnp.int32)
     order_pos = (first_pos[:, None] + offset_in[None, :] * tile_count).reshape(slot_count)
     usable = (offset_in[None, :] < per_source[:, None]).reshape(slot_count)
+    position = jnp.arange(slot_count, dtype=jnp.int32)
+    arc_length = jnp.sum(per_source)
     whitener = whiten_matrix(
-        order_pos, order_pos, usable, usable, autoreg[device_index], movavg[device_index]
+        position, order_pos, position < arc_length, usable,
+        autoreg[device_index], movavg[device_index],
     )
     design_bf, terms_bf, right_part = eliminate(whitener, got_design, got_params, got_obs, scale)
     swap = [(0, 1), (1, 0)]
     right_hand = lax.psum(right_part + lax.ppermute(right_part, "core", swap), "tmc")
-    own_rows = jnp.concatenate([design_bf, terms_bf], axis=0)
-    signed_rows = jnp.concatenate([design_bf, -terms_bf], axis=0)
+    short_most = 5 * rows_dev // 8
+    keep = (slot_count + short_most) // 2
+    moved = lax.ppermute(design_bf[keep:], "core", swap)
+    packed = design_bf[:keep].at[short_most : short_most + moved.shape[0]].add(moved)
+    own_rows = jnp.concatenate([packed, terms_bf], axis=0)
+    signed_rows = jnp.concatenate([packed, -terms_bf], axis=0)
     gathered = lax.all_gather(signed_rows, "panel", axis=1, tiled=True)
     gathered, right_hand = lax.optimization_barrier((gathered, right_hand))
     half = panel_width // core_count

time: 299 us -> 282 us (0.943)
  waiting for transfers between devices: 160 us -> 143 us
  matrix products: 31.3 us -> 27.6 us
    all_gather x1, waiting for transfers between devices: 23.1 us -> 8.56 us  [body(): gathered = lax.all_gather(signed_rows, 'panel', axis=1, tiled=True)]
    dot_general x1, matrix products: 22.7 us -> 19 us  [body(): lax.dot_general(row_side, col_side, (((0,), (0,)), ((), ())), preferred_e...]
    all_to_all x1, waiting for transfers between devices: 10.1 us -> 13.3 us  [body(): lax.all_to_all(send_design, TM, split_axis=0, concat_axis=0, tiled=True)]
  transfers between devices with their start and end apart: 8 -> 9, of which waited for: 8 -> 7; matrix products, arithmetic and copies ran while one was open for 8% -> 10% of each run, Pallas kernels for 0% -> 0%
where the time goes in v7:
time: 282 us; the launch traced here: 280 us
  waiting for transfers between devices  143 us (51%)
  blocking collectives  38 us (13%)
  matrix products  27.6 us (10%)
  other arithmetic  23.7 us (8%)
  starting transfers between devices  17.1 us (6%)
  between operations  16.4 us (6%)
  local copies, waits for them, and re-layouts  14 us (5%)
    reduce_scatter x1, waiting for transfers between devices, body(): lax.psum_scatter((product * scale).astype(jnp.bfloat16), 'tmc', scatter_d...  108 us
    psum x1, blocking collectives, body(): lax.psum(right_part + lax.ppermute(right_part, 'core', swap), 'tmc')  38 us
    dot_general x1, matrix products, body(): lax.dot_general(row_side, col_side, (((0,), (0,)), ((), ())), preferred_e...  19 us
    all_to_all x1, waiting for transfers between devices, body(): lax.all_to_all(send_design, TM, split_axis=0, concat_axis=0, tiled=True)  13.3 us
    ppermute x1, waiting for transfers between devices, body(): got_cols = lax.ppermute(own_rows, 'core', swap)  9.26 us
    all_gather x1, waiting for transfers between devices, body(): gathered = lax.all_gather(signed_rows, 'panel', axis=1, tiled=True)  8.56 us
    all_to_all x1, starting transfers between devices, body(): lax.all_to_all(send_params, TM, split_axis=0, concat_axis=0, tiled=True)  8.16 us
    all_to_all x1, starting transfers between devices, body(): lax.all_to_all(send_design, TM, split_axis=0, concat_axis=0, tiled=True)  7.39 us
  transfers between devices with their start and end apart: 9, of which 7 were waited for; matrix products, arithmetic and copies ran while one was open for 10% of the time, Pallas kernels for 0%

profile of v7, /device:TPU:24, one launch (start us, length us, event | category | flops | bytes accessed | tf_op | source)
XLA Modules:
  0.0 280.3 jit_solution(12313275589524442381)
XLA Ops:
  7.2 0.5 broadcast.199
  7.7 2.2 fusion.39
  9.9 0.1 reshape_squeeze.3
  10.0 0.2 dynamic-slice_reduce_fusion
  10.2 0.6 reduce-window.6
  10.8 0.2 slice_reduce_fusion.1
  11.0 0.1 fusion.43
  11.1 0.1 copy.11
  11.3 0.2 fusion.35
  11.5 1.4 scatter_custom_fusion
  12.9 0.1 broadcast_in_dim.53
  13.0 0.8 broadcast_in_dim.60
  13.8 0.9 copy.12
  14.7 0.1 fusion.37
  14.8 1.4 gather_fusion.1
  16.3 0.1 broadcast_select_fusion.1
  16.4 0.8 reshape.207
  17.2 8.2 %all-to-all-start.1 = ((bf16[32,2,390]{2,1,0:T(2,128)(2,1)}), bf16[32,2,390]{2,1,0:T(2,128)(2,1)S(1)}, u32[]{:S(2)}, u32[]{:S(2)}) async-start(bf16[32,2,390]{2,1,0:T(2,128)(2,1)} %reshape.207), calls=%async_computation.1 | async-start | bytes 131072 | tf_op jit(solution)/shard_map/all_to_all | solution.py:79
  25.4 0.2 concatenate.30
  25.7 2.5 gather_fusion
  28.2 0.4 gather.13
  28.6 1.6 broadcast_select_fusion
  30.2 0.7 and_select_fusion
  30.9 0.6 dynamic_slice.20
  31.5 0.6 dynamic_slice.19
  34.1 0.1 lt.84
  34.2 7.4 %all-to-all-start = ((bf16[32,12,1920]{2,1,0:T(8,128)(2,1)}), bf16[32,12,1920]{2,1,0:T(8,128)(2,1)S(1)}, u32[]{:S(2)}, u32[]{:S(2)}) async-start(bf16[32,12,1920]{2,1,0:T(8,128)(2,1)} %broadcast_select_fusion), calls=%async_computation | async-start | bytes 3932160 | tf_op jit(solution)/shard_map/all_to_all | solution.py:78
  41.8 0.1 add.129
  41.9 0.6 iota_compare_fusion.7
  42.5 0.2 reshape.208
  42.7 0.7 fusion.29
  43.4 0.2 fusion.77
  43.8 5.8 %cholesky.17 = f32[64,64]{1,0:T(8,128)S(1)} custom-call(f32[64,64]{1,0:T(8,128)S(1)} %fusion.47), custom_call_target="Cholesky" | custom-call | tf_op jit(solution)/shard_map/jit(cholesky)/cholesky | solution.py:32
  49.7 0.6 compare_reduce_fusion
  50.3 0.7 fusion.38
  51.0 4.9 %custom-call.6 = f32[1,64,64]{1,2,0:T(8,128)S(1)} custom-call(f32[1,64,64]{2,1,0:T(8,128)S(1)} %fusion.38), custom_call_target="InvertDiagBlocksLowerTriangular" | custom-call | tf_op jit(solution)/shard_map/triangular_solve | solution.py:33
  55.9 13.3 %all-to-all-done = bf16[32,12,1920]{2,1,0:T(8,128)(2,1)S(1)} async-done(((bf16[32,12,1920]{2,1,0:T(8,128)(2,1)}), bf16[32,12,1920]{2,1,0:T(8,128)(2,1)S(1)}, u32[]{:S(2)}, u32[]{:S(2)}) %all-to-all-start) | async-done | bytes 1474592 | tf_op jit(solution)/shard_map/all_to_all | solution.py:78
  69.1 1.3 reshape.146
  70.4 2.8 fusion.76
  73.2 0.3 collective-permute-start
  73.5 0.3 fusion.44
  73.8 0.1 slice.60
  73.9 1.7 fusion.75
  75.5 0.1 fusion.27
  75.7 1.8 pad_maximum_fusion.1
  77.6 1.1 slice_reduce_fusion
  78.7 0.7 convolution_bitcast_fusion
  79.3 0.2 convolution_bitcast_fusion.1
  79.5 0.4 convolution_reduce_fusion
  79.9 1.7 fusion.8
  81.6 0.6 collective-permute-start.1
  82.2 0.8 collective-permute-done.1
  83.0 38.0 %psum.7 = f32[1920]{0:T(1024)} all-reduce(f32[1920]{0:T(1024)S(1)} %add.144), channel_id=1, replica_groups=mesh['tmc'=16,'core'=2,'panel'=4] {'tmc'}, use_global_device_ids=true, to_apply=%region_9.10 | all-reduce | flops 1920 | bytes 15360 | tf_op jit(solution)/shard_map/psum | solution.py:99
  121.0 8.6 %all-gather.2.cloned.1.call-done = bf16[336,7680]{1,0:T(8,128)(2,1)} async-done(((bf16[336,1920]{1,0:T(8,128)(2,1)}), bf16[336,7680]{1,0:T(8,128)(2,1)}) %all-gather.2.cloned.1.call-update) | async-done | bytes 5160976 | tf_op jit(solution)/shard_map/all_gather | solution.py:106
  129.6 0.5 collective-permute-start.3
  130.1 9.3 %collective-permute-done.3 = bf16[336,1920]{1,0:T(8,128)(2,1)S(1)} collective-permute-done((bf16[336,1920]{1,0:T(8,128)(2,1)}, bf16[336,1920]{1,0:T(8,128)(2,1)S(1)}, u32[]{:S(2)}, u32[]{:S(2)}) %collective-permute-start.3) | collective-permute-done | bytes 1290272 | tf_op jit(solution)/shard_map/ppermute | solution.py:110
  139.4 1.0 collective-permute-done.2
  140.3 19.0 %multiply_convert_fusion = bf16[7680,960]{1,0:T(8,128)(2,1)} fusion(bf16[336,7680]{1,0:T(8,128)(2,1)} %collective-permute-done.2, bf16[336,7680]{1,0:T(8,128)(2,1)} %all-gather.2.cloned.1.call-done, s32[]{:T(128)S(6)} %select_n.84, bf16[272,1920]{1,0:T(8,128)(2,1)} %copy-done, bf16[64,1920]{1,0:T(8,128)(2,1)} %copy-done.1, ...), kind=kOutput, calls=%fused_computation.3 | convolution fusion | flops 9948303360 | bytes 27648004 | tf_op jit(solution)/shard_map/dot_general | solution.py:115
  159.4 108.0 %reduce-scatter.2.cloned.1.call-done = bf16[480,960]{1,0:T(8,128)(2,1)} async-done(((bf16[7680,960]{1,0:T(8,128)(2,1)}), bf16[480,960]{1,0:T(8,128)(2,1)}) %reduce-scatter.2.cloned.1.call-update) | async-done | bytes 921616 | tf_op jit(solution)/shard_map/reduce_scatter | solution.py:118
  267.4 1.4 convert.1
  268.8 0.1 dynamic-slice_bitcast_fusion.1
  269.0 0.1 collective-permute-start.4
  269.1 2.5 collective-permute-done.4
  271.6 1.8 maximum_select_fusion
  (39 shorter events, 0.7 us)
Async XLA Ops:
  7.2 18.3 %copy-start.2 = (bf16[256,1920]{1,0:T(8,128)(2,1)S(1)}, bf16[256,1920]{1,0:T(8,128)(2,1)}, u32[]{:S(2)}) copy-start(bf16[256,1920]{1,0:T(8,128)(2,1)} %param.8) | copy-start | bytes 2949124
  17.2 17.0 %all-to-all-start.1 = ((bf16[32,2,390]{2,1,0:T(2,128)(2,1)}), bf16[32,2,390]{2,1,0:T(2,128)(2,1)S(1)}, u32[]{:S(2)}, u32[]{:S(2)}) async-start(bf16[32,2,390]{2,1,0:T(2,128)(2,1)} %reshape.207), calls=%async_computation.1 | async-start | bytes 131072 | tf_op jit(solution)/shard_map/all_to_all | solution.py:79
  28.6 2.3 copy-start.4
  28.6 2.9 %copy-start.5 = (f32[32]{0:T(128)S(1)}, f32[32]{0:T(128)}, u32[]{:S(2)}) copy-start(f32[32]{0:T(128)} %param.12) | copy-start | bytes 388
  34.2 34.9 %all-to-all-start = ((bf16[32,12,1920]{2,1,0:T(8,128)(2,1)}), bf16[32,12,1920]{2,1,0:T(8,128)(2,1)S(1)}, u32[]{:S(2)}, u32[]{:S(2)}) async-start(bf16[32,12,1920]{2,1,0:T(8,128)(2,1)} %broadcast_select_fusion), calls=%async_computation | async-start | bytes 3932160 | tf_op jit(solution)/shard_map/all_to_all | solution.py:78
  41.6 88.0 %all-gather.2.cloned.1.call-start = ((), (), s32[]{:S(2)}) async-start(), calls=%async_computation.3 | async-start | bytes 6451200 | tf_op jit(solution)/shard_map/all_gather | solution.py:106
  42.7 6.9 %copy-start.3 = (bf16[384,65]{1,0:T(8,128)(2,1)}, bf16[384,65]{1,0:T(8,128)(2,1)S(1)}, u32[]{:S(2)}) copy-start(bf16[384,65]{1,0:T(8,128)(2,1)S(1)} %reshape.147) | copy-start | bytes 149764
  73.2 2.3 collective-permute-start
  75.5 2.0 copy-start.1
  75.7 1.8 copy-start
  77.5 189.9 %reduce-scatter.2.cloned.1.call-start = ((), (), s32[]{:S(2)}) async-start(), calls=%async_computation.4 | async-start | bytes 16711680 | tf_op jit(solution)/shard_map/reduce_scatter | solution.py:118
  81.6 1.4 collective-permute-start.1
  129.6 10.7 %collective-permute-start.2 = (bf16[336,7680]{1,0:T(8,128)(2,1)}, bf16[336,7680]{1,0:T(8,128)(2,1)}, u32[]{:S(2)}, u32[]{:S(2)}) collective-permute-start(bf16[336,7680]{1,0:T(8,128)(2,1)} %all-gather.2.cloned.1.call-done), channel_id=1, source_target_pairs={{0,4},{4,0},{1,5},{5,1},{2,6},{6,2},{3,7},{7,3},{8,12},{12,8},{9,1... | collective-permute-start | bytes 15482888 | tf_op jit(solution)/shard_map/ppermute | solution.py:109
  129.6 9.8 %collective-permute-start.3 = (bf16[336,1920]{1,0:T(8,128)(2,1)}, bf16[336,1920]{1,0:T(8,128)(2,1)S(1)}, u32[]{:S(2)}, u32[]{:S(2)}) collective-permute-start(bf16[336,1920]{1,0:T(8,128)(2,1)} %get-tuple-element.25), channel_id=1, source_target_pairs={{0,4},{4,0},{1,5},{5,1},{2,6},{6,2},{3,7},{7,3},{8,12},{12,8},{9,1... | collective-permute-start | bytes 3870728 | tf_op jit(solution)/shard_map/ppermute | solution.py:110
  269.0 2.6 collective-permute-start.4
Sparse Core Ops, SparseCore 0:
  77.6 51.9 all-gather.1
  159.5 107.8 reduce-scatter.1

commit v8 on v7

--- a/solution.py
+++ b/solution.py
@@ -37,7 +37,7 @@
         jnp.dot(white_design.T, white_obs, precision=lax.Precision.HIGHEST)
         - jnp.dot(arc_terms.T, arc_rhs, precision=lax.Precision.HIGHEST)
     ) * scale
-    return (white_design.astype(jnp.bfloat16), arc_terms.astype(jnp.bfloat16), right_part)
+    return (white_design.astype(jnp.bfloat16), basis, right_part)
 
 
 def body(design, partials, observed, arc_of_row, autoreg, movavg):
@@ -94,23 +94,37 @@
         position, order_pos, position < arc_length, usable,
         autoreg[device_index], movavg[device_index],
     )
-    design_bf, terms_bf, right_part = eliminate(whitener, got_design, got_params, got_obs, scale)
+    design_bf, basis, right_part = eliminate(whitener, got_design, got_params, got_obs, scale)
     swap = [(0, 1), (1, 0)]
     right_hand = lax.psum(right_part + lax.ppermute(right_part, "core", swap), "tmc")
     short_most = 5 * rows_dev // 8
     keep = (slot_count + short_most) // 2
     moved = lax.ppermute(design_bf[keep:], "core", swap)
     packed = design_bf[:keep].at[short_most : short_most + moved.shape[0]].add(moved)
-    own_rows = jnp.concatenate([packed, terms_bf], axis=0)
-    signed_rows = jnp.concatenate([packed, -terms_bf], axis=0)
-    gathered = lax.all_gather(signed_rows, "panel", axis=1, tiled=True)
+    gathered = lax.all_gather(packed, "panel", axis=1, tiled=True)
     gathered, right_hand = lax.optimization_barrier((gathered, right_hand))
     half = panel_width // core_count
     got_rows = lax.ppermute(gathered, "core", swap)
-    got_cols = lax.ppermute(own_rows, "core", swap)
-    row_side = jnp.concatenate([gathered, got_rows], axis=0)
+    got_basis = lax.ppermute(basis, "core", swap)
+    moved_count = slot_count - keep
+
+    def arc_terms(own_basis, home, away):
+        upper = jnp.dot(own_basis[:, :keep], home.astype(jnp.float32), precision=lax.Precision.HIGHEST)
+        lower = jnp.dot(
+            own_basis[:, keep:],
+            away[short_most : short_most + moved_count].astype(jnp.float32),
+            precision=lax.Precision.HIGHEST,
+        )
+        return (upper + lower).astype(jnp.bfloat16)
+
+    terms = jnp.concatenate(
+        [arc_terms(basis, gathered, got_rows), arc_terms(got_basis, got_rows, gathered)], axis=0
+    )
+    design_side = jnp.concatenate([gathered, got_rows], axis=0)
+    row_side = jnp.concatenate([design_side, -terms], axis=0)
     col_side = lax.dynamic_slice_in_dim(
-        jnp.concatenate([own_rows, got_cols], axis=0), core_index * half, half, 1
+        jnp.concatenate([design_side, terms], axis=0),
+        lax.axis_index("panel") * panel_width + core_index * half, half, 1,
     )
     product = lax.dot_general(
         row_side, col_side, (((0,), (0,)), ((), ())), preferred_element_type=jnp.float32

time: 282 us -> 293 us (1.039)
  matrix products: 27.6 us -> 46 us
  blocking collectives: 38 us -> 49 us
  waiting for transfers between devices: 143 us -> 134 us
  starting transfers between devices: 17.1 us -> 9.24 us
    dot_general x0 -> x4, matrix products: none -> 15.1 us  [the longest x2 10.1 us: arc_terms(): jnp.dot(own_basis[:, :keep], home.astype(jnp.float32), precision=lax.Prec...]
    all_to_all x0 -> x1, blocking collectives: none -> 10.6 us  [body(): lax.all_to_all(send_params, TM, split_axis=0, concat_axis=0, tiled=True)]
    all_to_all x1, waiting for transfers between devices: 13.3 us -> 22.5 us  [body(): lax.all_to_all(send_design, TM, split_axis=0, concat_axis=0, tiled=True)]
    all_gather x1, waiting for transfers between devices: 8.56 us -> 0.01 us  [body(): gathered = lax.all_gather(packed, 'panel', axis=1, tiled=True)]
    all_to_all x1 -> x0, starting transfers between devices: 8.16 us -> none  [body(): lax.all_to_all(send_params, TM, split_axis=0, concat_axis=0, tiled=True)]
    reduce_scatter x1, waiting for transfers between devices: 108 us -> 102 us  [body(): lax.psum_scatter((product * scale).astype(jnp.bfloat16), 'tmc', scatter_d...]
    ppermute x1, waiting for transfers between devices: 9.26 us -> 5.63 us  [body(): got_basis = lax.ppermute(basis, 'core', swap)]
    dot_general x1, matrix products: 1.65 us -> 5.07 us  [eliminate(): arc_terms = jnp.dot(basis, white_design, precision=lax.Precision.HIGHEST)]
  transfers between devices with their start and end apart: 9 -> 8, of which waited for: 7 -> 6; matrix products, arithmetic and copies ran while one was open for 10% -> 12% of each run, Pallas kernels for 0% -> 0%
where the time goes in v8:
time: 293 us; the launch traced here: 291 us
  waiting for transfers between devices  134 us (46%)
  blocking collectives  49 us (17%)
  matrix products  46 us (16%)
  other arithmetic  23 us (8%)
  between operations  16.4 us (6%)
  local copies, waits for them, and re-layouts  13.3 us (5%)
  starting transfers between devices  9.24 us (3%)
    reduce_scatter x1, waiting for transfers between devices, body(): lax.psum_scatter((product * scale).astype(jnp.bfloat16), 'tmc', scatter_d...  102 us
    psum x1, blocking collectives, body(): lax.psum(right_part + lax.ppermute(right_part, 'core', swap), 'tmc')  38.4 us
    all_to_all x1, waiting for transfers between devices, body(): lax.all_to_all(send_design, TM, split_axis=0, concat_axis=0, tiled=True)  22.5 us
    dot_general x1, matrix products, body(): lax.dot_general(row_side, col_side, (((0,), (0,)), ((), ())), preferred_e...  18.3 us
    all_to_all x1, blocking collectives, body(): lax.all_to_all(send_params, TM, split_axis=0, concat_axis=0, tiled=True)  10.6 us
    dot_general x2, matrix products, arc_terms(): jnp.dot(own_basis[:, :keep], home.astype(jnp.float32), precision=lax.Prec...  10.1 us
    all_to_all x1, starting transfers between devices, body(): lax.all_to_all(send_design, TM, split_axis=0, concat_axis=0, tiled=True)  8.29 us
    another operation x3, other arithmetic, eliminate(): factor = jnp.linalg.cholesky(param_gram)  6.52 us
  transfers between devices with their start and end apart: 8, of which 6 were waited for; matrix products, arithmetic and copies ran while one was open for 12% of the time, Pallas kernels for 0%

profile of v8, /device:TPU:24, one launch (start us, length us, event | category | flops | bytes accessed | tf_op | source)
XLA Modules:
  0.0 291.4 jit_solution(3240795007972703994)
XLA Ops:
  7.2 0.5 broadcast.199
  7.7 2.2 fusion.47
  10.0 0.2 dynamic-slice_reduce_fusion
  10.2 0.6 reduce-window.6
  10.8 0.2 slice_reduce_fusion.1
  11.0 0.1 fusion.51
  11.1 0.1 copy.11
  11.3 0.2 fusion.40
  11.5 1.4 scatter_custom_fusion
  12.9 0.1 broadcast_in_dim.53
  13.0 1.4 concatenate.29
  14.5 2.5 gather_fusion
  17.0 0.4 gather.13
  17.4 1.6 broadcast_select_fusion
  18.9 8.3 %all-to-all-start = ((bf16[32,12,1920]{2,1,0:T(8,128)(2,1)}), bf16[32,12,1920]{2,1,0:T(8,128)(2,1)S(1)}, u32[]{:S(2)}, u32[]{:S(2)}) async-start(bf16[32,12,1920]{2,1,0:T(8,128)(2,1)} %broadcast_select_fusion), calls=%async_computation | async-start | bytes 3932160 | tf_op jit(solution)/shard_map/all_to_all | solution.py:78
  27.3 0.7 dynamic_slice.20
  28.0 0.6 dynamic_slice.19
  30.6 0.1 lt.84
  30.7 0.6 and_select_fusion
  31.5 0.1 add.138
  31.6 0.7 iota_compare_fusion.7
  32.2 22.5 %all-to-all-done = bf16[32,12,1920]{2,1,0:T(8,128)(2,1)S(1)} async-done(((bf16[32,12,1920]{2,1,0:T(8,128)(2,1)}), bf16[32,12,1920]{2,1,0:T(8,128)(2,1)S(1)}, u32[]{:S(2)}, u32[]{:S(2)}) %all-to-all-start) | async-done | bytes 1474592 | tf_op jit(solution)/shard_map/all_to_all | solution.py:78
  54.7 1.3 reshape.146
  56.0 2.8 fusion.85
  58.9 1.0 slice.84
  60.0 0.7 collective-permute-done
  60.7 0.9 fusion.32
  61.6 0.1 broadcast_in_dim.60
  61.8 0.1 copy.12
  61.9 0.1 fusion.45
  62.0 1.4 gather_fusion.1
  63.5 0.1 broadcast_select_fusion.1
  63.6 0.2 reshape.207
  63.8 10.6 %all_to_all.10 = bf16[32,2,390]{2,1,0:T(2,128)(2,1)S(1)} all-to-all(bf16[32,2,390]{2,1,0:T(2,128)(2,1)S(1)} %reshape.207), channel_id=1, replica_groups=mesh['tmc'=16,'core'=2,'panel'=4] {'tmc','core'}, dimensions={0} | all-to-all | bytes 99840 | tf_op jit(solution)/shard_map/all_to_all | solution.py:79
  74.4 0.2 reshape.208
  74.6 0.7 fusion.33
  75.3 0.2 fusion.86
  75.6 5.8 %cholesky.17 = f32[64,64]{1,0:T(8,128)S(1)} custom-call(f32[64,64]{1,0:T(8,128)S(1)} %fusion.57), custom_call_target="Cholesky" | custom-call | tf_op jit(solution)/shard_map/jit(cholesky)/cholesky | solution.py:32
  81.5 0.6 compare_reduce_fusion
  82.2 0.7 fusion.46
  82.8 4.9 %custom-call.6 = f32[1,64,64]{1,2,0:T(8,128)S(1)} custom-call(f32[1,64,64]{2,1,0:T(8,128)S(1)} %fusion.46), custom_call_target="InvertDiagBlocksLowerTriangular" | custom-call | tf_op jit(solution)/shard_map/triangular_solve | solution.py:33
  87.7 0.2 slice_reduce_fusion
  87.9 0.7 convolution_bitcast_fusion
  88.6 0.3 fusion.54
  88.9 0.2 convolution_bitcast_fusion.1
  89.1 5.1 %fusion.87 = f32[1920,64]{1,0:T(8,128)S(1)} fusion(f32[384,1920]{1,0:T(8,128)S(1)} %get-tuple-element.24, f32[64,384]{1,0:T(8,128)S(1)} %fusion.54), kind=kOutput, calls=%fused_computation.135 | convolution fusion | flops 566231040 | bytes 3538944 | tf_op jit(solution)/shard_map/dot_general | solution.py:34
  94.1 1.0 convolution_reduce_fusion
  95.2 1.7 fusion.14
  96.9 0.2 collective-permute-start.1
  97.0 1.1 collective-permute-done.1
  98.1 38.4 %psum.7 = f32[1920]{0:T(1024)} all-reduce(f32[1920]{0:T(1024)S(1)} %add.153), channel_id=1, replica_groups=mesh['tmc'=16,'core'=2,'panel'=4] {'tmc'}, use_global_device_ids=true, to_apply=%region_9.10 | all-reduce | flops 1920 | bytes 15360 | tf_op jit(solution)/shard_map/psum | solution.py:99
  136.5 0.5 collective-permute-start.3
  137.0 5.6 %collective-permute-done.3 = f32[64,384]{1,0:T(8,128)S(1)} collective-permute-done((f32[64,384]{1,0:T(8,128)S(1)}, f32[64,384]{1,0:T(8,128)S(1)}, u32[]{:S(2)}, u32[]{:S(2)}) %collective-permute-start.3) | collective-permute-done | bytes 98336 | tf_op jit(solution)/shard_map/ppermute | solution.py:108
  142.6 2.4 fusion.8
  145.1 4.8 %fusion.42 = f32[64,7680]{1,0:T(8,128)S(1)} fusion(bf16[272,7680]{1,0:T(8,128)(2,1)} %all-gather.2.cloned.1.call-done, f32[64,384]{1,0:T(8,128)S(1)} %fusion.54), kind=kOutput, calls=%fused_computation.65 | convolution fusion | flops 1604321280 | bytes 6242304 | tf_op jit(solution)/shard_map/dot_general | solution.py:112
  149.9 2.5 fusion.3
  152.5 5.3 %fusion.4 = bf16[64,7680]{1,0:T(8,128)(2,1)S(1)} fusion(f32[64,7680]{1,0:T(8,128)S(1)} %fusion.8, bf16[272,7680]{1,0:T(8,128)(2,1)} %collective-permute-done.2, f32[64,384]{1,0:T(8,128)S(1)} %collective-permute-done.3), kind=kOutput, calls=%fused_computation.14 | convolution fusion | flops 1605304320 | bytes 7225344 | tf_op jit(solution)/shard_map/dot_general | solution.py:112
  157.8 0.3 maximum_negate_fusion
  158.1 18.3 %multiply_convert_fusion = bf16[7680,960]{1,0:T(8,128)(2,1)} fusion(bf16[272,7680]{1,0:T(8,128)(2,1)} %collective-permute-done.2, bf16[272,7680]{1,0:T(8,128)(2,1)S(1)} %copy-done, bf16[128,7680]{1,0:T(8,128)(2,1)S(1)} %maximum_negate_fusion, s32[]{:T(128)S(6)} %select_n.84, bf16[64,7680]{1,0:T(8,128)(2,1)S(1)} %fusion.4, bf16[64,7680]{1,0:T(8,128)(2,1)S(1)} %fusion.3), kind=kOutput, calls=%fused_computation.3 | convolution fusion | flops 9959915520 | bytes 35389444 | tf_op jit(solution)/shard_map/dot_general | solution.py:129
  176.5 102.0 %reduce-scatter.2.cloned.1.call-done = bf16[480,960]{1,0:T(8,128)(2,1)} async-done(((bf16[7680,960]{1,0:T(8,128)(2,1)}), bf16[480,960]{1,0:T(8,128)(2,1)}) %reduce-scatter.2.cloned.1.call-update) | async-done | bytes 921616 | tf_op jit(solution)/shard_map/reduce_scatter | solution.py:132
  278.5 1.4 convert.1
  279.9 0.1 dynamic-slice_bitcast_fusion.1
  280.1 2.5 collective-permute-done.4
  282.7 1.8 maximum_select_fusion
  (44 shorter events, 0.9 us)
Async XLA Ops:
  10.0 2.9 %copy-start.1 = (s32[256,32]{1,0:T(8,128)}, s32[256,32]{1,0:T(8,128)S(1)}, u32[]{:S(2)}) copy-start(s32[256,32]{1,0:T(8,128)S(1)} %reshape_squeeze.3) | copy-start | bytes 98308
  18.9 8.4 %copy-start.5 = (f32[32]{0:T(128)S(1)}, f32[32]{0:T(128)}, u32[]{:S(2)}) copy-start(f32[32]{0:T(128)} %param.13) | copy-start | bytes 388
  18.9 9.0 %copy-start.6 = (f32[32]{0:T(128)S(1)}, f32[32]{0:T(128)}, u32[]{:S(2)}) copy-start(f32[32]{0:T(128)} %param.12) | copy-start | bytes 388
  18.9 11.5 %copy-start.2 = (s32[256,32]{1,0:T(8,128)S(1)}, s32[256,32]{1,0:T(8,128)}, u32[]{:S(2)}) copy-start(s32[256,32]{1,0:T(8,128)} %copy-done.1) | copy-start | bytes 98308
  18.9 35.8 %all-to-all-start = ((bf16[32,12,1920]{2,1,0:T(8,128)(2,1)}), bf16[32,12,1920]{2,1,0:T(8,128)(2,1)S(1)}, u32[]{:S(2)}, u32[]{:S(2)}) async-start(bf16[32,12,1920]{2,1,0:T(8,128)(2,1)} %broadcast_select_fusion), calls=%async_computation | async-start | bytes 3932160 | tf_op jit(solution)/shard_map/all_to_all | solution.py:78
  27.2 109.2 %all-gather.2.cloned.1.call-start = ((), (), s32[]{:S(2)}) async-start(), calls=%async_computation.3 | async-start | bytes 5222400 | tf_op jit(solution)/shard_map/all_gather | solution.py:104
  58.8 2.9 copy-start.4
  58.8 3.0 %copy-start.3 = (bf16[256,64]{0,1:T(8,128)(2,1)S(1)}, bf16[256,64]{0,1:T(8,128)(2,1)}, u32[]{:S(2)}) copy-start(bf16[256,64]{0,1:T(8,128)(2,1)} %param.9) | copy-start | bytes 98308
  58.8 1.9 collective-permute-start
  61.6 216.9 %reduce-scatter.2.cloned.1.call-start = ((), (), s32[]{:S(2)}) async-start(), calls=%async_computation.4 | async-start | bytes 16711680 | tf_op jit(solution)/shard_map/reduce_scatter | solution.py:132
  96.9 1.3 collective-permute-start.1
  136.5 13.4 %collective-permute-start.2 = (bf16[272,7680]{1,0:T(8,128)(2,1)}, bf16[272,7680]{1,0:T(8,128)(2,1)}, u32[]{:S(2)}, u32[]{:S(2)}) collective-permute-start(bf16[272,7680]{1,0:T(8,128)(2,1)} %all-gather.2.cloned.1.call-done), channel_id=1, source_target_pairs={{0,4},{4,0},{1,5},{5,1},{2,6},{6,2},{3,7},{7,3},{8,12},{12,8},{9,1... | collective-permute-start | bytes 12533768 | tf_op jit(solution)/shard_map/ppermute | solution.py:107
  136.5 6.1 %collective-permute-start.3 = (f32[64,384]{1,0:T(8,128)S(1)}, f32[64,384]{1,0:T(8,128)S(1)}, u32[]{:S(2)}, u32[]{:S(2)}) collective-permute-start(f32[64,384]{1,0:T(8,128)S(1)} %fusion.54), channel_id=1, source_target_pairs={{0,4},{4,0},{1,5},{5,1},{2,6},{6,2},{3,7},{7,3},{8,12},{12,8},{9,1... | collective-permute-start | bytes 294920 | tf_op jit(solution)/shard_map/ppermute | solution.py:108
  152.5 5.7 %copy-start = (bf16[272,7680]{1,0:T(8,128)(2,1)S(1)}, bf16[272,7680]{1,0:T(8,128)(2,1)}, u32[]{:S(2)}) copy-start(bf16[272,7680]{1,0:T(8,128)(2,1)} %all-gather.2.cloned.1.call-done) | copy-start | bytes 12533764
  280.0 2.6 collective-permute-start.4
Sparse Core Ops, SparseCore 0:
  61.7 43.4 all-gather.1
  176.6 101.8 reduce-scatter.1

commit v9 on v8

--- a/solution.py
+++ b/solution.py
@@ -74,10 +74,9 @@
     send_design = pick_rows(design).reshape(tile_count, capacity, panel_width)
     with_obs = jnp.concatenate([partials, observed[:, None]], axis=1)
     send_params = pick_rows(with_obs).reshape(tile_count, capacity, param_count + 1)
-    got_design, got_params = (
-        lax.all_to_all(send_design, TM, split_axis=0, concat_axis=0, tiled=True),
-        lax.all_to_all(send_params, TM, split_axis=0, concat_axis=0, tiled=True),
-    )
+    got_params = lax.all_to_all(send_params, TM, split_axis=0, concat_axis=0, tiled=True)
+    send_design, got_params = lax.optimization_barrier((send_design, got_params))
+    got_design = lax.all_to_all(send_design, TM, split_axis=0, concat_axis=0, tiled=True)
     got_design = got_design.reshape(slot_count, panel_width)
     got_params = got_params.reshape(slot_count, param_count + 1)
     got_obs = got_params[:, param_count]
@@ -109,11 +108,12 @@
     moved_count = slot_count - keep
 
     def arc_terms(own_basis, home, away):
-        upper = jnp.dot(own_basis[:, :keep], home.astype(jnp.float32), precision=lax.Precision.HIGHEST)
+        own_basis = own_basis.astype(jnp.bfloat16)
+        upper = jnp.dot(own_basis[:, :keep], home, preferred_element_type=jnp.float32)
         lower = jnp.dot(
             own_basis[:, keep:],
-            away[short_most : short_most + moved_count].astype(jnp.float32),
-            precision=lax.Precision.HIGHEST,
+            away[short_most : short_most + moved_count],
+            preferred_element_type=jnp.float32,
         )
         return (upper + lower).astype(jnp.bfloat16)
 

time: 293 us -> 286 us (0.976)
  blocking collectives: 49 us -> 38 us
  starting transfers between devices: 9.24 us -> 13.9 us
  matrix products: 46 us -> 41.4 us
  waiting for transfers between devices: 134 us -> 137 us
    all_to_all x1 -> x0, blocking collectives: 10.6 us -> none  [body(): lax.all_to_all(send_params, TM, split_axis=0, concat_axis=0, tiled=True)]
    all_to_all x0 -> x1, starting transfers between devices: none -> 8.16 us  [body(): lax.all_to_all(send_params, TM, split_axis=0, concat_axis=0, tiled=True)]
    dot_general x4, matrix products: 15.1 us -> 10.5 us  [the longest x2 6.64 us: arc_terms(): jnp.dot(own_basis[:, :keep], home, preferred_element_type=jnp.float32)]
    all_to_all x1, starting transfers between devices: 8.29 us -> 4.59 us  [body(): lax.all_to_all(send_design, TM, split_axis=0, concat_axis=0, tiled=True)]
  transfers between devices with their start and end apart: 8 -> 9, of which waited for: 6 -> 7; matrix products, arithmetic and copies ran while one was open for 12% -> 13% of each run, Pallas kernels for 0% -> 0%
where the time goes in v9:
time: 286 us; the launch traced here: 284 us
  waiting for transfers between devices  137 us (48%)
  matrix products  41.4 us (14%)
  blocking collectives  38 us (13%)
  other arithmetic  23.1 us (8%)
  between operations  16.4 us (6%)
  local copies, waits for them, and re-layouts  14.1 us (5%)
  starting transfers between devices  13.9 us (5%)
    reduce_scatter x1, waiting for transfers between devices, body(): lax.psum_scatter((product * scale).astype(jnp.bfloat16), 'tmc', scatter_d...  102 us
    psum x1, blocking collectives, body(): lax.psum(right_part + lax.ppermute(right_part, 'core', swap), 'tmc')  38 us
    all_to_all x1, waiting for transfers between devices, body(): lax.all_to_all(send_design, TM, split_axis=0, concat_axis=0, tiled=True)  22.4 us
    dot_general x1, matrix products, body(): lax.dot_general(row_side, col_side, (((0,), (0,)), ((), ())), preferred_e...  18.3 us
    all_to_all x1, starting transfers between devices, body(): lax.all_to_all(send_params, TM, split_axis=0, concat_axis=0, tiled=True)  8.16 us
    dot_general x2, matrix products, arc_terms(): jnp.dot(own_basis[:, :keep], home, preferred_element_type=jnp.float32)  6.64 us
    another operation x3, other arithmetic, eliminate(): factor = jnp.linalg.cholesky(param_gram)  6.52 us
  transfers between devices with their start and end apart: 9, of which 7 were waited for; matrix products, arithmetic and copies ran while one was open for 13% of the time, Pallas kernels for 0%

profile of v9, /device:TPU:24, one launch (start us, length us, event | category | flops | bytes accessed | tf_op | source)
XLA Modules:
  0.0 283.9 jit_solution(15471324224820011392)
XLA Ops:
  7.2 0.5 broadcast.199
  7.7 2.2 fusion.47
  10.0 0.2 dynamic-slice_reduce_fusion
  10.2 0.6 reduce-window.6
  10.8 0.2 slice_reduce_fusion.1
  11.2 0.1 copy.11
  11.3 0.2 fusion.40
  11.5 1.4 scatter_custom_fusion
  13.0 0.1 broadcast_in_dim.53
  13.1 0.8 broadcast_in_dim.60
  13.8 0.9 copy.12
  14.8 1.4 gather_fusion.1
  16.3 0.1 broadcast_select_fusion.1
  16.5 0.8 reshape.207
  17.3 8.2 %all-to-all-start = ((bf16[32,2,390]{2,1,0:T(2,128)(2,1)}), bf16[32,2,390]{2,1,0:T(2,128)(2,1)S(1)}, u32[]{:S(2)}, u32[]{:S(2)}) async-start(bf16[32,2,390]{2,1,0:T(2,128)(2,1)} %reshape.207), calls=%async_computation | async-start | bytes 131072 | tf_op jit(solution)/shard_map/all_to_all | solution.py:77
  25.4 0.2 concatenate.29
  25.7 2.5 gather_fusion
  28.2 0.4 gather.13
  28.6 1.6 broadcast_select_fusion
  30.1 2.8 all-to-all-done
  33.0 0.2 reshape.208
  33.1 4.6 %all-to-all-start.1 = ((bf16[32,12,1920]{2,1,0:T(8,128)(2,1)}), bf16[32,12,1920]{2,1,0:T(8,128)(2,1)S(1)}, u32[]{:S(2)}, u32[]{:S(2)}) async-start(bf16[32,12,1920]{2,1,0:T(8,128)(2,1)} %broadcast_select_fusion), calls=%async_computation.1 | async-start | bytes 3932160 | tf_op jit(solution)/shard_map/all_to_all | solution.py:79
  37.8 0.6 dynamic_slice.20
  38.4 0.6 dynamic_slice.19
  41.1 0.1 lt.84
  41.2 0.7 and_select_fusion
  42.0 0.1 add.138
  42.1 0.7 iota_compare_fusion.7
  42.8 22.4 %all-to-all-done.1 = bf16[32,12,1920]{2,1,0:T(8,128)(2,1)S(1)} async-done(((bf16[32,12,1920]{2,1,0:T(8,128)(2,1)}), bf16[32,12,1920]{2,1,0:T(8,128)(2,1)S(1)}, u32[]{:S(2)}, u32[]{:S(2)}) %all-to-all-start.1) | async-done | bytes 1474592 | tf_op jit(solution)/shard_map/all_to_all | solution.py:79
  65.2 1.3 reshape.146
  66.5 2.8 fusion.86
  69.4 1.0 slice.84
  70.4 0.7 collective-permute-done
  71.1 0.9 fusion.32
  72.0 0.2 reduce-scatter.2.cloned.1.call-start
  72.3 0.7 fusion.33
  73.0 0.2 fusion.87
  73.4 5.8 %cholesky.17 = f32[64,64]{1,0:T(8,128)S(1)} custom-call(f32[64,64]{1,0:T(8,128)S(1)} %fusion.55), custom_call_target="Cholesky" | custom-call | tf_op jit(solution)/shard_map/jit(cholesky)/cholesky | solution.py:32
  79.2 0.6 compare_reduce_fusion
  79.9 0.7 fusion.46
  80.5 4.9 %custom-call.6 = f32[1,64,64]{1,2,0:T(8,128)S(1)} custom-call(f32[1,64,64]{2,1,0:T(8,128)S(1)} %fusion.46), custom_call_target="InvertDiagBlocksLowerTriangular" | custom-call | tf_op jit(solution)/shard_map/triangular_solve | solution.py:33
  85.4 0.2 slice_reduce_fusion
  85.7 0.7 convolution_bitcast_fusion
  86.3 0.3 fusion.85
  86.6 0.2 convolution_bitcast_fusion.1
  86.8 5.1 %fusion.88 = f32[1920,64]{1,0:T(8,128)S(1)} fusion(f32[384,1920]{1,0:T(8,128)S(1)} %get-tuple-element.30, f32[64,384]{1,0:T(8,128)S(1)} %get-tuple-element.31), kind=kOutput, calls=%fused_computation.136 | convolution fusion | flops 566231040 | bytes 3538944 | tf_op jit(solution)/shard_map/dot_general | solution.py:34
  91.9 1.0 convolution_reduce_fusion
  92.9 1.7 fusion.14
  94.6 0.2 collective-permute-start.1
  94.8 1.0 collective-permute-done.1
  95.8 38.0 %psum.7 = f32[1920]{0:T(1024)} all-reduce(f32[1920]{0:T(1024)S(1)} %add.153), channel_id=1, replica_groups=mesh['tmc'=16,'core'=2,'panel'=4] {'tmc'}, use_global_device_ids=true, to_apply=%region_9.10 | all-reduce | flops 1920 | bytes 15360 | tf_op jit(solution)/shard_map/psum | solution.py:98
  133.8 0.5 collective-permute-start.3
  134.4 5.5 %collective-permute-done.3 = bf16[64,384]{1,0:T(8,128)(2,1)S(1)} collective-permute-done((bf16[64,384]{1,0:T(8,128)(2,1)S(1)}, bf16[64,384]{1,0:T(8,128)(2,1)S(1)}, u32[]{:S(2)}, u32[]{:S(2)}) %collective-permute-start.3) | collective-permute-done | bytes 49184 | tf_op jit(solution)/shard_map/ppermute | solution.py:107
  139.9 1.9 fusion.8
  141.8 3.2 %fusion.44 = f32[64,7680]{1,0:T(8,128)S(1)} fusion(bf16[272,7680]{1,0:T(8,128)(2,1)} %all-gather.2.cloned.1.call-done, bf16[64,384]{1,0:T(8,128)(2,1)S(1)} %get-tuple-element.27), kind=kOutput, calls=%fused_computation.68 | convolution fusion | flops 267386880 | bytes 6193152 | tf_op jit(solution)/shard_map/dot_general | solution.py:112
  145.0 1.9 fusion.3
  147.0 3.4 %fusion.4 = bf16[64,7680]{1,0:T(8,128)(2,1)S(1)} fusion(f32[64,7680]{1,0:T(8,128)S(1)} %fusion.8, bf16[272,7680]{1,0:T(8,128)(2,1)} %collective-permute-done.2, bf16[64,384]{1,0:T(8,128)(2,1)S(1)} %collective-permute-done.3), kind=kOutput, calls=%fused_computation.14 | convolution fusion | flops 268369920 | bytes 7176192 | tf_op jit(solution)/shard_map/dot_general | solution.py:112
  150.4 0.3 maximum_negate_fusion
  150.7 18.3 %multiply_convert_fusion = bf16[7680,960]{1,0:T(8,128)(2,1)} fusion(bf16[272,7680]{1,0:T(8,128)(2,1)} %collective-permute-done.2, bf16[272,7680]{1,0:T(8,128)(2,1)S(1)} %copy-done, bf16[128,7680]{1,0:T(8,128)(2,1)S(1)} %maximum_negate_fusion, s32[]{:T(128)S(6)} %select_n.84, bf16[64,7680]{1,0:T(8,128)(2,1)S(1)} %fusion.4, bf16[64,7680]{1,0:T(8,128)(2,1)S(1)} %fusion.3), kind=kOutput, calls=%fused_computation.3 | convolution fusion | flops 9959915520 | bytes 35389444 | tf_op jit(solution)/shard_map/dot_general | solution.py:129
  169.1 102.0 %reduce-scatter.2.cloned.1.call-done = bf16[480,960]{1,0:T(8,128)(2,1)} async-done(((bf16[7680,960]{1,0:T(8,128)(2,1)}), bf16[480,960]{1,0:T(8,128)(2,1)}) %reduce-scatter.2.cloned.1.call-update) | async-done | bytes 921616 | tf_op jit(solution)/shard_map/reduce_scatter | solution.py:132
  271.0 1.4 convert.1
  272.5 0.1 dynamic-slice_bitcast_fusion.1
  272.7 2.5 collective-permute-done.4
  275.3 1.8 maximum_select_fusion
  (43 shorter events, 1.1 us)
Async XLA Ops:
  7.2 18.3 %copy-start.3 = (bf16[256,1920]{1,0:T(8,128)(2,1)S(1)}, bf16[256,1920]{1,0:T(8,128)(2,1)}, u32[]{:S(2)}) copy-start(bf16[256,1920]{1,0:T(8,128)(2,1)} %param.8) | copy-start | bytes 2949124
  10.0 3.8 %copy-start.1 = (s32[256,32]{1,0:T(8,128)}, s32[256,32]{1,0:T(8,128)S(1)}, u32[]{:S(2)}) copy-start(s32[256,32]{1,0:T(8,128)S(1)} %reshape_squeeze.3) | copy-start | bytes 98308
  17.3 15.7 %all-to-all-start = ((bf16[32,2,390]{2,1,0:T(2,128)(2,1)}), bf16[32,2,390]{2,1,0:T(2,128)(2,1)S(1)}, u32[]{:S(2)}, u32[]{:S(2)}) async-start(bf16[32,2,390]{2,1,0:T(2,128)(2,1)} %reshape.207), calls=%async_computation | async-start | bytes 131072 | tf_op jit(solution)/shard_map/all_to_all | solution.py:77
  30.1 7.6 %copy-start.4 = (f32[32]{0:T(128)S(1)}, f32[32]{0:T(128)}, u32[]{:S(2)}) copy-start(f32[32]{0:T(128)} %param.13) | copy-start | bytes 388
  30.1 8.3 %copy-start.5 = (f32[32]{0:T(128)S(1)}, f32[32]{0:T(128)}, u32[]{:S(2)}) copy-start(f32[32]{0:T(128)} %param.12) | copy-start | bytes 388
  30.1 10.8 %copy-start.2 = (s32[256,32]{1,0:T(8,128)S(1)}, s32[256,32]{1,0:T(8,128)}, u32[]{:S(2)}) copy-start(s32[256,32]{1,0:T(8,128)} %copy-done.1) | copy-start | bytes 98308
  33.1 32.1 %all-to-all-start.1 = ((bf16[32,12,1920]{2,1,0:T(8,128)(2,1)}), bf16[32,12,1920]{2,1,0:T(8,128)(2,1)S(1)}, u32[]{:S(2)}, u32[]{:S(2)}) async-start(bf16[32,12,1920]{2,1,0:T(8,128)(2,1)} %broadcast_select_fusion), calls=%async_computation.1 | async-start | bytes 3932160 | tf_op jit(solution)/shard_map/all_to_all | solution.py:79
  37.7 96.1 %all-gather.2.cloned.1.call-start = ((), (), s32[]{:S(2)}) async-start(), calls=%async_computation.3 | async-start | bytes 5222400 | tf_op jit(solution)/shard_map/all_gather | solution.py:103
  69.3 1.9 collective-permute-start
  72.0 199.0 %reduce-scatter.2.cloned.1.call-start = ((), (), s32[]{:S(2)}) async-start(), calls=%async_computation.4 | async-start | bytes 16711680 | tf_op jit(solution)/shard_map/reduce_scatter | solution.py:132
  94.6 1.3 collective-permute-start.1
  133.8 11.2 %collective-permute-start.2 = (bf16[272,7680]{1,0:T(8,128)(2,1)}, bf16[272,7680]{1,0:T(8,128)(2,1)}, u32[]{:S(2)}, u32[]{:S(2)}) collective-permute-start(bf16[272,7680]{1,0:T(8,128)(2,1)} %all-gather.2.cloned.1.call-done), channel_id=1, source_target_pairs={{0,4},{4,0},{1,5},{5,1},{2,6},{6,2},{3,7},{7,3},{8,12},{12,8},{9,1... | collective-permute-start | bytes 12533768 | tf_op jit(solution)/shard_map/ppermute | solution.py:106
  133.8 6.0 %collective-permute-start.3 = (bf16[64,384]{1,0:T(8,128)(2,1)S(1)}, bf16[64,384]{1,0:T(8,128)(2,1)S(1)}, u32[]{:S(2)}, u32[]{:S(2)}) collective-permute-start(bf16[64,384]{1,0:T(8,128)(2,1)S(1)} %get-tuple-element.27), channel_id=1, source_target_pairs={{0,4},{4,0},{1,5},{5,1},{2,6},{6,2},{3,7},{7,3},{8,12},{12,8},{9,1... | collective-permute-start | bytes 147464 | tf_op jit(solution)/shard_map/ppermute | solution.py:107
  146.9 3.7 %copy-start = (bf16[272,7680]{1,0:T(8,128)(2,1)S(1)}, bf16[272,7680]{1,0:T(8,128)(2,1)}, u32[]{:S(2)}) copy-start(bf16[272,7680]{1,0:T(8,128)(2,1)} %all-gather.2.cloned.1.call-done) | copy-start | bytes 12533764
  272.6 2.6 collective-permute-start.4
Sparse Core Ops, SparseCore 0:
  72.2 43.5 all-gather.1
  169.2 101.8 reduce-scatter.1

commit v10 on v9

--- a/solution.py
+++ b/solution.py
@@ -95,32 +95,37 @@
     )
     design_bf, basis, right_part = eliminate(whitener, got_design, got_params, got_obs, scale)
     swap = [(0, 1), (1, 0)]
-    right_hand = lax.psum(right_part + lax.ppermute(right_part, "core", swap), "tmc")
     short_most = 5 * rows_dev // 8
     keep = (slot_count + short_most) // 2
     moved = lax.ppermute(design_bf[keep:], "core", swap)
     packed = design_bf[:keep].at[short_most : short_most + moved.shape[0]].add(moved)
+    packed, right_part = lax.optimization_barrier((packed, right_part))
     gathered = lax.all_gather(packed, "panel", axis=1, tiled=True)
+    right_hand = lax.psum(right_part + lax.ppermute(right_part, "core", swap), "tmc")
     gathered, right_hand = lax.optimization_barrier((gathered, right_hand))
     half = panel_width // core_count
     got_rows = lax.ppermute(gathered, "core", swap)
     got_basis = lax.ppermute(basis, "core", swap)
     moved_count = slot_count - keep
 
-    def arc_terms(own_basis, home, away):
-        own_basis = own_basis.astype(jnp.bfloat16)
-        upper = jnp.dot(own_basis[:, :keep], home, preferred_element_type=jnp.float32)
-        lower = jnp.dot(
-            own_basis[:, keep:],
-            away[short_most : short_most + moved_count],
-            preferred_element_type=jnp.float32,
-        )
-        return (upper + lower).astype(jnp.bfloat16)
+    def spread(own_basis):
+        lead = own_basis[:, :keep]
+        tail = jnp.pad(own_basis[:, keep:], ((0, 0), (short_most, keep - short_most - moved_count)))
+        return lead, tail
 
-    terms = jnp.concatenate(
-        [arc_terms(basis, gathered, got_rows), arc_terms(got_basis, got_rows, gathered)], axis=0
+    own_lead, own_tail = spread(basis)
+    far_lead, far_tail = spread(got_basis)
+    stacked_basis = jnp.concatenate(
+        [
+            jnp.concatenate([own_lead, own_tail], axis=1),
+            jnp.concatenate([far_tail, far_lead], axis=1),
+        ],
+        axis=0,
+    ).astype(jnp.bfloat16)
+    design_side = jnp.concatenate([gathered, got_rows], axis=0)
+    terms = jnp.dot(stacked_basis, design_side, preferred_element_type=jnp.float32).astype(
+        jnp.bfloat16
     )
-    design_side = jnp.concatenate([gathered, got_rows], axis=0)
     row_side = jnp.concatenate([design_side, -terms], axis=0)
     col_side = lax.dynamic_slice_in_dim(
         jnp.concatenate([design_side, terms], axis=0),

time: 286 us -> 280 us (0.979)
  matrix products: 41.4 us -> 35.8 us
  starting transfers between devices: 13.9 us -> 17.3 us
    all_to_all x1, waiting for transfers between devices: 22.4 us -> 13.2 us  [body(): lax.all_to_all(send_design, TM, split_axis=0, concat_axis=0, tiled=True)]
    reduce_scatter x1, waiting for transfers between devices: 102 us -> 108 us  [body(): lax.psum_scatter((product * scale).astype(jnp.bfloat16), 'tmc', scatter_d...]
    dot_general x4 -> x1, matrix products: 10.5 us -> 5.31 us  [body(): jnp.dot(stacked_basis, design_side, preferred_element_type=jnp.float32)]
    all_gather x1, waiting for transfers between devices: 0.01 us -> 4.07 us  [body(): gathered = lax.all_gather(packed, 'panel', axis=1, tiled=True)]
  transfers between devices with their start and end apart: 9 -> 9, of which waited for: 7 -> 7; matrix products, arithmetic and copies ran while one was open for 13% -> 9% of each run, Pallas kernels for 0% -> 0%
where the time goes in v10:
time: 280 us; the launch traced here: 278 us
  waiting for transfers between devices  136 us (49%)
  blocking collectives  38 us (14%)
  matrix products  35.8 us (13%)
  other arithmetic  21.9 us (8%)
  starting transfers between devices  17.3 us (6%)
  between operations  16.4 us (6%)
  local copies, waits for them, and re-layouts  13.3 us (5%)
    reduce_scatter x1, waiting for transfers between devices, body(): lax.psum_scatter((product * scale).astype(jnp.bfloat16), 'tmc', scatter_d...  108 us
    psum x1, blocking collectives, body(): lax.psum(right_part + lax.ppermute(right_part, 'core', swap), 'tmc')  38 us
    dot_general x1, matrix products, body(): lax.dot_general(row_side, col_side, (((0,), (0,)), ((), ())), preferred_e...  18.1 us
    all_to_all x1, waiting for transfers between devices, body(): lax.all_to_all(send_design, TM, split_axis=0, concat_axis=0, tiled=True)  13.2 us
    all_to_all x1, starting transfers between devices, body(): lax.all_to_all(send_params, TM, split_axis=0, concat_axis=0, tiled=True)  8.16 us
    all_to_all x1, starting transfers between devices, body(): lax.all_to_all(send_design, TM, split_axis=0, concat_axis=0, tiled=True)  7.39 us
    another operation x3, other arithmetic, eliminate(): factor = jnp.linalg.cholesky(param_gram)  6.52 us
  transfers between devices with their start and end apart: 9, of which 7 were waited for; matrix products, arithmetic and copies ran while one was open for 9% of the time, Pallas kernels for 0%

profile of v10, /device:TPU:24, one launch (start us, length us, event | category | flops | bytes accessed | tf_op | source)
XLA Modules:
  0.0 278.3 jit_solution(9605522035914984274)
XLA Ops:
  7.2 0.5 broadcast.223
  7.7 2.2 fusion.61
  10.0 0.2 dynamic-slice_reduce_fusion
  10.2 0.6 reduce-window.6
  10.8 0.2 slice_reduce_fusion.1
  11.0 0.1 fusion.65
  11.1 0.1 copy.11
  11.3 0.2 fusion.56
  11.5 1.4 scatter_custom_fusion
  12.9 0.1 broadcast_in_dim.53
  13.0 0.8 broadcast_in_dim.60
  13.8 0.9 copy.12
  14.7 0.1 fusion.59
  14.8 1.4 gather_fusion.1
  16.3 0.1 broadcast_select_fusion.1
  16.4 0.8 reshape.207
  17.2 8.2 %all-to-all-start = ((bf16[32,2,390]{2,1,0:T(2,128)(2,1)}), bf16[32,2,390]{2,1,0:T(2,128)(2,1)S(1)}, u32[]{:S(2)}, u32[]{:S(2)}) async-start(bf16[32,2,390]{2,1,0:T(2,128)(2,1)} %reshape.207), calls=%async_computation | async-start | bytes 131072 | tf_op jit(solution)/shard_map/all_to_all | solution.py:77
  25.4 0.2 concatenate.40
  25.7 2.5 gather_fusion
  28.2 0.4 gather.13
  28.6 1.6 broadcast_select_fusion
  30.2 0.6 and_select_fusion
  31.0 0.7 iota_compare_fusion.11
  31.6 0.6 dynamic_slice.20
  32.2 0.6 dynamic_slice.19
  34.8 0.1 lt.84
  34.9 0.1 add.136
  35.0 0.2 reshape.208
  35.3 0.7 fusion.36
  35.9 0.2 fusion.104
  36.3 7.4 %all-to-all-start.1 = ((bf16[32,12,1920]{2,1,0:T(8,128)(2,1)}), bf16[32,12,1920]{2,1,0:T(8,128)(2,1)S(1)}, u32[]{:S(2)}, u32[]{:S(2)}) async-start(bf16[32,12,1920]{2,1,0:T(8,128)(2,1)} %broadcast_select_fusion), calls=%async_computation.1 | async-start | bytes 3932160 | tf_op jit(solution)/shard_map/all_to_all | solution.py:79
  43.7 0.2 all-gather.2.cloned.1.call-start
  43.9 5.8 %cholesky.17 = f32[64,64]{1,0:T(8,128)S(1)} custom-call(f32[64,64]{1,0:T(8,128)S(1)} %fusion.69), custom_call_target="Cholesky" | custom-call | tf_op jit(solution)/shard_map/jit(cholesky)/cholesky | solution.py:32
  49.8 0.6 compare_reduce_fusion
  50.4 0.7 fusion.60
  51.1 4.9 %custom-call.6 = f32[1,64,64]{1,2,0:T(8,128)S(1)} custom-call(f32[1,64,64]{2,1,0:T(8,128)S(1)} %fusion.60), custom_call_target="InvertDiagBlocksLowerTriangular" | custom-call | tf_op jit(solution)/shard_map/triangular_solve | solution.py:33
  56.0 0.2 slice_reduce_fusion
  56.2 0.7 convolution_bitcast_fusion
  56.9 0.9 fusion.101
  57.8 0.2 convolution_bitcast_fusion.1
  58.0 13.2 %all-to-all-done.1 = bf16[32,12,1920]{2,1,0:T(8,128)(2,1)S(1)} async-done(((bf16[32,12,1920]{2,1,0:T(8,128)(2,1)}), bf16[32,12,1920]{2,1,0:T(8,128)(2,1)S(1)}, u32[]{:S(2)}, u32[]{:S(2)}) %all-to-all-start.1) | async-done | bytes 1474592 | tf_op jit(solution)/shard_map/all_to_all | solution.py:79
  71.1 0.4 reshape.146
  71.5 2.0 fusion.102
  73.7 5.0 %fusion.105 = f32[1920,64]{1,0:T(8,128)S(1)} fusion(f32[384,1920]{1,0:T(8,128)S(1)} %get-tuple-element.34, f32[64,384]{1,0:T(8,128)S(1)} %get-tuple-element.35), kind=kOutput, calls=%fused_computation.150 | convolution fusion | flops 566231040 | bytes 3538944 | tf_op jit(solution)/shard_map/dot_general | solution.py:34
  78.6 0.1 collective-permute-start
  78.7 1.0 convolution_reduce_fusion
  79.8 1.7 fusion.11
  81.5 0.1 fusion.29
  81.6 1.0 copy-done
  82.6 0.8 collective-permute-start.1
  83.4 0.8 collective-permute-done.1
  84.3 38.0 %psum.7 = f32[1920]{0:T(1024)} all-reduce(f32[1920]{0:T(1024)S(1)} %add.151), channel_id=1, replica_groups=mesh['tmc'=16,'core'=2,'panel'=4] {'tmc'}, use_global_device_ids=true, to_apply=%region_9.10 | all-reduce | flops 1920 | bytes 15360 | tf_op jit(solution)/shard_map/psum | solution.py:104
  122.3 4.1 %all-gather.2.cloned.1.call-done = bf16[272,7680]{1,0:T(8,128)(2,1)} async-done(((bf16[272,1920]{1,0:T(8,128)(2,1)}), bf16[272,7680]{1,0:T(8,128)(2,1)}) %all-gather.2.cloned.1.call-update) | async-done | bytes 4177936 | tf_op jit(solution)/shard_map/all_gather | solution.py:103
  126.4 0.5 collective-permute-start.3
  126.9 5.4 %collective-permute-done.3 = bf16[64,384]{1,0:T(8,128)(2,1)S(1)} collective-permute-done((bf16[64,384]{1,0:T(8,128)(2,1)S(1)}, bf16[64,384]{1,0:T(8,128)(2,1)S(1)}, u32[]{:S(2)}, u32[]{:S(2)}) %collective-permute-start.3) | collective-permute-done | bytes 49184 | tf_op jit(solution)/shard_map/ppermute | solution.py:108
  132.5 1.4 collective-permute-done.2
  133.9 5.3 %fusion.103 = (bf16[128,7680]{1,0:T(8,128)(2,1)S(1)}, bf16[128,7680]{1,0:T(8,128)(2,1)S(1)}) fusion(bf16[272,7680]{1,0:T(8,128)(2,1)} %collective-permute-done.2, bf16[272,7680]{1,0:T(8,128)(2,1)} %all-gather.2.cloned.1.call-done, bf16[64,112]{1,0:T(8,128)(2,1)S(1)} %slice.87, bf16[64,112]{1,0:T(8,128)(2,1)S(1)} %slice.86, ...), kind=kOutput, calls=%fused_computation.148 | convolution fusion | flops 1089478656 | bytes 12386304 | tf_op jit(solution)/shard_map/dot_general | solution.py:126
  139.2 18.1 %multiply_convert_fusion = bf16[7680,960]{1,0:T(8,128)(2,1)} fusion(bf16[272,7680]{1,0:T(8,128)(2,1)} %collective-permute-done.2, bf16[272,7680]{1,0:T(8,128)(2,1)S(1)} %copy-done.4, bf16[128,7680]{1,0:T(8,128)(2,1)S(1)} %get-tuple-element.36, s32[]{:T(128)S(6)} %select_n.84, bf16[128,7680]{1,0:T(8,128)(2,1)S(1)} %get-tuple-element.37), kind=kOutput, calls=%fused_computation.3 | convolution fusion | flops 9958625280 | bytes 35389444 | tf_op jit(solution)/shard_map/dot_general | solution.py:134
  157.4 108.0 %reduce-scatter.2.cloned.1.call-done = bf16[480,960]{1,0:T(8,128)(2,1)} async-done(((bf16[7680,960]{1,0:T(8,128)(2,1)}), bf16[480,960]{1,0:T(8,128)(2,1)}) %reduce-scatter.2.cloned.1.call-update) | async-done | bytes 921616 | tf_op jit(solution)/shard_map/reduce_scatter | solution.py:137
  265.4 1.4 convert.21
  266.9 0.1 dynamic-slice_bitcast_fusion.1
  267.0 0.1 collective-permute-start.4
  267.1 2.5 collective-permute-done.4
  269.6 1.8 maximum_select_fusion
  (43 shorter events, 0.9 us)
Async XLA Ops:
  7.2 18.3 %copy-start.1 = (bf16[256,1920]{1,0:T(8,128)(2,1)S(1)}, bf16[256,1920]{1,0:T(8,128)(2,1)}, u32[]{:S(2)}) copy-start(bf16[256,1920]{1,0:T(8,128)(2,1)} %param.8) | copy-start | bytes 2949124
  17.2 17.8 %all-to-all-start = ((bf16[32,2,390]{2,1,0:T(2,128)(2,1)}), bf16[32,2,390]{2,1,0:T(2,128)(2,1)S(1)}, u32[]{:S(2)}, u32[]{:S(2)}) async-start(bf16[32,2,390]{2,1,0:T(2,128)(2,1)} %reshape.207), calls=%async_computation | async-start | bytes 131072 | tf_op jit(solution)/shard_map/all_to_all | solution.py:77
  28.2 3.4 %copy-start.5 = (f32[32]{0:T(128)S(1)}, f32[32]{0:T(128)}, u32[]{:S(2)}) copy-start(f32[32]{0:T(128)} %param.13) | copy-start | bytes 388
  28.2 4.0 %copy-start.6 = (f32[32]{0:T(128)S(1)}, f32[32]{0:T(128)}, u32[]{:S(2)}) copy-start(f32[32]{0:T(128)} %param.12) | copy-start | bytes 388
  31.6 24.6 %copy-start.3 = (pred[384]{0:T(512)(128)(4,1)}, pred[384]{0:T(512)(128)(4,1)S(1)}, u32[]{:S(2)}) copy-start(pred[384]{0:T(512)(128)(4,1)S(1)} %iota_compare_fusion.11) | copy-start | bytes 1156
  36.3 34.9 %all-to-all-start.1 = ((bf16[32,12,1920]{2,1,0:T(8,128)(2,1)}), bf16[32,12,1920]{2,1,0:T(8,128)(2,1)S(1)}, u32[]{:S(2)}, u32[]{:S(2)}) async-start(bf16[32,12,1920]{2,1,0:T(8,128)(2,1)} %broadcast_select_fusion), calls=%async_computation.1 | async-start | bytes 3932160 | tf_op jit(solution)/shard_map/all_to_all | solution.py:79
  43.7 82.7 %all-gather.2.cloned.1.call-start = ((), (), s32[]{:S(2)}) async-start(), calls=%async_computation.3 | async-start | bytes 5222400 | tf_op jit(solution)/shard_map/all_gather | solution.py:103
  78.6 47.7 %copy-start.2 = (bf16[64,384]{1,0:T(8,128)(2,1)S(1)}, bf16[64,384]{1,0:T(8,128)(2,1)}, u32[]{:S(2)}) copy-start(bf16[64,384]{1,0:T(8,128)(2,1)} %get-tuple-element.31) | copy-start | bytes 147460
  78.6 2.8 %collective-permute-start = (bf16[112,1920]{1,0:T(8,128)(2,1)S(1)}, bf16[112,1920]{1,0:T(8,128)(2,1)S(1)}, u32[]{:S(2)}, u32[]{:S(2)}) collective-permute-start(bf16[112,1920]{1,0:T(8,128)(2,1)S(1)} %slice.82), channel_id=1, source_target_pairs={{0,4},{4,0},{1,5},{5,1},{2,6},{6,2},{3,7},{7,3},{8,12},{12,8},{9,1... | collective-permute-start | bytes 1290248 | tf_op jit(solution)/shard_map/ppermute | solution.py:100
  81.6 1.0 copy-start
  82.6 182.8 %reduce-scatter.2.cloned.1.call-start = ((), (), s32[]{:S(2)}) async-start(), calls=%async_computation.4 | async-start | bytes 16711680 | tf_op jit(solution)/shard_map/reduce_scatter | solution.py:137
  82.6 1.6 collective-permute-start.1
  126.4 7.5 %collective-permute-start.2 = (bf16[272,7680]{1,0:T(8,128)(2,1)}, bf16[272,7680]{1,0:T(8,128)(2,1)}, u32[]{:S(2)}, u32[]{:S(2)}) collective-permute-start(bf16[272,7680]{1,0:T(8,128)(2,1)} %all-gather.2.cloned.1.call-done), channel_id=1, source_target_pairs={{0,4},{4,0},{1,5},{5,1},{2,6},{6,2},{3,7},{7,3},{8,12},{12,8},{9,1... | collective-permute-start | bytes 12533768 | tf_op jit(solution)/shard_map/ppermute | solution.py:107
  126.4 6.0 %collective-permute-start.3 = (bf16[64,384]{1,0:T(8,128)(2,1)S(1)}, bf16[64,384]{1,0:T(8,128)(2,1)S(1)}, u32[]{:S(2)}, u32[]{:S(2)}) collective-permute-start(bf16[64,384]{1,0:T(8,128)(2,1)S(1)} %copy-done.2), channel_id=1, source_target_pairs={{0,4},{4,0},{1,5},{5,1},{2,6},{6,2},{3,7},{7,3},{8,12},{12,8},{9,1... | collective-permute-start | bytes 147464 | tf_op jit(solution)/shard_map/ppermute | solution.py:108
  133.9 5.3 %copy-start.4 = (bf16[272,7680]{1,0:T(8,128)(2,1)S(1)}, bf16[272,7680]{1,0:T(8,128)(2,1)}, u32[]{:S(2)}) copy-start(bf16[272,7680]{1,0:T(8,128)(2,1)} %all-gather.2.cloned.1.call-done) | copy-start | bytes 12533764
  267.0 2.6 collective-permute-start.4
Sparse Core Ops, SparseCore 0:
  82.7 43.6 all-gather.1
  157.5 107.8 reduce-scatter.1

commit v11 on v10

--- a/solution.py
+++ b/solution.py
@@ -99,13 +99,13 @@
     keep = (slot_count + short_most) // 2
     moved = lax.ppermute(design_bf[keep:], "core", swap)
     packed = design_bf[:keep].at[short_most : short_most + moved.shape[0]].add(moved)
-    packed, right_part = lax.optimization_barrier((packed, right_part))
+    got_basis = lax.ppermute(basis, "core", swap)
+    packed, right_part, got_basis = lax.optimization_barrier((packed, right_part, got_basis))
     gathered = lax.all_gather(packed, "panel", axis=1, tiled=True)
     right_hand = lax.psum(right_part + lax.ppermute(right_part, "core", swap), "tmc")
     gathered, right_hand = lax.optimization_barrier((gathered, right_hand))
     half = panel_width // core_count
     got_rows = lax.ppermute(gathered, "core", swap)
-    got_basis = lax.ppermute(basis, "core", swap)
     moved_count = slot_count - keep
 
     def spread(own_basis):

time: 280 us -> 280 us (level)
    ppermute x1, waiting for transfers between devices: 5.45 us -> 0.01 us  [body(): got_basis = lax.ppermute(basis, 'core', swap)]
    ppermute x1, waiting for transfers between devices: 1.44 us -> 5.89 us  [body(): got_rows = lax.ppermute(gathered, 'core', swap)]
  transfers between devices with their start and end apart: 9 -> 9, of which waited for: 7 -> 6; matrix products, arithmetic and copies ran while one was open for 9% -> 12% of each run, Pallas kernels for 0% -> 0%
where the time goes in v11:
time: 280 us; the launch traced here: 278 us
  waiting for transfers between devices  135 us (48%)
  blocking collectives  38 us (14%)
  matrix products  35.8 us (13%)
  other arithmetic  21.9 us (8%)
  starting transfers between devices  16.7 us (6%)
  between operations  16.4 us (6%)
  local copies, waits for them, and re-layouts  14.7 us (5%)
    reduce_scatter x1, waiting for transfers between devices, body(): lax.psum_scatter((product * scale).astype(jnp.bfloat16), 'tmc', scatter_d...  108 us
    psum x1, blocking collectives, body(): lax.psum(right_part + lax.ppermute(right_part, 'core', swap), 'tmc')  38 us
    dot_general x1, matrix products, body(): lax.dot_general(row_side, col_side, (((0,), (0,)), ((), ())), preferred_e...  18.1 us
    all_to_all x1, waiting for transfers between devices, body(): lax.all_to_all(send_design, TM, split_axis=0, concat_axis=0, tiled=True)  13.1 us
    all_to_all x1, starting transfers between devices, body(): lax.all_to_all(send_params, TM, split_axis=0, concat_axis=0, tiled=True)  8.16 us
    all_to_all x1, starting transfers between devices, body(): lax.all_to_all(send_design, TM, split_axis=0, concat_axis=0, tiled=True)  7.39 us
    another operation x3, other arithmetic, eliminate(): factor = jnp.linalg.cholesky(param_gram)  6.52 us
    ppermute x1, waiting for transfers between devices, body(): got_rows = lax.ppermute(gathered, 'core', swap)  5.89 us
  transfers between devices with their start and end apart: 9, of which 6 were waited for; matrix products, arithmetic and copies ran while one was open for 12% of the time, Pallas kernels for 0%

profile of v11, /device:TPU:24, one launch (start us, length us, event | category | flops | bytes accessed | tf_op | source)
XLA Modules:
  0.0 278.2 jit_solution(12463256219009741785)
XLA Ops:
  7.2 0.5 broadcast.223
  7.7 2.2 fusion.61
  10.0 0.2 dynamic-slice_reduce_fusion
  10.2 0.6 reduce-window.6
  10.8 0.2 slice_reduce_fusion.1
  11.0 0.1 fusion.65
  11.1 0.1 copy.11
  11.3 0.2 fusion.56
  11.5 1.4 scatter_custom_fusion
  12.9 0.1 broadcast_in_dim.53
  13.0 0.8 broadcast_in_dim.60
  13.8 0.9 copy.12
  14.7 0.1 fusion.59
  14.8 1.4 gather_fusion.1
  16.3 0.1 broadcast_select_fusion.1
  16.4 0.8 reshape.207
  17.2 8.2 %all-to-all-start = ((bf16[32,2,390]{2,1,0:T(2,128)(2,1)}), bf16[32,2,390]{2,1,0:T(2,128)(2,1)S(1)}, u32[]{:S(2)}, u32[]{:S(2)}) async-start(bf16[32,2,390]{2,1,0:T(2,128)(2,1)} %reshape.207), calls=%async_computation | async-start | bytes 131072 | tf_op jit(solution)/shard_map/all_to_all | solution.py:77
  25.4 0.2 concatenate.40
  25.7 2.5 gather_fusion
  28.2 0.4 gather.13
  28.6 1.6 broadcast_select_fusion
  30.2 0.6 and_select_fusion
  31.0 0.7 iota_compare_fusion.11
  31.6 0.6 dynamic_slice.20
  32.2 0.6 dynamic_slice.19
  34.8 0.1 lt.84
  34.9 0.1 add.136
  35.0 0.2 reshape.208
  35.3 0.7 fusion.36
  35.9 0.2 fusion.104
  36.3 7.4 %all-to-all-start.1 = ((bf16[32,12,1920]{2,1,0:T(8,128)(2,1)}), bf16[32,12,1920]{2,1,0:T(8,128)(2,1)S(1)}, u32[]{:S(2)}, u32[]{:S(2)}) async-start(bf16[32,12,1920]{2,1,0:T(8,128)(2,1)} %broadcast_select_fusion), calls=%async_computation.1 | async-start | bytes 3932160 | tf_op jit(solution)/shard_map/all_to_all | solution.py:79
  43.7 5.8 %cholesky.17 = f32[64,64]{1,0:T(8,128)S(1)} custom-call(f32[64,64]{1,0:T(8,128)S(1)} %fusion.69), custom_call_target="Cholesky" | custom-call | tf_op jit(solution)/shard_map/jit(cholesky)/cholesky | solution.py:32
  49.6 0.6 compare_reduce_fusion
  50.3 0.7 fusion.60
  50.9 4.9 %custom-call.6 = f32[1,64,64]{1,2,0:T(8,128)S(1)} custom-call(f32[1,64,64]{2,1,0:T(8,128)S(1)} %fusion.60), custom_call_target="InvertDiagBlocksLowerTriangular" | custom-call | tf_op jit(solution)/shard_map/triangular_solve | solution.py:33
  55.8 0.2 slice_reduce_fusion
  56.0 0.9 fusion.101
  56.9 0.3 collective-permute-start.1
  57.2 0.6 convolution_bitcast_fusion
  57.8 0.2 convolution_bitcast_fusion.1
  58.0 13.1 %all-to-all-done.1 = bf16[32,12,1920]{2,1,0:T(8,128)(2,1)S(1)} async-done(((bf16[32,12,1920]{2,1,0:T(8,128)(2,1)}), bf16[32,12,1920]{2,1,0:T(8,128)(2,1)S(1)}, u32[]{:S(2)}, u32[]{:S(2)}) %all-to-all-start.1) | async-done | bytes 1474592 | tf_op jit(solution)/shard_map/all_to_all | solution.py:79
  71.1 0.4 reshape.146
  71.5 2.0 fusion.102
  73.7 5.0 %fusion.105 = f32[1920,64]{1,0:T(8,128)S(1)} fusion(f32[384,1920]{1,0:T(8,128)S(1)} %get-tuple-element.36, f32[64,384]{1,0:T(8,128)S(1)} %get-tuple-element.37), kind=kOutput, calls=%fused_computation.150 | convolution fusion | flops 566231040 | bytes 3538944 | tf_op jit(solution)/shard_map/dot_general | solution.py:34
  78.6 0.1 collective-permute-start
  78.7 1.0 convolution_reduce_fusion
  79.8 1.7 fusion.11
  81.4 0.1 fusion.29
  81.6 0.9 copy-done
  82.6 0.6 collective-permute-start.2
  83.2 0.8 collective-permute-done.2
  84.0 38.0 %psum.7 = f32[1920]{0:T(1024)} all-reduce(f32[1920]{0:T(1024)S(1)} %add.151), channel_id=1, replica_groups=mesh['tmc'=16,'core'=2,'panel'=4] {'tmc'}, use_global_device_ids=true, to_apply=%region_9.10 | all-reduce | flops 1920 | bytes 15360 | tf_op jit(solution)/shard_map/psum | solution.py:105
  122.1 4.3 %all-gather.2.cloned.1.call-done = bf16[272,7680]{1,0:T(8,128)(2,1)} async-done(((bf16[272,1920]{1,0:T(8,128)(2,1)}), bf16[272,7680]{1,0:T(8,128)(2,1)}) %all-gather.2.cloned.1.call-update) | async-done | bytes 4177936 | tf_op jit(solution)/shard_map/all_gather | solution.py:104
  126.3 0.8 slice.86
  127.1 0.8 slice.87
  127.9 5.9 %collective-permute-done.3 = bf16[272,7680]{1,0:T(8,128)(2,1)} collective-permute-done((bf16[272,7680]{1,0:T(8,128)(2,1)}, bf16[272,7680]{1,0:T(8,128)(2,1)}, u32[]{:S(2)}, u32[]{:S(2)}) %collective-permute-start.3) | collective-permute-done | bytes 4177952 | tf_op jit(solution)/shard_map/ppermute | solution.py:108
  133.8 5.4 %fusion.103 = (bf16[128,7680]{1,0:T(8,128)(2,1)S(1)}, bf16[128,7680]{1,0:T(8,128)(2,1)S(1)}) fusion(bf16[272,7680]{1,0:T(8,128)(2,1)} %collective-permute-done.3, bf16[272,7680]{1,0:T(8,128)(2,1)} %all-gather.2.cloned.1.call-done, bf16[64,112]{1,0:T(8,128)(2,1)S(1)} %slice.87, bf16[64,112]{1,0:T(8,128)(2,1)S(1)} %slice.86, bf16[64,272]{1,0:T(8,128)(2,1)} %bitcast.65, ...), kind=kOutput, calls=%fused_computation.148 | convolution fusion | flops 1089478656 | bytes 12386304 | tf_op jit(solution)/shard_map/dot_general | solution.py:126
  139.2 18.1 %multiply_convert_fusion = bf16[7680,960]{1,0:T(8,128)(2,1)} fusion(bf16[272,7680]{1,0:T(8,128)(2,1)} %collective-permute-done.3, bf16[272,7680]{1,0:T(8,128)(2,1)S(1)} %copy-done.3, bf16[128,7680]{1,0:T(8,128)(2,1)S(1)} %get-tuple-element.38, s32[]{:T(128)S(6)} %select_n.84, bf16[128,7680]{1,0:T(8,128)(2,1)S(1)} %get-tuple-element.39), kind=kOutput, calls=%fused_computation.3 | convolution fusion | flops 9958625280 | bytes 35389444 | tf_op jit(solution)/shard_map/dot_general | solution.py:134
  157.4 108.0 %reduce-scatter.2.cloned.1.call-done = bf16[480,960]{1,0:T(8,128)(2,1)} async-done(((bf16[7680,960]{1,0:T(8,128)(2,1)}), bf16[480,960]{1,0:T(8,128)(2,1)}) %reduce-scatter.2.cloned.1.call-update) | async-done | bytes 921616 | tf_op jit(solution)/shard_map/reduce_scatter | solution.py:137
  265.3 1.4 convert.21
  266.8 0.1 dynamic-slice_bitcast_fusion.1
  266.9 0.1 collective-permute-start.4
  267.0 2.5 collective-permute-done.4
  269.6 1.8 maximum_select_fusion
  (41 shorter events, 0.8 us)
Async XLA Ops:
  7.2 18.3 %copy-start.1 = (bf16[256,1920]{1,0:T(8,128)(2,1)S(1)}, bf16[256,1920]{1,0:T(8,128)(2,1)}, u32[]{:S(2)}) copy-start(bf16[256,1920]{1,0:T(8,128)(2,1)} %param.8) | copy-start | bytes 2949124
  17.2 17.8 %all-to-all-start = ((bf16[32,2,390]{2,1,0:T(2,128)(2,1)}), bf16[32,2,390]{2,1,0:T(2,128)(2,1)S(1)}, u32[]{:S(2)}, u32[]{:S(2)}) async-start(bf16[32,2,390]{2,1,0:T(2,128)(2,1)} %reshape.207), calls=%async_computation | async-start | bytes 131072 | tf_op jit(solution)/shard_map/all_to_all | solution.py:77
  28.2 3.4 %copy-start.4 = (f32[32]{0:T(128)S(1)}, f32[32]{0:T(128)}, u32[]{:S(2)}) copy-start(f32[32]{0:T(128)} %param.13) | copy-start | bytes 388
  28.2 4.0 %copy-start.5 = (f32[32]{0:T(128)S(1)}, f32[32]{0:T(128)}, u32[]{:S(2)}) copy-start(f32[32]{0:T(128)} %param.12) | copy-start | bytes 388
  31.6 26.4 %copy-start.2 = (pred[384]{0:T(512)(128)(4,1)}, pred[384]{0:T(512)(128)(4,1)S(1)}, u32[]{:S(2)}) copy-start(pred[384]{0:T(512)(128)(4,1)S(1)} %iota_compare_fusion.11) | copy-start | bytes 1156
  36.3 34.9 %all-to-all-start.1 = ((bf16[32,12,1920]{2,1,0:T(8,128)(2,1)}), bf16[32,12,1920]{2,1,0:T(8,128)(2,1)S(1)}, u32[]{:S(2)}, u32[]{:S(2)}) async-start(bf16[32,12,1920]{2,1,0:T(8,128)(2,1)} %broadcast_select_fusion), calls=%async_computation.1 | async-start | bytes 3932160 | tf_op jit(solution)/shard_map/all_to_all | solution.py:79
  43.7 82.7 %all-gather.2.cloned.1.call-start = ((), (), s32[]{:S(2)}) async-start(), calls=%async_computation.3 | async-start | bytes 5222400 | tf_op jit(solution)/shard_map/all_gather | solution.py:104
  56.9 24.7 %collective-permute-start.1 = (bf16[64,384]{1,0:T(8,128)(2,1)}, bf16[64,384]{1,0:T(8,128)(2,1)}, u32[]{:S(2)}, u32[]{:S(2)}) collective-permute-start(bf16[64,384]{1,0:T(8,128)(2,1)} %get-tuple-element.34), channel_id=1, source_target_pairs={{0,4},{4,0},{1,5},{5,1},{2,6},{6,2},{3,7},{7,3},{8,12},{12,8},{9,1... | collective-permute-start | bytes 147464 | tf_op jit(solution)/shard_map/ppermute | solution.py:102
  78.6 2.8 %collective-permute-start = (bf16[112,1920]{1,0:T(8,128)(2,1)S(1)}, bf16[112,1920]{1,0:T(8,128)(2,1)S(1)}, u32[]{:S(2)}, u32[]{:S(2)}) collective-permute-start(bf16[112,1920]{1,0:T(8,128)(2,1)S(1)} %slice.82), channel_id=1, source_target_pairs={{0,4},{4,0},{1,5},{5,1},{2,6},{6,2},{3,7},{7,3},{8,12},{12,8},{9,1... | collective-permute-start | bytes 1290248 | tf_op jit(solution)/shard_map/ppermute | solution.py:100
  81.6 1.0 copy-start
  82.6 182.8 %reduce-scatter.2.cloned.1.call-start = ((), (), s32[]{:S(2)}) async-start(), calls=%async_computation.4 | async-start | bytes 16711680 | tf_op jit(solution)/shard_map/reduce_scatter | solution.py:137
  82.6 1.4 collective-permute-start.2
  126.3 7.5 %collective-permute-start.3 = (bf16[272,7680]{1,0:T(8,128)(2,1)}, bf16[272,7680]{1,0:T(8,128)(2,1)}, u32[]{:S(2)}, u32[]{:S(2)}) collective-permute-start(bf16[272,7680]{1,0:T(8,128)(2,1)} %all-gather.2.cloned.1.call-done), channel_id=1, source_target_pairs={{0,4},{4,0},{1,5},{5,1},{2,6},{6,2},{3,7},{7,3},{8,12},{12,8},{9,1... | collective-permute-start | bytes 12533768 | tf_op jit(solution)/shard_map/ppermute | solution.py:108
  133.8 5.4 %copy-start.3 = (bf16[272,7680]{1,0:T(8,128)(2,1)S(1)}, bf16[272,7680]{1,0:T(8,128)(2,1)}, u32[]{:S(2)}) copy-start(bf16[272,7680]{1,0:T(8,128)(2,1)} %all-gather.2.cloned.1.call-done) | copy-start | bytes 12533764
  266.9 2.6 collective-permute-start.4
Sparse Core Ops, SparseCore 0:
  82.7 43.6 all-gather.1
  157.5 107.8 reduce-scatter.1

commit v12 on v11

--- a/solution.py
+++ b/solution.py
@@ -61,15 +61,13 @@
     earlier = jnp.cumsum(onehot, axis=0) - onehot
     within = jnp.sum(earlier * onehot, axis=1)
     target_slot = local_arcs * capacity + within
-    source_row = (
-        jnp.zeros((slot_count,), jnp.int32)
-        .at[target_slot]
-        .set(jnp.arange(1, rows_dev + 1, dtype=jnp.int32))
-    )
+    chooser = (
+        target_slot[None, :] == jnp.arange(slot_count, dtype=jnp.int32)[:, None]
+    ).astype(jnp.bfloat16)
 
     def pick_rows(values):
-        padded = jnp.concatenate([jnp.zeros((1,) + values.shape[1:], values.dtype), values], axis=0)
-        return jnp.take(padded, source_row, axis=0)
+        picked = jnp.dot(chooser, values, preferred_element_type=jnp.float32)
+        return picked.astype(values.dtype)
 
     send_design = pick_rows(design).reshape(tile_count, capacity, panel_width)
     with_obs = jnp.concatenate([partials, observed[:, None]], axis=1)

time: 280 us -> 274 us (0.979)
  local copies, waits for them, and re-layouts: 14.7 us -> 8.65 us
    gather x4 -> x0, local copies, waits for them, and re-layouts: 4.36 us -> none  [pick_rows(): return jnp.take(padded, source_row, axis=0)]
    dot_general x1, matrix products: 4.98 us -> 1.85 us  [eliminate(): arc_terms = jnp.dot(basis, white_design, precision=lax.Precision.HIGHEST)]
  transfers between devices with their start and end apart: 9 -> 9, of which waited for: 6 -> 7; matrix products, arithmetic and copies ran while one was open for 12% -> 10% of each run, Pallas kernels for 0% -> 0%
where the time goes in v12:
time: 274 us; the launch traced here: 272 us
  waiting for transfers between devices  137 us (50%)
  blocking collectives  38 us (14%)
  matrix products  33.7 us (12%)
  other arithmetic  21.5 us (8%)
  starting transfers between devices  16.5 us (6%)
  between operations  16.3 us (6%)
  local copies, waits for them, and re-layouts  8.65 us (3%)
    reduce_scatter x1, waiting for transfers between devices, body(): lax.psum_scatter((product * scale).astype(jnp.bfloat16), 'tmc', scatter_d...  108 us
    psum x1, blocking collectives, body(): lax.psum(right_part + lax.ppermute(right_part, 'core', swap), 'tmc')  38 us
    dot_general x1, matrix products, body(): lax.dot_general(row_side, col_side, (((0,), (0,)), ((), ())), preferred_e...  18.1 us
    all_to_all x1, waiting for transfers between devices, body(): lax.all_to_all(send_design, TM, split_axis=0, concat_axis=0, tiled=True)  13.6 us
    all_to_all x1, starting transfers between devices, body(): lax.all_to_all(send_params, TM, split_axis=0, concat_axis=0, tiled=True)  8.16 us
    ppermute x1, waiting for transfers between devices, body(): got_rows = lax.ppermute(gathered, 'core', swap)  7.32 us
    all_to_all x1, starting transfers between devices, body(): lax.all_to_all(send_design, TM, split_axis=0, concat_axis=0, tiled=True)  6.93 us
    another operation x3, other arithmetic, eliminate(): factor = jnp.linalg.cholesky(param_gram)  6.52 us
  transfers between devices with their start and end apart: 9, of which 7 were waited for; matrix products, arithmetic and copies ran while one was open for 10% of the time, Pallas kernels for 0%

profile of v12, /device:TPU:24, one launch (start us, length us, event | category | flops | bytes accessed | tf_op | source)
XLA Modules:
  0.0 271.9 jit_solution(11491113980562645863)
XLA Ops:
  7.2 0.5 broadcast.199
  7.7 2.3 fusion.62
  10.0 0.1 reshape_squeeze.3
  10.0 0.2 dynamic-slice_reduce_fusion
  10.2 0.6 reduce-window.6
  10.8 0.2 slice_reduce_fusion.1
  11.1 0.1 fusion.66
  11.2 0.7 broadcast_in_dim.12
  11.8 1.0 convolution_convert_fusion.2
  12.8 0.1 copy.13
  13.0 0.8 reshape.175
  13.8 8.2 %all-to-all-start = ((bf16[32,2,390]{2,1,0:T(2,128)(2,1)}), bf16[32,2,390]{2,1,0:T(2,128)(2,1)S(1)}, u32[]{:S(2)}, u32[]{:S(2)}) async-start(bf16[32,2,390]{2,1,0:T(2,128)(2,1)} %reshape.175), calls=%async_computation | async-start | bytes 131072 | tf_op jit(solution)/shard_map/all_to_all | solution.py:75
  22.0 0.1 convert_reduce_fusion
  22.0 0.6 convolution_convert_fusion.1
  22.6 0.1 iota_compare_fusion.12
  22.7 0.7 and_select_fusion
  23.4 0.1 broadcast_add_fusion
  23.5 0.7 iota_compare_fusion.13
  24.1 1.5 reshape.141
  25.6 0.6 dynamic_slice.20
  26.2 0.6 dynamic_slice.19
  28.8 0.1 lt.67
  28.9 0.1 add.110
  29.0 0.5 all-to-all-done
  29.5 0.2 reshape.176
  29.7 0.7 fusion.36
  30.4 0.2 fusion.104
  30.6 0.1 copy.14
  30.7 6.9 %all-to-all-start.1 = ((bf16[32,12,1920]{2,1,0:T(8,128)(2,1)}), bf16[32,12,1920]{2,1,0:T(8,128)(2,1)S(1)}, u32[]{:S(2)}, u32[]{:S(2)}) async-start(bf16[32,12,1920]{2,1,0:T(8,128)(2,1)} %reshape.141), calls=%async_computation.1 | async-start | bytes 3932160 | tf_op jit(solution)/shard_map/all_to_all | solution.py:77
  37.7 5.8 %cholesky.17 = f32[64,64]{1,0:T(8,128)S(1)} custom-call(f32[64,64]{1,0:T(8,128)S(1)} %fusion.70), custom_call_target="Cholesky" | custom-call | tf_op jit(solution)/shard_map/jit(cholesky)/cholesky | solution.py:32
  43.6 0.6 compare_reduce_fusion
  44.2 0.7 fusion.61
  44.9 4.9 %custom-call.6 = f32[1,64,64]{1,2,0:T(8,128)S(1)} custom-call(f32[1,64,64]{2,1,0:T(8,128)S(1)} %fusion.61), custom_call_target="InvertDiagBlocksLowerTriangular" | custom-call | tf_op jit(solution)/shard_map/triangular_solve | solution.py:33
  49.8 0.2 slice_reduce_fusion
  50.0 0.3 fusion.101
  50.3 0.4 collective-permute-start.1
  50.7 0.6 convolution_bitcast_fusion
  51.3 0.2 convolution_bitcast_fusion.1
  51.5 13.6 %all-to-all-done.1 = bf16[32,12,1920]{2,1,0:T(8,128)(2,1)S(1)} async-done(((bf16[32,12,1920]{2,1,0:T(8,128)(2,1)}), bf16[32,12,1920]{2,1,0:T(8,128)(2,1)S(1)}, u32[]{:S(2)}, u32[]{:S(2)}) %all-to-all-start.1) | async-done | bytes 1474592 | tf_op jit(solution)/shard_map/all_to_all | solution.py:77
  65.1 1.3 reshape.143
  66.4 2.8 %fusion.102 = (bf16[384,1920]{1,0:T(8,128)(2,1)S(1)}, f32[384,1920]{1,0:T(8,128)S(1)}) fusion(bf16[384,1920]{1,0:T(8,128)(2,1)} %reshape.143, f32[]{:T(128)} %bitcast.1, f32[]{:T(128)} %bitcast, s32[384]{0:T(512)S(1)} %add.110, pred[384]{0:T(512)(128)(4,1)S(1)} %lt.67, pred[384]{0:T(512)(128)(4,1)S(1)} %iota_compare_fusion.13), kind=kOutput, calls=%fused_computation.140 | convolution fusion | flops 570359808 | bytes 5900552 | tf_op jit(solution)/shard_map/dot_general | solution.py:25
  69.2 0.1 slice.76
  69.3 1.8 fusion.105
  71.2 0.3 collective-permute-start
  71.4 0.4 convolution_reduce_fusion
  71.8 1.7 fusion.11
  73.5 0.1 fusion.29
  73.7 0.9 copy-done.1
  74.6 0.0 reduce-scatter.2.cloned.1.call-start
  74.7 0.6 collective-permute-start.2
  75.3 0.8 collective-permute-done.2
  76.1 38.0 %psum.7 = f32[1920]{0:T(1024)} all-reduce(f32[1920]{0:T(1024)S(1)} %add.119), channel_id=1, replica_groups=mesh['tmc'=16,'core'=2,'panel'=4] {'tmc'}, use_global_device_ids=true, to_apply=%region_8.9 | all-reduce | flops 1920 | bytes 15360 | tf_op jit(solution)/shard_map/psum | solution.py:103
  114.1 4.3 %all-gather.2.cloned.1.call-done = bf16[272,7680]{1,0:T(8,128)(2,1)} async-done(((bf16[272,1920]{1,0:T(8,128)(2,1)}), bf16[272,7680]{1,0:T(8,128)(2,1)}) %all-gather.2.cloned.1.call-update) | async-done | bytes 4177936 | tf_op jit(solution)/shard_map/all_gather | solution.py:102
  118.4 0.1 slice.82
  118.5 0.1 slice.83
  118.6 7.3 %collective-permute-done.3 = bf16[272,7680]{1,0:T(8,128)(2,1)} collective-permute-done((bf16[272,7680]{1,0:T(8,128)(2,1)}, bf16[272,7680]{1,0:T(8,128)(2,1)}, u32[]{:S(2)}, u32[]{:S(2)}) %collective-permute-start.3) | collective-permute-done | bytes 4177952 | tf_op jit(solution)/shard_map/ppermute | solution.py:106
  125.9 5.3 %fusion.103 = (bf16[128,7680]{1,0:T(8,128)(2,1)S(1)}, bf16[128,7680]{1,0:T(8,128)(2,1)S(1)}) fusion(bf16[272,7680]{1,0:T(8,128)(2,1)} %collective-permute-done.3, bf16[272,7680]{1,0:T(8,128)(2,1)} %all-gather.2.cloned.1.call-done, bf16[64,112]{1,0:T(8,128)(2,1)S(1)} %slice.83, bf16[64,112]{1,0:T(8,128)(2,1)S(1)} %slice.82, ...), kind=kOutput, calls=%fused_computation.141 | convolution fusion | flops 1089478656 | bytes 12386304 | tf_op jit(solution)/shard_map/dot_general | solution.py:124
  131.2 18.1 %multiply_convert_fusion = bf16[7680,960]{1,0:T(8,128)(2,1)} fusion(bf16[272,7680]{1,0:T(8,128)(2,1)} %collective-permute-done.3, bf16[272,7680]{1,0:T(8,128)(2,1)S(1)} %copy-done.2, bf16[128,7680]{1,0:T(8,128)(2,1)S(1)} %get-tuple-element.38, s32[]{:T(128)S(6)} %select_n.59, bf16[128,7680]{1,0:T(8,128)(2,1)S(1)} %get-tuple-element.39), kind=kOutput, calls=%fused_computation | convolution fusion | flops 9958625280 | bytes 35389444 | tf_op jit(solution)/shard_map/dot_general | solution.py:132
  149.4 108.0 %reduce-scatter.2.cloned.1.call-done = bf16[480,960]{1,0:T(8,128)(2,1)} async-done(((bf16[7680,960]{1,0:T(8,128)(2,1)}), bf16[480,960]{1,0:T(8,128)(2,1)}) %reduce-scatter.2.cloned.1.call-update) | async-done | bytes 921616 | tf_op jit(solution)/shard_map/reduce_scatter | solution.py:135
  257.3 1.4 convert.21
  258.8 0.1 dynamic-slice_bitcast_fusion.1
  258.9 0.1 collective-permute-start.4
  259.0 2.7 collective-permute-done.4
  261.7 3.3 %maximum_select_fusion = f32[240,1920]{1,0:T(8,128)} fusion(f32[240,960]{1,0:T(8,128)} %collective-permute-done.4, f32[240,960]{1,0:T(8,128)S(1)} %get-tuple-element.31, pred[]{:T(512)S(6)} %eq.65), kind=kLoop, calls=%fused_computation.14 | loop fusion | flops 1382400 | bytes 3686401 | tf_op jit(solution)/shard_map/jit(_where)/select_n | solution.py:143
  (28 shorter events, 0.3 us)
Async XLA Ops:
  7.2 14.9 %copy-start = (bf16[256,1920]{1,0:T(8,128)(2,1)S(1)}, bf16[256,1920]{1,0:T(8,128)(2,1)}, u32[]{:S(2)}) copy-start(bf16[256,1920]{1,0:T(8,128)(2,1)} %param.8) | copy-start | bytes 2949124
  13.8 15.7 %all-to-all-start = ((bf16[32,2,390]{2,1,0:T(2,128)(2,1)}), bf16[32,2,390]{2,1,0:T(2,128)(2,1)S(1)}, u32[]{:S(2)}, u32[]{:S(2)}) async-start(bf16[32,2,390]{2,1,0:T(2,128)(2,1)} %reshape.175), calls=%async_computation | async-start | bytes 131072 | tf_op jit(solution)/shard_map/all_to_all | solution.py:75
  22.0 3.6 %copy-start.3 = (f32[32]{0:T(128)S(1)}, f32[32]{0:T(128)}, u32[]{:S(2)}) copy-start(f32[32]{0:T(128)} %param.13) | copy-start | bytes 388
  22.0 4.2 %copy-start.4 = (f32[32]{0:T(128)S(1)}, f32[32]{0:T(128)}, u32[]{:S(2)}) copy-start(f32[32]{0:T(128)} %param.12) | copy-start | bytes 388
  30.7 34.4 %all-to-all-start.1 = ((bf16[32,12,1920]{2,1,0:T(8,128)(2,1)}), bf16[32,12,1920]{2,1,0:T(8,128)(2,1)S(1)}, u32[]{:S(2)}, u32[]{:S(2)}) async-start(bf16[32,12,1920]{2,1,0:T(8,128)(2,1)} %reshape.141), calls=%async_computation.1 | async-start | bytes 3932160 | tf_op jit(solution)/shard_map/all_to_all | solution.py:77
  37.7 80.8 %all-gather.2.cloned.1.call-start = ((), (), s32[]{:S(2)}) async-start(), calls=%async_computation.3 | async-start | bytes 5222400 | tf_op jit(solution)/shard_map/all_gather | solution.py:102
  50.3 23.3 %collective-permute-start.1 = (bf16[64,384]{1,0:T(8,128)(2,1)S(1)}, bf16[64,384]{1,0:T(8,128)(2,1)S(1)}, u32[]{:S(2)}, u32[]{:S(2)}) collective-permute-start(bf16[64,384]{1,0:T(8,128)(2,1)S(1)} %get-tuple-element.33), channel_id=1, source_target_pairs={{0,4},{4,0},{1,5},{5,1},{2,6},{6,2},{3,7},{7,3},{8,12},{12,8},{9,1... | collective-permute-start | bytes 147464 | tf_op jit(solution)/shard_map/ppermute | solution.py:100
  71.2 2.4 collective-permute-start
  73.6 1.0 copy-start.1
  74.6 182.7 %reduce-scatter.2.cloned.1.call-start = ((), (), s32[]{:S(2)}) async-start(), calls=%async_computation.4 | async-start | bytes 16711680 | tf_op jit(solution)/shard_map/reduce_scatter | solution.py:135
  74.7 1.4 collective-permute-start.2
  118.4 7.5 %collective-permute-start.3 = (bf16[272,7680]{1,0:T(8,128)(2,1)}, bf16[272,7680]{1,0:T(8,128)(2,1)}, u32[]{:S(2)}, u32[]{:S(2)}) collective-permute-start(bf16[272,7680]{1,0:T(8,128)(2,1)} %all-gather.2.cloned.1.call-done), channel_id=1, source_target_pairs={{0,4},{4,0},{1,5},{5,1},{2,6},{6,2},{3,7},{7,3},{8,12},{12,8},{9,1... | collective-permute-start | bytes 12533768 | tf_op jit(solution)/shard_map/ppermute | solution.py:106
  125.9 5.3 %copy-start.2 = (bf16[272,7680]{1,0:T(8,128)(2,1)S(1)}, bf16[272,7680]{1,0:T(8,128)(2,1)}, u32[]{:S(2)}) copy-start(bf16[272,7680]{1,0:T(8,128)(2,1)} %all-gather.2.cloned.1.call-done) | copy-start | bytes 12533764
  258.9 2.8 %collective-permute-start.4 = (f32[240,960]{1,0:T(8,128)S(1)}, f32[240,960]{1,0:T(8,128)}, u32[]{:S(2)}, u32[]{:S(2)}) collective-permute-start(f32[240,960]{1,0:T(8,128)S(1)} %get-tuple-element.32), channel_id=1, source_target_pairs={{0,4},{4,0},{1,5},{5,1},{2,6},{6,2},{3,7},{7,3},{8,12},{12,8},{9,1... | collective-permute-start | bytes 2764808 | tf_op jit(solution)/shard_map/ppermute | solution.py:142
Sparse Core Ops, SparseCore 0:
  74.8 43.6 all-gather.1
  149.5 107.8 reduce-scatter.1

commit v13 on v12

--- a/solution.py
+++ b/solution.py
@@ -69,16 +69,13 @@
         picked = jnp.dot(chooser, values, preferred_element_type=jnp.float32)
         return picked.astype(values.dtype)
 
-    send_design = pick_rows(design).reshape(tile_count, capacity, panel_width)
-    with_obs = jnp.concatenate([partials, observed[:, None]], axis=1)
-    send_params = pick_rows(with_obs).reshape(tile_count, capacity, param_count + 1)
-    got_params = lax.all_to_all(send_params, TM, split_axis=0, concat_axis=0, tiled=True)
-    send_design, got_params = lax.optimization_barrier((send_design, got_params))
-    got_design = lax.all_to_all(send_design, TM, split_axis=0, concat_axis=0, tiled=True)
-    got_design = got_design.reshape(slot_count, panel_width)
-    got_params = got_params.reshape(slot_count, param_count + 1)
-    got_obs = got_params[:, param_count]
-    got_params = got_params[:, :param_count]
+    bundle = jnp.concatenate([design, partials, observed[:, None]], axis=1)
+    sent = pick_rows(bundle).reshape(tile_count, capacity, bundle.shape[1])
+    got = lax.all_to_all(sent, TM, split_axis=0, concat_axis=0, tiled=True)
+    got = got.reshape(slot_count, bundle.shape[1])
+    got_design = got[:, :panel_width]
+    got_params = got[:, panel_width : panel_width + param_count]
+    got_obs = got[:, panel_width + param_count]
     per_source = jnp.sum((epoch_table == device_index).astype(jnp.int32), axis=0)
     arc_start = jnp.sum((arc_ids < device_index).astype(jnp.int32))
     first_pos = jnp.mod(jnp.arange(tile_count, dtype=jnp.int32) - arc_start, tile_count)

time: 274 us -> 284 us (1.036)
  waiting for transfers between devices: 137 us -> 147 us
  starting transfers between devices: 16.5 us -> 9.4 us
  local copies, waits for them, and re-layouts: 8.65 us -> 14 us
    all_to_all x2 -> x1, waiting for transfers between devices: 14.1 us -> 24 us  [body(): got = lax.all_to_all(sent, TM, split_axis=0, concat_axis=0, tiled=True)]
    all_to_all x2 -> x1, starting transfers between devices: 15.1 us -> 8.3 us  [body(): got = lax.all_to_all(sent, TM, split_axis=0, concat_axis=0, tiled=True)]
  transfers between devices with their start and end apart: 9 -> 8, of which waited for: 7 -> 6; matrix products, arithmetic and copies ran while one was open for 10% -> 3% of each run, Pallas kernels for 0% -> 0%
where the time goes in v13:
time: 284 us; the launch traced here: 282 us
  waiting for transfers between devices  147 us (52%)
  blocking collectives  38 us (13%)
  matrix products  33.9 us (12%)
  other arithmetic  23.7 us (8%)
  between operations  16.2 us (6%)
  local copies, waits for them, and re-layouts  14 us (5%)
  starting transfers between devices  9.4 us (3%)
    reduce_scatter x1, waiting for transfers between devices, body(): lax.psum_scatter((product * scale).astype(jnp.bfloat16), 'tmc', scatter_d...  108 us
    psum x1, blocking collectives, body(): lax.psum(right_part + lax.ppermute(right_part, 'core', swap), 'tmc')  38 us
    all_to_all x1, waiting for transfers between devices, body(): got = lax.all_to_all(sent, TM, split_axis=0, concat_axis=0, tiled=True)  24 us
    dot_general x1, matrix products, body(): lax.dot_general(row_side, col_side, (((0,), (0,)), ((), ())), preferred_e...  18.1 us
    all_to_all x1, starting transfers between devices, body(): got = lax.all_to_all(sent, TM, split_axis=0, concat_axis=0, tiled=True)  8.3 us
    ppermute x1, waiting for transfers between devices, body(): got_rows = lax.ppermute(gathered, 'core', swap)  7.32 us
    another operation x3, other arithmetic, eliminate(): factor = jnp.linalg.cholesky(param_gram)  7.27 us
    another operation x2, other arithmetic, eliminate(): lax.linalg.triangular_solve(factor, white_params.T, left_side=True, lower...  6.17 us
  transfers between devices with their start and end apart: 8, of which 6 were waited for; matrix products, arithmetic and copies ran while one was open for 3% of the time, Pallas kernels for 0%

profile of v13, /device:TPU:24, one launch (start us, length us, event | category | flops | bytes accessed | tf_op | source)
XLA Modules:
  0.0 282.3 jit_solution(473147996435925269)
XLA Ops:
  7.2 0.5 broadcast.199
  7.7 2.2 fusion.59
  9.9 0.1 reshape_squeeze.3
  9.9 0.2 dynamic-slice_reduce_fusion
  10.1 0.6 reduce-window.6
  10.7 0.2 slice_reduce_fusion.1
  11.0 0.1 fusion.63
  11.1 0.8 broadcast_in_dim.14
  11.8 0.9 copy.16
  12.7 2.2 concatenate.34
  15.0 0.7 convolution_convert_fusion.1
  15.7 1.4 copy.18
  17.1 1.6 reshape.135
  18.7 8.3 %all-to-all-start = ((bf16[32,12,1985]{2,1,0:T(8,128)(2,1)}), bf16[32,12,1985]{2,1,0:T(8,128)(2,1)S(1)}, u32[]{:S(2)}, u32[]{:S(2)}) async-start(bf16[32,12,1985]{2,1,0:T(8,128)(2,1)} %reshape.135), calls=%async_computation | async-start | bytes 4194304 | tf_op jit(solution)/shard_map/all_to_all | solution.py:74
  27.0 0.0 all-gather.2.cloned.1.call-start
  27.1 0.6 dynamic_slice.20
  27.7 0.6 dynamic_slice.19
  30.2 0.1 convert_reduce_fusion
  30.2 0.1 iota_compare_fusion.11
  30.3 0.1 lt.67
  30.4 0.7 and_select_fusion
  31.1 0.1 broadcast_add_fusion
  31.1 0.1 add.110
  31.3 0.7 iota_compare_fusion.12
  31.9 24.0 %all-to-all-done = bf16[32,12,1985]{2,1,0:T(8,128)(2,1)S(1)} async-done(((bf16[32,12,1985]{2,1,0:T(8,128)(2,1)}), bf16[32,12,1985]{2,1,0:T(8,128)(2,1)S(1)}, u32[]{:S(2)}, u32[]{:S(2)}) %all-to-all-start) | async-done | bytes 1524512 | tf_op jit(solution)/shard_map/all_to_all | solution.py:74
  55.9 1.7 reshape.136
  57.6 1.2 slice_reduce_fusion
  58.8 1.6 fusion.38
  60.4 1.4 fusion.98
  61.8 1.1 slice.81
  63.0 0.3 copy-done
  63.3 0.2 fusion.100
  63.6 0.1 copy.19
  63.6 0.6 fusion.67
  64.3 6.6 %cholesky.17 = f32[64,64]{1,0:T(8,128)S(1)} custom-call(f32[64,64]{1,0:T(8,128)} %fusion.67), custom_call_target="Cholesky" | custom-call | tf_op jit(solution)/shard_map/jit(cholesky)/cholesky | solution.py:32
  70.9 0.6 compare_reduce_fusion
  71.6 0.7 fusion.58
  72.2 5.5 %custom-call.6 = f32[1,64,64]{1,2,0:T(8,128)} custom-call(f32[1,64,64]{2,1,0:T(8,128)S(1)} %fusion.58), custom_call_target="InvertDiagBlocksLowerTriangular" | custom-call | tf_op jit(solution)/shard_map/triangular_solve | solution.py:33
  77.7 1.0 fusion.97
  78.8 1.3 convolution_bitcast_fusion
  80.0 0.2 convolution_bitcast_fusion.1
  80.2 1.9 fusion.101
  82.1 0.1 collective-permute-start.1
  82.2 0.5 collective-permute-start
  82.7 0.4 convolution_reduce_fusion
  83.1 1.7 fusion.13
  84.8 1.9 fusion.31
  86.7 0.0 all-gather.2.cloned.1.call-update
  86.7 0.0 reduce-scatter.2.cloned.1.call-start
  86.8 0.4 collective-permute-start.2
  87.1 0.9 collective-permute-done.2
  88.0 38.0 %psum.7 = f32[1920]{0:T(1024)} all-reduce(f32[1920]{0:T(1024)S(1)} %add.119), channel_id=1, replica_groups=mesh['tmc'=16,'core'=2,'panel'=4] {'tmc'}, use_global_device_ids=true, to_apply=%region_8.9 | all-reduce | flops 1920 | bytes 15360 | tf_op jit(solution)/shard_map/psum | solution.py:100
  126.0 4.3 %all-gather.2.cloned.1.call-done = bf16[272,7680]{1,0:T(8,128)(2,1)} async-done(((bf16[272,1920]{1,0:T(8,128)(2,1)}), bf16[272,7680]{1,0:T(8,128)(2,1)}) %all-gather.2.cloned.1.call-update) | async-done | bytes 4177936 | tf_op jit(solution)/shard_map/all_gather | solution.py:99
  130.3 0.1 slice.87
  130.4 0.1 slice.88
  130.5 7.3 %collective-permute-done.3 = bf16[272,7680]{1,0:T(8,128)(2,1)} collective-permute-done((bf16[272,7680]{1,0:T(8,128)(2,1)}, bf16[272,7680]{1,0:T(8,128)(2,1)}, u32[]{:S(2)}, u32[]{:S(2)}) %collective-permute-start.3) | collective-permute-done | bytes 4177952 | tf_op jit(solution)/shard_map/ppermute | solution.py:103
  137.8 5.3 %fusion.99 = (bf16[128,7680]{1,0:T(8,128)(2,1)S(1)}, bf16[128,7680]{1,0:T(8,128)(2,1)S(1)}) fusion(bf16[272,7680]{1,0:T(8,128)(2,1)} %collective-permute-done.3, bf16[272,7680]{1,0:T(8,128)(2,1)} %all-gather.2.cloned.1.call-done, bf16[64,112]{1,0:T(8,128)(2,1)S(1)} %slice.88, bf16[64,112]{1,0:T(8,128)(2,1)S(1)} %slice.87, ...), kind=kOutput, calls=%fused_computation.136 | convolution fusion | flops 1089478656 | bytes 12386304 | tf_op jit(solution)/shard_map/dot_general | solution.py:121
  143.2 18.1 %multiply_convert_fusion = bf16[7680,960]{1,0:T(8,128)(2,1)} fusion(bf16[272,7680]{1,0:T(8,128)(2,1)} %collective-permute-done.3, bf16[272,7680]{1,0:T(8,128)(2,1)S(1)} %copy-done.2, bf16[128,7680]{1,0:T(8,128)(2,1)S(1)} %get-tuple-element.34, s32[]{:T(128)S(6)} %select_n.59, bf16[128,7680]{1,0:T(8,128)(2,1)S(1)} %get-tuple-element.35), kind=kOutput, calls=%fused_computation | convolution fusion | flops 9958625280 | bytes 35389444 | tf_op jit(solution)/shard_map/dot_general | solution.py:129
  161.3 108.0 %reduce-scatter.2.cloned.1.call-done = bf16[480,960]{1,0:T(8,128)(2,1)} async-done(((bf16[7680,960]{1,0:T(8,128)(2,1)}), bf16[480,960]{1,0:T(8,128)(2,1)}) %reduce-scatter.2.cloned.1.call-update) | async-done | bytes 921616 | tf_op jit(solution)/shard_map/reduce_scatter | solution.py:132
  269.4 1.4 convert.21
  270.8 0.1 dynamic-slice_bitcast_fusion.1
  270.9 0.1 collective-permute-start.4
  271.0 2.5 collective-permute-done.4
  273.6 1.8 maximum_select_fusion
  (25 shorter events, 0.2 us)
Async XLA Ops:
  18.7 8.4 %copy-start.3 = (f32[32]{0:T(128)S(1)}, f32[32]{0:T(128)}, u32[]{:S(2)}) copy-start(f32[32]{0:T(128)} %param.13) | copy-start | bytes 388
  18.7 9.0 %copy-start.4 = (f32[32]{0:T(128)S(1)}, f32[32]{0:T(128)}, u32[]{:S(2)}) copy-start(f32[32]{0:T(128)} %param.12) | copy-start | bytes 388
  18.7 37.2 %all-to-all-start = ((bf16[32,12,1985]{2,1,0:T(8,128)(2,1)}), bf16[32,12,1985]{2,1,0:T(8,128)(2,1)S(1)}, u32[]{:S(2)}, u32[]{:S(2)}) async-start(bf16[32,12,1985]{2,1,0:T(8,128)(2,1)} %reshape.135), calls=%async_computation | async-start | bytes 4194304 | tf_op jit(solution)/shard_map/all_to_all | solution.py:74
  27.0 103.3 %all-gather.2.cloned.1.call-start = ((), (), s32[]{:S(2)}) async-start(), calls=%async_computation.2 | async-start | bytes 5222400 | tf_op jit(solution)/shard_map/all_gather | solution.py:99
  31.9 28.5 %copy-start.5 = (pred[384]{0:T(512)(128)(4,1)}, pred[384]{0:T(512)(128)(4,1)S(1)}, u32[]{:S(2)}) copy-start(pred[384]{0:T(512)(128)(4,1)S(1)} %iota_compare_fusion.12) | copy-start | bytes 1156
  57.6 2.8 copy-start.1
  61.8 1.5 copy-start
  82.1 4.6 %collective-permute-start.1 = (bf16[64,384]{1,0:T(8,128)(2,1)S(1)}, bf16[64,384]{1,0:T(8,128)(2,1)S(1)}, u32[]{:S(2)}, u32[]{:S(2)}) collective-permute-start(bf16[64,384]{1,0:T(8,128)(2,1)S(1)} %get-tuple-element.29), channel_id=1, source_target_pairs={{0,4},{4,0},{1,5},{5,1},{2,6},{6,2},{3,7},{7,3},{8,12},{12,8},{9,1... | collective-permute-start | bytes 147464 | tf_op jit(solution)/shard_map/ppermute | solution.py:97
  82.2 2.6 collective-permute-start
  86.7 182.6 %reduce-scatter.2.cloned.1.call-start = ((), (), s32[]{:S(2)}) async-start(), calls=%async_computation.3 | async-start | bytes 16711680 | tf_op jit(solution)/shard_map/reduce_scatter | solution.py:132
  86.8 1.3 collective-permute-start.2
  130.3 7.5 %collective-permute-start.3 = (bf16[272,7680]{1,0:T(8,128)(2,1)}, bf16[272,7680]{1,0:T(8,128)(2,1)}, u32[]{:S(2)}, u32[]{:S(2)}) collective-permute-start(bf16[272,7680]{1,0:T(8,128)(2,1)} %all-gather.2.cloned.1.call-done), channel_id=1, source_target_pairs={{0,4},{4,0},{1,5},{5,1},{2,6},{6,2},{3,7},{7,3},{8,12},{12,8},{9,1... | collective-permute-start | bytes 12533768 | tf_op jit(solution)/shard_map/ppermute | solution.py:103
  137.8 5.4 %copy-start.2 = (bf16[272,7680]{1,0:T(8,128)(2,1)S(1)}, bf16[272,7680]{1,0:T(8,128)(2,1)}, u32[]{:S(2)}) copy-start(bf16[272,7680]{1,0:T(8,128)(2,1)} %all-gather.2.cloned.1.call-done) | copy-start | bytes 12533764
  270.9 2.6 collective-permute-start.4
Sparse Core Ops, SparseCore 0:
  86.9 43.4 all-gather.1
  161.4 107.8 reduce-scatter.1

commit v14 on v12

--- a/solution.py
+++ b/solution.py
@@ -134,17 +134,15 @@
     )
     pair = lax.psum_scatter(
         (product * scale).astype(jnp.bfloat16), "tmc", scatter_dimension=0, tiled=True
-    ).astype(jnp.float32)
+    )
     block_rows = pair.shape[0] // core_count
     by_core = pair.reshape(core_count, block_rows, half)
     mine = lax.dynamic_index_in_dim(by_core, core_index, 0, keepdims=False)
     given = lax.dynamic_index_in_dim(by_core, 1 - core_index, 0, keepdims=False)
     got = lax.ppermute(given, "core", swap)
-    normal = jnp.where(
-        core_index == 0,
-        jnp.concatenate([mine, got], axis=1),
-        jnp.concatenate([got, mine], axis=1),
-    )
+    first = jnp.where(core_index == 0, mine, got)
+    second = jnp.where(core_index == 0, got, mine)
+    normal = jnp.concatenate([first, second], axis=1).astype(jnp.float32)
     return (normal, right_hand)
 
 

time: 274 us -> 272 us (level)
  no operation moved by 1% of the time
where the time goes in v14:
time: 272 us; the launch traced here: 270 us
  waiting for transfers between devices  136 us (50%)
  blocking collectives  38 us (14%)
  matrix products  33.7 us (12%)
  other arithmetic  19.3 us (7%)
  starting transfers between devices  16.5 us (6%)
  between operations  16.3 us (6%)
  local copies, waits for them, and re-layouts  9.58 us (4%)
    reduce_scatter x1, waiting for transfers between devices, body(): lax.psum_scatter((product * scale).astype(jnp.bfloat16), 'tmc', scatter_d...  108 us
    psum x1, blocking collectives, body(): lax.psum(right_part + lax.ppermute(right_part, 'core', swap), 'tmc')  38 us
    dot_general x1, matrix products, body(): lax.dot_general(row_side, col_side, (((0,), (0,)), ((), ())), preferred_e...  18.1 us
    all_to_all x1, waiting for transfers between devices, body(): lax.all_to_all(send_design, TM, split_axis=0, concat_axis=0, tiled=True)  13.6 us
    all_to_all x1, starting transfers between devices, body(): lax.all_to_all(send_params, TM, split_axis=0, concat_axis=0, tiled=True)  8.16 us
    ppermute x1, waiting for transfers between devices, body(): got_rows = lax.ppermute(gathered, 'core', swap)  7.32 us
    all_to_all x1, starting transfers between devices, body(): lax.all_to_all(send_design, TM, split_axis=0, concat_axis=0, tiled=True)  6.93 us
    another operation x3, other arithmetic, eliminate(): factor = jnp.linalg.cholesky(param_gram)  6.52 us
  transfers between devices with their start and end apart: 9, of which 7 were waited for; matrix products, arithmetic and copies ran while one was open for 10% of the time, Pallas kernels for 0%

profile of v14, /device:TPU:24, one launch (start us, length us, event | category | flops | bytes accessed | tf_op | source)
XLA Modules:
  0.0 269.8 jit_solution(11405174341676064039)
XLA Ops:
  7.2 0.5 broadcast.199
  7.7 2.3 fusion.62
  10.0 0.1 reshape_squeeze.3
  10.0 0.2 dynamic-slice_reduce_fusion
  10.2 0.6 reduce-window.6
  10.8 0.2 slice_reduce_fusion.1
  11.1 0.1 fusion.66
  11.2 0.7 broadcast_in_dim.12
  11.8 1.0 convolution_convert_fusion.2
  12.8 0.1 copy.13
  13.0 0.8 reshape.169
  13.8 8.2 %all-to-all-start = ((bf16[32,2,390]{2,1,0:T(2,128)(2,1)}), bf16[32,2,390]{2,1,0:T(2,128)(2,1)S(1)}, u32[]{:S(2)}, u32[]{:S(2)}) async-start(bf16[32,2,390]{2,1,0:T(2,128)(2,1)} %reshape.169), calls=%async_computation | async-start | bytes 131072 | tf_op jit(solution)/shard_map/all_to_all | solution.py:75
  22.0 0.1 convert_reduce_fusion
  22.0 0.6 convolution_convert_fusion.1
  22.6 0.1 iota_compare_fusion.12
  22.7 0.7 and_select_fusion
  23.4 0.1 broadcast_add_fusion
  23.5 0.7 iota_compare_fusion.13
  24.1 1.5 reshape.138
  25.6 0.6 dynamic_slice.20
  26.2 0.6 dynamic_slice.19
  28.8 0.1 lt.67
  28.9 0.1 add.110
  29.0 0.5 all-to-all-done
  29.5 0.2 reshape.170
  29.7 0.7 fusion.36
  30.4 0.2 fusion.104
  30.6 0.1 copy.14
  30.7 6.9 %all-to-all-start.1 = ((bf16[32,12,1920]{2,1,0:T(8,128)(2,1)}), bf16[32,12,1920]{2,1,0:T(8,128)(2,1)S(1)}, u32[]{:S(2)}, u32[]{:S(2)}) async-start(bf16[32,12,1920]{2,1,0:T(8,128)(2,1)} %reshape.138), calls=%async_computation.1 | async-start | bytes 3932160 | tf_op jit(solution)/shard_map/all_to_all | solution.py:77
  37.7 5.8 %cholesky.17 = f32[64,64]{1,0:T(8,128)S(1)} custom-call(f32[64,64]{1,0:T(8,128)S(1)} %fusion.70), custom_call_target="Cholesky" | custom-call | tf_op jit(solution)/shard_map/jit(cholesky)/cholesky | solution.py:32
  43.6 0.6 compare_reduce_fusion
  44.2 0.7 fusion.61
  44.9 4.9 %custom-call.6 = f32[1,64,64]{1,2,0:T(8,128)S(1)} custom-call(f32[1,64,64]{2,1,0:T(8,128)S(1)} %fusion.61), custom_call_target="InvertDiagBlocksLowerTriangular" | custom-call | tf_op jit(solution)/shard_map/triangular_solve | solution.py:33
  49.8 0.2 slice_reduce_fusion
  50.0 0.3 fusion.101
  50.3 0.4 collective-permute-start.1
  50.7 0.6 convolution_bitcast_fusion
  51.3 0.2 convolution_bitcast_fusion.1
  51.5 13.6 %all-to-all-done.1 = bf16[32,12,1920]{2,1,0:T(8,128)(2,1)S(1)} async-done(((bf16[32,12,1920]{2,1,0:T(8,128)(2,1)}), bf16[32,12,1920]{2,1,0:T(8,128)(2,1)S(1)}, u32[]{:S(2)}, u32[]{:S(2)}) %all-to-all-start.1) | async-done | bytes 1474592 | tf_op jit(solution)/shard_map/all_to_all | solution.py:77
  65.1 1.3 reshape.140
  66.4 2.8 %fusion.102 = (bf16[384,1920]{1,0:T(8,128)(2,1)S(1)}, f32[384,1920]{1,0:T(8,128)S(1)}) fusion(bf16[384,1920]{1,0:T(8,128)(2,1)} %reshape.140, f32[]{:T(128)} %bitcast.1, f32[]{:T(128)} %bitcast, s32[384]{0:T(512)S(1)} %add.110, pred[384]{0:T(512)(128)(4,1)S(1)} %lt.67, pred[384]{0:T(512)(128)(4,1)S(1)} %iota_compare_fusion.13), kind=kOutput, calls=%fused_computation.141 | convolution fusion | flops 570359808 | bytes 5900552 | tf_op jit(solution)/shard_map/dot_general | solution.py:25
  69.2 0.1 slice.76
  69.3 1.8 fusion.105
  71.2 0.3 collective-permute-start
  71.4 0.4 convolution_reduce_fusion
  71.8 1.7 fusion.11
  73.5 0.1 fusion.29
  73.7 0.9 copy-done.1
  74.6 0.0 reduce-scatter.2.cloned.1.call-start
  74.7 0.6 collective-permute-start.2
  75.3 0.8 collective-permute-done.2
  76.1 38.0 %psum.7 = f32[1920]{0:T(1024)} all-reduce(f32[1920]{0:T(1024)S(1)} %add.119), channel_id=1, replica_groups=mesh['tmc'=16,'core'=2,'panel'=4] {'tmc'}, use_global_device_ids=true, to_apply=%region_8.9 | all-reduce | flops 1920 | bytes 15360 | tf_op jit(solution)/shard_map/psum | solution.py:103
  114.1 4.3 %all-gather.2.cloned.1.call-done = bf16[272,7680]{1,0:T(8,128)(2,1)} async-done(((bf16[272,1920]{1,0:T(8,128)(2,1)}), bf16[272,7680]{1,0:T(8,128)(2,1)}) %all-gather.2.cloned.1.call-update) | async-done | bytes 4177936 | tf_op jit(solution)/shard_map/all_gather | solution.py:102
  118.4 0.1 slice.82
  118.5 0.1 slice.83
  118.6 7.3 %collective-permute-done.3 = bf16[272,7680]{1,0:T(8,128)(2,1)} collective-permute-done((bf16[272,7680]{1,0:T(8,128)(2,1)}, bf16[272,7680]{1,0:T(8,128)(2,1)}, u32[]{:S(2)}, u32[]{:S(2)}) %collective-permute-start.3) | collective-permute-done | bytes 4177952 | tf_op jit(solution)/shard_map/ppermute | solution.py:106
  125.9 5.3 %fusion.103 = (bf16[128,7680]{1,0:T(8,128)(2,1)S(1)}, bf16[128,7680]{1,0:T(8,128)(2,1)S(1)}) fusion(bf16[272,7680]{1,0:T(8,128)(2,1)} %collective-permute-done.3, bf16[272,7680]{1,0:T(8,128)(2,1)} %all-gather.2.cloned.1.call-done, bf16[64,112]{1,0:T(8,128)(2,1)S(1)} %slice.83, bf16[64,112]{1,0:T(8,128)(2,1)S(1)} %slice.82, ...), kind=kOutput, calls=%fused_computation.142 | convolution fusion | flops 1089478656 | bytes 12386304 | tf_op jit(solution)/shard_map/dot_general | solution.py:124
  131.2 18.1 %multiply_convert_fusion = bf16[7680,960]{1,0:T(8,128)(2,1)} fusion(bf16[272,7680]{1,0:T(8,128)(2,1)} %collective-permute-done.3, bf16[272,7680]{1,0:T(8,128)(2,1)S(1)} %copy-done.2, bf16[128,7680]{1,0:T(8,128)(2,1)S(1)} %get-tuple-element.38, s32[]{:T(128)S(6)} %select_n.63, bf16[128,7680]{1,0:T(8,128)(2,1)S(1)} %get-tuple-element.39), kind=kOutput, calls=%fused_computation | convolution fusion | flops 9958625280 | bytes 35389444 | tf_op jit(solution)/shard_map/dot_general | solution.py:132
  149.4 108.0 %reduce-scatter.2.cloned.1.call-done = bf16[480,960]{1,0:T(8,128)(2,1)} async-done(((bf16[7680,960]{1,0:T(8,128)(2,1)}), bf16[480,960]{1,0:T(8,128)(2,1)}) %reduce-scatter.2.cloned.1.call-update) | async-done | bytes 921616 | tf_op jit(solution)/shard_map/reduce_scatter | solution.py:135
  257.3 1.1 dynamic-slice_bitcast_fusion
  258.4 0.1 collective-permute-start.4
  258.5 1.8 collective-permute-done.4
  260.4 1.1 bitcast_select_fusion.1
  261.5 1.5 maximum_convert_fusion
  (28 shorter events, 0.3 us)
Async XLA Ops:
  7.2 14.9 %copy-start = (bf16[256,1920]{1,0:T(8,128)(2,1)S(1)}, bf16[256,1920]{1,0:T(8,128)(2,1)}, u32[]{:S(2)}) copy-start(bf16[256,1920]{1,0:T(8,128)(2,1)} %param.8) | copy-start | bytes 2949124
  13.8 15.7 %all-to-all-start = ((bf16[32,2,390]{2,1,0:T(2,128)(2,1)}), bf16[32,2,390]{2,1,0:T(2,128)(2,1)S(1)}, u32[]{:S(2)}, u32[]{:S(2)}) async-start(bf16[32,2,390]{2,1,0:T(2,128)(2,1)} %reshape.169), calls=%async_computation | async-start | bytes 131072 | tf_op jit(solution)/shard_map/all_to_all | solution.py:75
  22.0 3.6 %copy-start.3 = (f32[32]{0:T(128)S(1)}, f32[32]{0:T(128)}, u32[]{:S(2)}) copy-start(f32[32]{0:T(128)} %param.13) | copy-start | bytes 388
  22.0 4.2 %copy-start.4 = (f32[32]{0:T(128)S(1)}, f32[32]{0:T(128)}, u32[]{:S(2)}) copy-start(f32[32]{0:T(128)} %param.12) | copy-start | bytes 388
  30.7 34.4 %all-to-all-start.1 = ((bf16[32,12,1920]{2,1,0:T(8,128)(2,1)}), bf16[32,12,1920]{2,1,0:T(8,128)(2,1)S(1)}, u32[]{:S(2)}, u32[]{:S(2)}) async-start(bf16[32,12,1920]{2,1,0:T(8,128)(2,1)} %reshape.138), calls=%async_computation.1 | async-start | bytes 3932160 | tf_op jit(solution)/shard_map/all_to_all | solution.py:77
  37.7 80.8 %all-gather.2.cloned.1.call-start = ((), (), s32[]{:S(2)}) async-start(), calls=%async_computation.3 | async-start | bytes 5222400 | tf_op jit(solution)/shard_map/all_gather | solution.py:102
  50.3 23.3 %collective-permute-start.1 = (bf16[64,384]{1,0:T(8,128)(2,1)S(1)}, bf16[64,384]{1,0:T(8,128)(2,1)S(1)}, u32[]{:S(2)}, u32[]{:S(2)}) collective-permute-start(bf16[64,384]{1,0:T(8,128)(2,1)S(1)} %get-tuple-element.33), channel_id=1, source_target_pairs={{0,4},{4,0},{1,5},{5,1},{2,6},{6,2},{3,7},{7,3},{8,12},{12,8},{9,1... | collective-permute-start | bytes 147464 | tf_op jit(solution)/shard_map/ppermute | solution.py:100
  71.2 2.4 collective-permute-start
  73.6 1.0 copy-start.1
  74.6 182.7 %reduce-scatter.2.cloned.1.call-start = ((), (), s32[]{:S(2)}) async-start(), calls=%async_computation.4 | async-start | bytes 16711680 | tf_op jit(solution)/shard_map/reduce_scatter | solution.py:135
  74.7 1.4 collective-permute-start.2
  118.4 7.5 %collective-permute-start.3 = (bf16[272,7680]{1,0:T(8,128)(2,1)}, bf16[272,7680]{1,0:T(8,128)(2,1)}, u32[]{:S(2)}, u32[]{:S(2)}) collective-permute-start(bf16[272,7680]{1,0:T(8,128)(2,1)} %all-gather.2.cloned.1.call-done), channel_id=1, source_target_pairs={{0,4},{4,0},{1,5},{5,1},{2,6},{6,2},{3,7},{7,3},{8,12},{12,8},{9,1... | collective-permute-start | bytes 12533768 | tf_op jit(solution)/shard_map/ppermute | solution.py:106
  125.9 5.3 %copy-start.2 = (bf16[272,7680]{1,0:T(8,128)(2,1)S(1)}, bf16[272,7680]{1,0:T(8,128)(2,1)}, u32[]{:S(2)}) copy-start(bf16[272,7680]{1,0:T(8,128)(2,1)} %all-gather.2.cloned.1.call-done) | copy-start | bytes 12533764
  258.4 1.9 collective-permute-start.4
Sparse Core Ops, SparseCore 0:
  74.8 43.6 all-gather.1
  149.5 107.8 reduce-scatter.1

commit v15 on v14

--- a/solution.py
+++ b/solution.py
@@ -121,9 +121,9 @@
         axis=0,
     ).astype(jnp.bfloat16)
     design_side = jnp.concatenate([gathered, got_rows], axis=0)
-    terms = jnp.dot(stacked_basis, design_side, preferred_element_type=jnp.float32).astype(
-        jnp.bfloat16
-    )
+    own_share = jnp.dot(stacked_basis[:, :keep], gathered, preferred_element_type=jnp.float32)
+    far_share = jnp.dot(stacked_basis[:, keep:], got_rows, preferred_element_type=jnp.float32)
+    terms = (own_share + far_share).astype(jnp.bfloat16)
     row_side = jnp.concatenate([design_side, -terms], axis=0)
     col_side = lax.dynamic_slice_in_dim(
         jnp.concatenate([design_side, terms], axis=0),

time: 272 us -> 270 us (level)
  waiting for transfers between devices: 136 us -> 133 us
    ppermute x1, waiting for transfers between devices: 7.32 us -> 3.83 us  [body(): got_rows = lax.ppermute(gathered, 'core', swap)]
    dot_general x1 -> x2, matrix products: 5.31 us -> 6.78 us  [the longest x1 3.42 us: body(): jnp.dot(stacked_basis[:, keep:], got_rows, preferred_element_type=jnp.flo...]
  transfers between devices with their start and end apart: 9 -> 9, of which waited for: 7 -> 7; matrix products, arithmetic and copies ran while one was open for 10% -> 11% of each run, Pallas kernels for 0% -> 0%
where the time goes in v15:
time: 270 us; the launch traced here: 268 us
  waiting for transfers between devices  133 us (49%)
  blocking collectives  38 us (14%)
  matrix products  35.2 us (13%)
  other arithmetic  19.4 us (7%)
  starting transfers between devices  16.5 us (6%)
  between operations  16.3 us (6%)
  local copies, waits for them, and re-layouts  9.58 us (4%)
    reduce_scatter x1, waiting for transfers between devices, body(): lax.psum_scatter((product * scale).astype(jnp.bfloat16), 'tmc', scatter_d...  108 us
    psum x1, blocking collectives, body(): lax.psum(right_part + lax.ppermute(right_part, 'core', swap), 'tmc')  38 us
    dot_general x1, matrix products, body(): lax.dot_general(row_side, col_side, (((0,), (0,)), ((), ())), preferred_e...  18.1 us
    all_to_all x1, waiting for transfers between devices, body(): lax.all_to_all(send_design, TM, split_axis=0, concat_axis=0, tiled=True)  13.6 us
    all_to_all x1, starting transfers between devices, body(): lax.all_to_all(send_params, TM, split_axis=0, concat_axis=0, tiled=True)  8.16 us
    all_to_all x1, starting transfers between devices, body(): lax.all_to_all(send_design, TM, split_axis=0, concat_axis=0, tiled=True)  6.93 us
    another operation x3, other arithmetic, eliminate(): factor = jnp.linalg.cholesky(param_gram)  6.52 us
    another operation x2, other arithmetic, eliminate(): lax.linalg.triangular_solve(factor, white_params.T, left_side=True, lower...  5.55 us
  transfers between devices with their start and end apart: 9, of which 7 were waited for; matrix products, arithmetic and copies ran while one was open for 11% of the time, Pallas kernels for 0%

profile of v15, /device:TPU:24, one launch (start us, length us, event | category | flops | bytes accessed | tf_op | source)
XLA Modules:
  0.0 267.9 jit_solution(1347444503536471045)
XLA Ops:
  7.2 0.5 broadcast.190
  7.7 2.3 fusion.52
  10.0 0.1 reshape_squeeze.3
  10.0 0.2 dynamic-slice_reduce_fusion
  10.2 0.6 reduce-window.6
  10.8 0.2 slice_reduce_fusion.1
  11.1 0.1 fusion.56
  11.2 0.7 broadcast_in_dim.12
  11.8 1.0 convolution_convert_fusion.1
  12.8 0.1 copy.13
  13.0 0.8 reshape.169
  13.8 8.2 %all-to-all-start = ((bf16[32,2,390]{2,1,0:T(2,128)(2,1)}), bf16[32,2,390]{2,1,0:T(2,128)(2,1)S(1)}, u32[]{:S(2)}, u32[]{:S(2)}) async-start(bf16[32,2,390]{2,1,0:T(2,128)(2,1)} %reshape.169), calls=%async_computation | async-start | bytes 131072 | tf_op jit(solution)/shard_map/all_to_all | solution.py:75
  22.0 0.6 convolution_convert_fusion
  22.6 0.1 iota_compare_fusion.12
  22.7 0.7 and_select_fusion
  23.4 0.1 broadcast_add_fusion
  23.5 0.7 iota_compare_fusion.13
  24.1 1.5 reshape.138
  25.6 0.6 dynamic_slice.20
  26.2 0.6 dynamic_slice.19
  28.8 0.1 lt.67
  28.9 0.1 add.113
  29.0 0.5 all-to-all-done
  29.5 0.2 reshape.170
  29.7 0.7 fusion.34
  30.4 0.2 fusion.90
  30.6 0.1 copy.14
  30.7 6.9 %all-to-all-start.1 = ((bf16[32,12,1920]{2,1,0:T(8,128)(2,1)}), bf16[32,12,1920]{2,1,0:T(8,128)(2,1)S(1)}, u32[]{:S(2)}, u32[]{:S(2)}) async-start(bf16[32,12,1920]{2,1,0:T(8,128)(2,1)} %reshape.138), calls=%async_computation.1 | async-start | bytes 3932160 | tf_op jit(solution)/shard_map/all_to_all | solution.py:77
  37.7 5.8 %cholesky.17 = f32[64,64]{1,0:T(8,128)S(1)} custom-call(f32[64,64]{1,0:T(8,128)S(1)} %fusion.60), custom_call_target="Cholesky" | custom-call | tf_op jit(solution)/shard_map/jit(cholesky)/cholesky | solution.py:32
  43.6 0.6 compare_reduce_fusion
  44.2 0.7 fusion.51
  44.9 4.9 %custom-call.6 = f32[1,64,64]{1,2,0:T(8,128)S(1)} custom-call(f32[1,64,64]{2,1,0:T(8,128)S(1)} %fusion.51), custom_call_target="InvertDiagBlocksLowerTriangular" | custom-call | tf_op jit(solution)/shard_map/triangular_solve | solution.py:33
  49.8 0.2 slice_reduce_fusion
  50.0 0.3 fusion.87
  50.3 0.4 collective-permute-start.1
  50.7 0.6 convolution_bitcast_fusion
  51.3 0.2 convolution_bitcast_fusion.1
  51.5 13.6 %all-to-all-done.1 = bf16[32,12,1920]{2,1,0:T(8,128)(2,1)S(1)} async-done(((bf16[32,12,1920]{2,1,0:T(8,128)(2,1)}), bf16[32,12,1920]{2,1,0:T(8,128)(2,1)S(1)}, u32[]{:S(2)}, u32[]{:S(2)}) %all-to-all-start.1) | async-done | bytes 1474592 | tf_op jit(solution)/shard_map/all_to_all | solution.py:77
  65.1 1.3 reshape.140
  66.4 2.8 %fusion.88 = (bf16[384,1920]{1,0:T(8,128)(2,1)S(1)}, f32[384,1920]{1,0:T(8,128)S(1)}) fusion(bf16[384,1920]{1,0:T(8,128)(2,1)} %reshape.140, f32[]{:T(128)} %bitcast.1, f32[]{:T(128)} %bitcast, s32[384]{0:T(512)S(1)} %add.113, pred[384]{0:T(512)(128)(4,1)S(1)} %lt.67, pred[384]{0:T(512)(128)(4,1)S(1)} %iota_compare_fusion.13), kind=kOutput, calls=%fused_computation.131 | convolution fusion | flops 570359808 | bytes 5900552 | tf_op jit(solution)/shard_map/dot_general | solution.py:25
  69.2 0.1 slice.84
  69.3 1.8 fusion.91
  71.2 0.3 collective-permute-start
  71.4 0.4 convolution_reduce_fusion
  71.8 1.7 fusion.9
  73.5 0.1 fusion.27
  73.7 0.9 copy-done.2
  74.7 0.6 collective-permute-start.2
  75.3 0.8 collective-permute-done.2
  76.1 38.0 %psum.7 = f32[1920]{0:T(1024)} all-reduce(f32[1920]{0:T(1024)S(1)} %add.122), channel_id=1, replica_groups=mesh['tmc'=16,'core'=2,'panel'=4] {'tmc'}, use_global_device_ids=true, to_apply=%region_8.9 | all-reduce | flops 1920 | bytes 15360 | tf_op jit(solution)/shard_map/psum | solution.py:103
  114.1 4.3 %all-gather.2.cloned.1.call-done = bf16[272,7680]{1,0:T(8,128)(2,1)} async-done(((bf16[272,1920]{1,0:T(8,128)(2,1)}), bf16[272,7680]{1,0:T(8,128)(2,1)}) %all-gather.2.cloned.1.call-update) | async-done | bytes 4177936 | tf_op jit(solution)/shard_map/all_gather | solution.py:102
  118.4 0.1 slice.90
  118.5 0.1 slice.91
  118.6 0.1 fusion.42
  118.7 3.4 %fusion.45 = f32[128,7680]{1,0:T(8,128)S(1)} fusion(bf16[272,7680]{1,0:T(8,128)(2,1)} %all-gather.2.cloned.1.call-done, bf16[128,544]{1,0:T(8,128)(2,1)S(1)} %fusion.42), kind=kOutput, calls=%fused_computation.66 | convolution fusion | flops 534773760 | bytes 8208384 | tf_op jit(solution)/shard_map/dot_general | solution.py:124
  122.1 3.8 %collective-permute-done.3 = bf16[272,7680]{1,0:T(8,128)(2,1)} collective-permute-done((bf16[272,7680]{1,0:T(8,128)(2,1)}, bf16[272,7680]{1,0:T(8,128)(2,1)}, u32[]{:S(2)}, u32[]{:S(2)}) %collective-permute-start.3) | collective-permute-done | bytes 4177952 | tf_op jit(solution)/shard_map/ppermute | solution.py:106
  125.9 3.4 %fusion.89 = (bf16[128,7680]{1,0:T(8,128)(2,1)S(1)}, bf16[128,7680]{1,0:T(8,128)(2,1)S(1)}) fusion(f32[128,7680]{1,0:T(8,128)S(1)} %fusion.45, bf16[272,7680]{1,0:T(8,128)(2,1)} %collective-permute-done.3, bf16[128,544]{1,0:T(8,128)(2,1)S(1)} %fusion.42), kind=kOutput, calls=%fused_computation.132 | convolution fusion | flops 537722880 | bytes 12140544 | tf_op jit(solution)/shard_map/dot_general | solution.py:125
  129.3 18.1 %multiply_convert_fusion = bf16[7680,960]{1,0:T(8,128)(2,1)} fusion(bf16[272,7680]{1,0:T(8,128)(2,1)} %collective-permute-done.3, bf16[272,7680]{1,0:T(8,128)(2,1)S(1)} %copy-done.1, bf16[128,7680]{1,0:T(8,128)(2,1)S(1)} %get-tuple-element.38, s32[]{:T(128)S(6)} %select_n.63, bf16[128,7680]{1,0:T(8,128)(2,1)S(1)} %get-tuple-element.39), kind=kOutput, calls=%fused_computation | convolution fusion | flops 9958625280 | bytes 35389444 | tf_op jit(solution)/shard_map/dot_general | solution.py:132
  147.5 108.0 %reduce-scatter.2.cloned.1.call-done = bf16[480,960]{1,0:T(8,128)(2,1)} async-done(((bf16[7680,960]{1,0:T(8,128)(2,1)}), bf16[480,960]{1,0:T(8,128)(2,1)}) %reduce-scatter.2.cloned.1.call-update) | async-done | bytes 921616 | tf_op jit(solution)/shard_map/reduce_scatter | solution.py:135
  255.5 1.1 dynamic-slice_bitcast_fusion
  256.5 0.1 collective-permute-start.4
  256.6 1.8 collective-permute-done.4
  258.5 1.1 bitcast_select_fusion.1
  259.6 1.5 maximum_convert_fusion
  (30 shorter events, 0.4 us)
Async XLA Ops:
  7.2 14.9 %copy-start = (bf16[256,1920]{1,0:T(8,128)(2,1)S(1)}, bf16[256,1920]{1,0:T(8,128)(2,1)}, u32[]{:S(2)}) copy-start(bf16[256,1920]{1,0:T(8,128)(2,1)} %param.8) | copy-start | bytes 2949124
  13.8 15.7 %all-to-all-start = ((bf16[32,2,390]{2,1,0:T(2,128)(2,1)}), bf16[32,2,390]{2,1,0:T(2,128)(2,1)S(1)}, u32[]{:S(2)}, u32[]{:S(2)}) async-start(bf16[32,2,390]{2,1,0:T(2,128)(2,1)} %reshape.169), calls=%async_computation | async-start | bytes 131072 | tf_op jit(solution)/shard_map/all_to_all | solution.py:75
  22.0 3.6 %copy-start.3 = (f32[32]{0:T(128)S(1)}, f32[32]{0:T(128)}, u32[]{:S(2)}) copy-start(f32[32]{0:T(128)} %param.13) | copy-start | bytes 388
  22.0 4.2 %copy-start.4 = (f32[32]{0:T(128)S(1)}, f32[32]{0:T(128)}, u32[]{:S(2)}) copy-start(f32[32]{0:T(128)} %param.12) | copy-start | bytes 388
  30.7 34.4 %all-to-all-start.1 = ((bf16[32,12,1920]{2,1,0:T(8,128)(2,1)}), bf16[32,12,1920]{2,1,0:T(8,128)(2,1)S(1)}, u32[]{:S(2)}, u32[]{:S(2)}) async-start(bf16[32,12,1920]{2,1,0:T(8,128)(2,1)} %reshape.138), calls=%async_computation.1 | async-start | bytes 3932160 | tf_op jit(solution)/shard_map/all_to_all | solution.py:77
  37.7 80.8 %all-gather.2.cloned.1.call-start = ((), (), s32[]{:S(2)}) async-start(), calls=%async_computation.3 | async-start | bytes 5222400 | tf_op jit(solution)/shard_map/all_gather | solution.py:102
  50.3 23.3 %collective-permute-start.1 = (bf16[64,384]{1,0:T(8,128)(2,1)S(1)}, bf16[64,384]{1,0:T(8,128)(2,1)S(1)}, u32[]{:S(2)}, u32[]{:S(2)}) collective-permute-start(bf16[64,384]{1,0:T(8,128)(2,1)S(1)} %get-tuple-element.33), channel_id=1, source_target_pairs={{0,4},{4,0},{1,5},{5,1},{2,6},{6,2},{3,7},{7,3},{8,12},{12,8},{9,1... | collective-permute-start | bytes 147464 | tf_op jit(solution)/shard_map/ppermute | solution.py:100
  71.2 2.4 collective-permute-start
  73.7 1.0 copy-start.2
  74.6 180.8 %reduce-scatter.2.cloned.1.call-start = ((), (), s32[]{:S(2)}) async-start(), calls=%async_computation.4 | async-start | bytes 16711680 | tf_op jit(solution)/shard_map/reduce_scatter | solution.py:135
  74.7 1.4 collective-permute-start.2
  118.4 7.5 %collective-permute-start.3 = (bf16[272,7680]{1,0:T(8,128)(2,1)}, bf16[272,7680]{1,0:T(8,128)(2,1)}, u32[]{:S(2)}, u32[]{:S(2)}) collective-permute-start(bf16[272,7680]{1,0:T(8,128)(2,1)} %all-gather.2.cloned.1.call-done), channel_id=1, source_target_pairs={{0,4},{4,0},{1,5},{5,1},{2,6},{6,2},{3,7},{7,3},{8,12},{12,8},{9,1... | collective-permute-start | bytes 12533768 | tf_op jit(solution)/shard_map/ppermute | solution.py:106
  122.1 7.3 %copy-start.1 = (bf16[272,7680]{1,0:T(8,128)(2,1)S(1)}, bf16[272,7680]{1,0:T(8,128)(2,1)}, u32[]{:S(2)}) copy-start(bf16[272,7680]{1,0:T(8,128)(2,1)} %all-gather.2.cloned.1.call-done) | copy-start | bytes 12533764
  256.5 1.9 collective-permute-start.4
Sparse Core Ops, SparseCore 0:
  74.8 43.6 all-gather.1
  147.6 107.8 reduce-scatter.1

commit v16 on v15

--- a/solution.py
+++ b/solution.py
@@ -98,7 +98,7 @@
     moved = lax.ppermute(design_bf[keep:], "core", swap)
     packed = design_bf[:keep].at[short_most : short_most + moved.shape[0]].add(moved)
     got_basis = lax.ppermute(basis, "core", swap)
-    packed, right_part, got_basis = lax.optimization_barrier((packed, right_part, got_basis))
+    packed, got_basis = lax.optimization_barrier((packed, got_basis))
     gathered = lax.all_gather(packed, "panel", axis=1, tiled=True)
     right_hand = lax.psum(right_part + lax.ppermute(right_part, "core", swap), "tmc")
     gathered, right_hand = lax.optimization_barrier((gathered, right_hand))

time: 270 us -> 274 us (1.015)
  matrix products: 35.2 us -> 39.9 us
  waiting for transfers between devices: 133 us -> 129 us
  local copies, waits for them, and re-layouts: 9.58 us -> 12.8 us
    reduce_scatter x1, waiting for transfers between devices: 108 us -> 104 us  [body(): lax.psum_scatter((product * scale).astype(jnp.bfloat16), 'tmc', scatter_d...]
    all_gather x1, waiting for transfers between devices: 4.29 us -> 0.01 us  [body(): gathered = lax.all_gather(packed, 'panel', axis=1, tiled=True)]
    all_to_all x1, waiting for transfers between devices: 13.6 us -> 17.7 us  [body(): lax.all_to_all(send_design, TM, split_axis=0, concat_axis=0, tiled=True)]
  transfers between devices with their start and end apart: 9 -> 9, of which waited for: 7 -> 6; matrix products, arithmetic and copies ran while one was open for 11% -> 12% of each run, Pallas kernels for 0% -> 0%
where the time goes in v16:
time: 274 us; the launch traced here: 271 us
  waiting for transfers between devices  129 us (47%)
  matrix products  39.9 us (15%)
  blocking collectives  38 us (14%)
  other arithmetic  21.1 us (8%)
  between operations  16.3 us (6%)
  starting transfers between devices  14.5 us (5%)
  local copies, waits for them, and re-layouts  12.8 us (5%)
    reduce_scatter x1, waiting for transfers between devices, body(): lax.psum_scatter((product * scale).astype(jnp.bfloat16), 'tmc', scatter_d...  104 us
    psum x1, blocking collectives, body(): lax.psum(right_part + lax.ppermute(right_part, 'core', swap), 'tmc')  38 us
    dot_general x1, matrix products, body(): lax.dot_general(row_side, col_side, (((0,), (0,)), ((), ())), preferred_e...  18.1 us
    all_to_all x1, waiting for transfers between devices, body(): lax.all_to_all(send_design, TM, split_axis=0, concat_axis=0, tiled=True)  17.7 us
    all_to_all x1, starting transfers between devices, body(): lax.all_to_all(send_params, TM, split_axis=0, concat_axis=0, tiled=True)  8.16 us
    another operation x3, other arithmetic, eliminate(): factor = jnp.linalg.cholesky(param_gram)  6.52 us
    another operation x2, other arithmetic, eliminate(): lax.linalg.triangular_solve(factor, white_params.T, left_side=True, lower...  5.55 us
  transfers between devices with their start and end apart: 9, of which 6 were waited for; matrix products, arithmetic and copies ran while one was open for 12% of the time, Pallas kernels for 0%

profile of v16, /device:TPU:24, one launch (start us, length us, event | category | flops | bytes accessed | tf_op | source)
XLA Modules:
  0.0 271.3 jit_solution(6843159748275065455)
XLA Ops:
  7.2 0.5 broadcast.190
  7.7 2.2 fusion.52
  9.9 0.1 reshape_squeeze.3
  10.0 0.2 dynamic-slice_reduce_fusion
  10.2 0.6 reduce-window.6
  10.8 0.2 slice_reduce_fusion.1
  11.0 0.1 fusion.56
  11.1 0.7 broadcast_in_dim.12
  11.8 1.0 convolution_convert_fusion.1
  12.8 0.1 copy.13
  12.9 0.8 reshape.169
  13.7 8.2 %all-to-all-start = ((bf16[32,2,390]{2,1,0:T(2,128)(2,1)}), bf16[32,2,390]{2,1,0:T(2,128)(2,1)S(1)}, u32[]{:S(2)}, u32[]{:S(2)}) async-start(bf16[32,2,390]{2,1,0:T(2,128)(2,1)} %reshape.169), calls=%async_computation | async-start | bytes 131072 | tf_op jit(solution)/shard_map/all_to_all | solution.py:75
  22.0 0.6 convolution_convert_fusion
  22.6 0.1 iota_compare_fusion.12
  22.6 1.4 reshape.138
  24.1 0.6 dynamic_slice.20
  24.7 0.6 dynamic_slice.19
  27.3 0.1 lt.67
  27.4 2.1 all-to-all-done
  29.4 0.2 reshape.170
  29.6 5.3 %all-to-all-start.1 = ((bf16[32,12,1920]{2,1,0:T(8,128)(2,1)}), bf16[32,12,1920]{2,1,0:T(8,128)(2,1)S(1)}, u32[]{:S(2)}, u32[]{:S(2)}) async-start(bf16[32,12,1920]{2,1,0:T(8,128)(2,1)} %reshape.138), calls=%async_computation.1 | async-start | bytes 3932160 | tf_op jit(solution)/shard_map/all_to_all | solution.py:77
  35.0 0.6 and_select_fusion
  35.7 0.1 add.113
  35.8 0.7 iota_compare_fusion.13
  36.6 0.7 fusion.35
  37.3 0.6 copy-done.4
  37.9 0.2 fusion.90
  38.1 0.1 copy.14
  38.2 5.8 %cholesky.17 = f32[64,64]{1,0:T(8,128)S(1)} custom-call(f32[64,64]{1,0:T(8,128)S(1)} %fusion.60), custom_call_target="Cholesky" | custom-call | tf_op jit(solution)/shard_map/jit(cholesky)/cholesky | solution.py:32
  44.1 0.6 compare_reduce_fusion
  44.8 17.7 %all-to-all-done.1 = bf16[32,12,1920]{2,1,0:T(8,128)(2,1)S(1)} async-done(((bf16[32,12,1920]{2,1,0:T(8,128)(2,1)}), bf16[32,12,1920]{2,1,0:T(8,128)(2,1)S(1)}, u32[]{:S(2)}, u32[]{:S(2)}) %all-to-all-start.1) | async-done | bytes 1474592 | tf_op jit(solution)/shard_map/all_to_all | solution.py:77
  62.4 1.3 reshape.140
  63.7 4.4 %fusion.88 = (bf16[384,1920]{1,0:T(8,128)(2,1)S(1)}, f32[384,1920]{1,0:T(8,128)}) fusion(bf16[384,1920]{1,0:T(8,128)(2,1)} %reshape.140, f32[]{:T(128)} %bitcast.1, f32[]{:T(128)} %bitcast, s32[384]{0:T(512)S(1)} %add.113, pred[384]{0:T(512)(128)(4,1)S(1)} %lt.67, pred[384]{0:T(512)(128)(4,1)S(1)} %iota_compare_fusion.13), kind=kOutput, calls=%fused_computation.131 | convolution fusion | flops 570359808 | bytes 5900552 | tf_op jit(solution)/shard_map/dot_general | solution.py:25
  68.1 0.8 slice.86
  68.9 0.7 fusion.51
  69.6 4.9 %custom-call.6 = f32[1,64,64]{1,2,0:T(8,128)S(1)} custom-call(f32[1,64,64]{2,1,0:T(8,128)S(1)} %fusion.51), custom_call_target="InvertDiagBlocksLowerTriangular" | custom-call | tf_op jit(solution)/shard_map/triangular_solve | solution.py:33
  74.5 0.9 fusion.87
  75.4 0.5 collective-permute-start.1
  76.0 0.1 slice.84
  76.0 1.1 fusion.27
  77.2 0.9 copy-done.3
  78.2 0.2 reduce-scatter.2.cloned.1.call-start
  78.4 1.2 slice_reduce_fusion
  79.7 1.3 convolution_bitcast_fusion
  81.0 1.1 convolution_bitcast_fusion.1
  82.1 2.8 %fusion.91 = f32[1920,64]{0,1:T(8,128)S(1)} fusion(f32[384,1920]{1,0:T(8,128)S(1)} %copy-done.1, f32[64,384]{1,0:T(8,128)} %get-tuple-element.35), kind=kOutput, calls=%fused_computation.134 | convolution fusion | flops 566231040 | bytes 3538944 | tf_op jit(solution)/shard_map/dot_general | solution.py:34
  84.9 0.4 convolution_reduce_fusion
  85.3 1.7 fusion.9
  86.9 0.1 collective-permute-start.2
  87.0 1.2 collective-permute-done.2
  88.2 38.0 %psum.7 = f32[1920]{0:T(1024)} all-reduce(f32[1920]{0:T(1024)S(1)} %add.122), channel_id=1, replica_groups=mesh['tmc'=16,'core'=2,'panel'=4] {'tmc'}, use_global_device_ids=true, to_apply=%region_8.9 | all-reduce | flops 1920 | bytes 15360 | tf_op jit(solution)/shard_map/psum | solution.py:103
  126.2 0.1 slice.90
  126.3 0.8 slice.91
  127.1 0.9 fusion.42
  128.0 3.4 %fusion.45 = f32[128,7680]{1,0:T(8,128)S(1)} fusion(bf16[272,7680]{1,0:T(8,128)(2,1)} %all-gather.2.cloned.1.call-done, bf16[128,544]{1,0:T(8,128)(2,1)S(1)} %fusion.42), kind=kOutput, calls=%fused_computation.66 | convolution fusion | flops 534773760 | bytes 8208384 | tf_op jit(solution)/shard_map/dot_general | solution.py:124
  131.4 2.3 collective-permute-done.3
  133.7 3.4 %fusion.89 = (bf16[128,7680]{1,0:T(8,128)(2,1)S(1)}, bf16[128,7680]{1,0:T(8,128)(2,1)S(1)}) fusion(f32[128,7680]{1,0:T(8,128)S(1)} %fusion.45, bf16[272,7680]{1,0:T(8,128)(2,1)} %collective-permute-done.3, bf16[128,544]{1,0:T(8,128)(2,1)S(1)} %fusion.42), kind=kOutput, calls=%fused_computation.132 | convolution fusion | flops 537722880 | bytes 12140544 | tf_op jit(solution)/shard_map/dot_general | solution.py:125
  137.1 18.1 %multiply_convert_fusion = bf16[7680,960]{1,0:T(8,128)(2,1)} fusion(bf16[272,7680]{1,0:T(8,128)(2,1)} %collective-permute-done.3, bf16[272,7680]{1,0:T(8,128)(2,1)S(1)} %copy-done.2, bf16[128,7680]{1,0:T(8,128)(2,1)S(1)} %get-tuple-element.36, s32[]{:T(128)S(6)} %select_n.63, bf16[128,7680]{1,0:T(8,128)(2,1)S(1)} %get-tuple-element.37), kind=kOutput, calls=%fused_computation | convolution fusion | flops 9958625280 | bytes 35389444 | tf_op jit(solution)/shard_map/dot_general | solution.py:132
  155.3 103.6 %reduce-scatter.2.cloned.1.call-done = bf16[480,960]{1,0:T(8,128)(2,1)} async-done(((bf16[7680,960]{1,0:T(8,128)(2,1)}), bf16[480,960]{1,0:T(8,128)(2,1)}) %reduce-scatter.2.cloned.1.call-update) | async-done | bytes 921616 | tf_op jit(solution)/shard_map/reduce_scatter | solution.py:135
  258.9 1.1 dynamic-slice_bitcast_fusion
  259.9 0.1 collective-permute-start.4
  260.0 1.8 collective-permute-done.4
  261.9 1.1 bitcast_select_fusion.1
  263.0 1.5 maximum_convert_fusion
  (42 shorter events, 0.5 us)
Async XLA Ops:
  7.2 14.8 %copy-start = (bf16[256,1920]{1,0:T(8,128)(2,1)S(1)}, bf16[256,1920]{1,0:T(8,128)(2,1)}, u32[]{:S(2)}) copy-start(bf16[256,1920]{1,0:T(8,128)(2,1)} %param.8) | copy-start | bytes 2949124
  13.7 15.7 %all-to-all-start = ((bf16[32,2,390]{2,1,0:T(2,128)(2,1)}), bf16[32,2,390]{2,1,0:T(2,128)(2,1)S(1)}, u32[]{:S(2)}, u32[]{:S(2)}) async-start(bf16[32,2,390]{2,1,0:T(2,128)(2,1)} %reshape.169), calls=%async_computation | async-start | bytes 131072 | tf_op jit(solution)/shard_map/all_to_all | solution.py:75
  22.0 2.1 copy-start.9
  22.0 2.8 %copy-start.10 = (f32[32]{0:T(128)S(1)}, f32[32]{0:T(128)}, u32[]{:S(2)}) copy-start(f32[32]{0:T(128)} %param.12) | copy-start | bytes 388
  27.4 36.3 %copy-start.7 = (pred[384]{0:T(512)(128)(4,1)}, pred[384]{0:T(512)(128)(4,1)S(1)}, u32[]{:S(2)}) copy-start(pred[384]{0:T(512)(128)(4,1)S(1)} %lt.67) | copy-start | bytes 1156
  29.6 32.8 %all-to-all-start.1 = ((bf16[32,12,1920]{2,1,0:T(8,128)(2,1)}), bf16[32,12,1920]{2,1,0:T(8,128)(2,1)S(1)}, u32[]{:S(2)}, u32[]{:S(2)}) async-start(bf16[32,12,1920]{2,1,0:T(8,128)(2,1)} %reshape.138), calls=%async_computation.1 | async-start | bytes 3932160 | tf_op jit(solution)/shard_map/all_to_all | solution.py:77
  35.0 91.3 %all-gather.2.cloned.1.call-start = ((), (), s32[]{:S(2)}) async-start(), calls=%async_computation.3 | async-start | bytes 5222400 | tf_op jit(solution)/shard_map/all_gather | solution.py:102
  36.5 27.2 %copy-start.8 = (pred[384]{0:T(512)(128)(4,1)}, pred[384]{0:T(512)(128)(4,1)S(1)}, u32[]{:S(2)}) copy-start(pred[384]{0:T(512)(128)(4,1)S(1)} %iota_compare_fusion.13) | copy-start | bytes 1156
  36.6 25.9 %copy-start.6 = (bf16[384,65]{1,0:T(8,128)(2,1)}, bf16[384,65]{1,0:T(8,128)(2,1)S(1)}, u32[]{:S(2)}) copy-start(bf16[384,65]{1,0:T(8,128)(2,1)S(1)} %reshape.141) | copy-start | bytes 149764
  37.2 0.7 copy-start.4
  63.7 10.8 %copy-start.5 = (f32[384,64]{0,1:T(8,128)S(1)}, f32[384,64]{0,1:T(8,128)}, u32[]{:S(2)}) copy-start(f32[384,64]{0,1:T(8,128)} %copy-done.4) | copy-start | bytes 294916
  68.9 7.1 %collective-permute-start = (bf16[112,1920]{1,0:T(8,128)(2,1)}, bf16[112,1920]{1,0:T(8,128)(2,1)}, u32[]{:S(2)}, u32[]{:S(2)}) collective-permute-start(bf16[112,1920]{1,0:T(8,128)(2,1)} %slice.86), channel_id=1, source_target_pairs={{0,4},{4,0},{1,5},{5,1},{2,6},{6,2},{3,7},{7,3},{8,12},{12,8},{9,1... | collective-permute-start | bytes 1290248 | tf_op jit(solution)/shard_map/ppermute | solution.py:98
  75.4 1.8 collective-permute-start.1
  77.2 1.0 copy-start.3
  78.2 180.7 %reduce-scatter.2.cloned.1.call-start = ((), (), s32[]{:S(2)}) async-start(), calls=%async_computation.4 | async-start | bytes 16711680 | tf_op jit(solution)/shard_map/reduce_scatter | solution.py:135
  78.4 3.7 %copy-start.1 = (f32[384,1920]{1,0:T(8,128)S(1)}, f32[384,1920]{1,0:T(8,128)}, u32[]{:S(2)}) copy-start(f32[384,1920]{1,0:T(8,128)} %get-tuple-element.34) | copy-start | bytes 8847364
  86.9 1.3 collective-permute-start.2
  126.2 7.5 %collective-permute-start.3 = (bf16[272,7680]{1,0:T(8,128)(2,1)}, bf16[272,7680]{1,0:T(8,128)(2,1)}, u32[]{:S(2)}, u32[]{:S(2)}) collective-permute-start(bf16[272,7680]{1,0:T(8,128)(2,1)} %all-gather.2.cloned.1.call-done), channel_id=1, source_target_pairs={{0,4},{4,0},{1,5},{5,1},{2,6},{6,2},{3,7},{7,3},{8,12},{12,8},{9,1... | collective-permute-start | bytes 12533768 | tf_op jit(solution)/shard_map/ppermute | solution.py:106
  131.4 5.8 %copy-start.2 = (bf16[272,7680]{1,0:T(8,128)(2,1)S(1)}, bf16[272,7680]{1,0:T(8,128)(2,1)}, u32[]{:S(2)}) copy-start(bf16[272,7680]{1,0:T(8,128)(2,1)} %all-gather.2.cloned.1.call-done) | copy-start | bytes 12533764
  259.9 1.9 collective-permute-start.4
Sparse Core Ops, SparseCore 0:
  78.3 43.4 all-gather.1
  155.4 103.4 reduce-scatter.1

commit v17 on v15

--- a/solution.py
+++ b/solution.py
@@ -122,7 +122,8 @@
     ).astype(jnp.bfloat16)
     design_side = jnp.concatenate([gathered, got_rows], axis=0)
     own_share = jnp.dot(stacked_basis[:, :keep], gathered, preferred_element_type=jnp.float32)
-    far_share = jnp.dot(stacked_basis[:, keep:], got_rows, preferred_element_type=jnp.float32)
+    far_share = lax.ppermute(own_share, "core", swap)
+    far_share = jnp.concatenate([far_share[own_lead.shape[0] :], far_share[: own_lead.shape[0]]], axis=0)
     terms = (own_share + far_share).astype(jnp.bfloat16)
     row_side = jnp.concatenate([design_side, -terms], axis=0)
     col_side = lax.dynamic_slice_in_dim(

time: 270 us -> 278 us (1.030)
  waiting for transfers between devices: 133 us -> 137 us
    ppermute x0 -> x1, waiting for transfers between devices: none -> 6.62 us  [body(): far_share = lax.ppermute(own_share, 'core', swap)]
    dot_general x1 -> x0, matrix products: 3.42 us -> none  [body(): jnp.dot(stacked_basis[:, keep:], got_rows, preferred_element_type=jnp.flo...]
    ppermute x1, waiting for transfers between devices: 3.83 us -> 0.95 us  [body(): got_rows = lax.ppermute(gathered, 'core', swap)]
  transfers between devices with their start and end apart: 9 -> 10, of which waited for: 7 -> 8; matrix products, arithmetic and copies ran while one was open for 11% -> 12% of each run, Pallas kernels for 0% -> 0%
where the time goes in v17:
time: 278 us; the launch traced here: 276 us
  waiting for transfers between devices  137 us (49%)
  blocking collectives  38 us (14%)
  matrix products  34.4 us (12%)
  other arithmetic  21.9 us (8%)
  starting transfers between devices  17 us (6%)
  between operations  16.3 us (6%)
  local copies, waits for them, and re-layouts  12 us (4%)
    reduce_scatter x1, waiting for transfers between devices, body(): lax.psum_scatter((product * scale).astype(jnp.bfloat16), 'tmc', scatter_d...  108 us
    psum x1, blocking collectives, body(): lax.psum(right_part + lax.ppermute(right_part, 'core', swap), 'tmc')  38 us
    dot_general x1, matrix products, body(): lax.dot_general(row_side, col_side, (((0,), (0,)), ((), ())), preferred_e...  18.9 us
    all_to_all x1, waiting for transfers between devices, body(): lax.all_to_all(send_design, TM, split_axis=0, concat_axis=0, tiled=True)  13.6 us
    all_to_all x1, starting transfers between devices, body(): lax.all_to_all(send_params, TM, split_axis=0, concat_axis=0, tiled=True)  8.16 us
    all_to_all x1, starting transfers between devices, body(): lax.all_to_all(send_design, TM, split_axis=0, concat_axis=0, tiled=True)  6.93 us
    ppermute x1, waiting for transfers between devices, body(): far_share = lax.ppermute(own_share, 'core', swap)  6.62 us
    another operation x3, other arithmetic, eliminate(): factor = jnp.linalg.cholesky(param_gram)  6.52 us
  transfers between devices with their start and end apart: 10, of which 8 were waited for; matrix products, arithmetic and copies ran while one was open for 12% of the time, Pallas kernels for 0%

profile of v17, /device:TPU:24, one launch (start us, length us, event | category | flops | bytes accessed | tf_op | source)
XLA Modules:
  0.0 276.1 jit_solution(4602261752720988438)
XLA Ops:
  7.2 0.5 broadcast.213
  7.7 2.3 fusion.64
  10.0 0.1 reshape_squeeze.3
  10.0 0.2 dynamic-slice_reduce_fusion
  10.2 0.6 reduce-window.6
  10.8 0.2 slice_reduce_fusion.1
  11.1 0.1 fusion.68
  11.2 0.7 broadcast_in_dim.12
  11.8 1.0 convolution_convert_fusion.1
  12.8 0.1 copy.13
  13.0 0.8 reshape.169
  13.8 8.2 %all-to-all-start = ((bf16[32,2,390]{2,1,0:T(2,128)(2,1)}), bf16[32,2,390]{2,1,0:T(2,128)(2,1)S(1)}, u32[]{:S(2)}, u32[]{:S(2)}) async-start(bf16[32,2,390]{2,1,0:T(2,128)(2,1)} %reshape.169), calls=%async_computation | async-start | bytes 131072 | tf_op jit(solution)/shard_map/all_to_all | solution.py:75
  22.0 0.6 convolution_convert_fusion
  22.7 0.7 and_select_fusion
  23.5 0.7 iota_compare_fusion.11
  24.1 1.5 reshape.138
  25.6 0.6 dynamic_slice.20
  26.2 0.6 dynamic_slice.19
  28.8 0.1 lt.67
  28.9 0.1 add.113
  29.0 0.5 all-to-all-done
  29.5 0.2 reshape.170
  29.7 0.7 fusion.28
  30.4 0.2 fusion.109
  30.6 0.1 copy.14
  30.7 6.9 %all-to-all-start.1 = ((bf16[32,12,1920]{2,1,0:T(8,128)(2,1)}), bf16[32,12,1920]{2,1,0:T(8,128)(2,1)S(1)}, u32[]{:S(2)}, u32[]{:S(2)}) async-start(bf16[32,12,1920]{2,1,0:T(8,128)(2,1)} %reshape.138), calls=%async_computation.1 | async-start | bytes 3932160 | tf_op jit(solution)/shard_map/all_to_all | solution.py:77
  37.7 5.8 %cholesky.17 = f32[64,64]{1,0:T(8,128)S(1)} custom-call(f32[64,64]{1,0:T(8,128)S(1)} %fusion.72), custom_call_target="Cholesky" | custom-call | tf_op jit(solution)/shard_map/jit(cholesky)/cholesky | solution.py:32
  43.6 0.6 compare_reduce_fusion
  44.2 0.7 fusion.63
  44.9 4.9 %custom-call.6 = f32[1,64,64]{1,2,0:T(8,128)S(1)} custom-call(f32[1,64,64]{2,1,0:T(8,128)S(1)} %fusion.63), custom_call_target="InvertDiagBlocksLowerTriangular" | custom-call | tf_op jit(solution)/shard_map/triangular_solve | solution.py:33
  49.8 0.2 slice_reduce_fusion
  50.0 0.3 fusion.107
  50.3 0.4 collective-permute-start.1
  50.7 0.6 convolution_bitcast_fusion
  51.3 0.2 convolution_bitcast_fusion.1
  51.5 13.6 %all-to-all-done.1 = bf16[32,12,1920]{2,1,0:T(8,128)(2,1)S(1)} async-done(((bf16[32,12,1920]{2,1,0:T(8,128)(2,1)}), bf16[32,12,1920]{2,1,0:T(8,128)(2,1)S(1)}, u32[]{:S(2)}, u32[]{:S(2)}) %all-to-all-start.1) | async-done | bytes 1474592 | tf_op jit(solution)/shard_map/all_to_all | solution.py:77
  65.1 1.3 reshape.140
  66.4 2.8 %fusion.108 = (bf16[384,1920]{1,0:T(8,128)(2,1)S(1)}, f32[384,1920]{1,0:T(8,128)S(1)}) fusion(bf16[384,1920]{1,0:T(8,128)(2,1)} %reshape.140, f32[]{:T(128)} %bitcast.1, f32[]{:T(128)} %bitcast, s32[384]{0:T(512)S(1)} %add.113, pred[384]{0:T(512)(128)(4,1)S(1)} %lt.67, pred[384]{0:T(512)(128)(4,1)S(1)} %iota_compare_fusion.11), kind=kOutput, calls=%fused_computation.145 | convolution fusion | flops 570359808 | bytes 5900552 | tf_op jit(solution)/shard_map/dot_general | solution.py:25
  69.2 0.1 slice.88
  69.3 1.8 fusion.110
  71.2 0.3 collective-permute-start
  71.4 0.4 convolution_reduce_fusion
  71.8 1.7 fusion.9
  73.5 0.1 fusion.27
  73.7 0.9 copy-done.1
  74.7 0.6 collective-permute-start.2
  75.3 0.1 slice.94
  75.3 0.1 slice.95
  75.4 0.7 collective-permute-done.2
  76.1 38.0 %psum.7 = f32[1920]{0:T(1024)} all-reduce(f32[1920]{0:T(1024)S(1)} %add.122), channel_id=1, replica_groups=mesh['tmc'=16,'core'=2,'panel'=4] {'tmc'}, use_global_device_ids=true, to_apply=%region_8.9 | all-reduce | flops 1920 | bytes 15360 | tf_op jit(solution)/shard_map/psum | solution.py:103
  114.1 4.3 %all-gather.2.cloned.1.call-done = bf16[272,7680]{1,0:T(8,128)(2,1)} async-done(((bf16[272,1920]{1,0:T(8,128)(2,1)}), bf16[272,7680]{1,0:T(8,128)(2,1)}) %all-gather.2.cloned.1.call-update) | async-done | bytes 4177936 | tf_op jit(solution)/shard_map/all_gather | solution.py:102
  118.4 5.3 %fusion.45 = f32[128,7680]{1,0:T(8,128)} fusion(bf16[272,7680]{1,0:T(8,128)(2,1)} %all-gather.2.cloned.1.call-done, bf16[64,272]{1,0:T(8,128)(2,1)S(1)} %bitcast.71, bf16[64,272]{1,0:T(8,128)(2,1)S(1)} %bitcast.70, bf16[64,112]{1,0:T(8,128)(2,1)S(1)} %slice.95, bf16[64,112]{1,0:T(8,128)(2,1)S(1)} %slice.94), kind=kOutput, calls=%fused_computation.65 | convolution fusion | flops 535435264 | bytes 8208384 | tf_op jit(solution)/shard_map/dot_general | solution.py:124
  123.7 0.5 collective-permute-start.3
  124.2 6.6 %collective-permute-done.4 = f32[128,7680]{1,0:T(8,128)} collective-permute-done((f32[128,7680]{1,0:T(8,128)}, f32[128,7680]{1,0:T(8,128)}, u32[]{:S(2)}, u32[]{:S(2)}) %collective-permute-start.4) | collective-permute-done | bytes 3932192 | tf_op jit(solution)/shard_map/ppermute | solution.py:125
  130.8 2.4 fusion.106
  133.2 2.6 fusion.104
  135.8 1.0 collective-permute-done.3
  136.8 18.9 %multiply_convert_fusion = bf16[7680,960]{1,0:T(8,128)(2,1)} fusion(bf16[272,7680]{1,0:T(8,128)(2,1)} %collective-permute-done.3, bf16[272,7680]{1,0:T(8,128)(2,1)} %all-gather.2.cloned.1.call-done, bf16[128,7680]{1,0:T(8,128)(2,1)S(1)} %get-tuple-element.31, s32[]{:T(128)S(6)} %select_n.63, bf16[128,7680]{1,0:T(8,128)(2,1)S(1)} %get-tuple-element.32), kind=kOutput, calls=%fused_computation | convolution fusion | flops 9958625280 | bytes 35389444 | tf_op jit(solution)/shard_map/dot_general | solution.py:133
  155.7 108.0 %reduce-scatter.2.cloned.1.call-done = bf16[480,960]{1,0:T(8,128)(2,1)} async-done(((bf16[7680,960]{1,0:T(8,128)(2,1)}), bf16[480,960]{1,0:T(8,128)(2,1)}) %reduce-scatter.2.cloned.1.call-update) | async-done | bytes 921616 | tf_op jit(solution)/shard_map/reduce_scatter | solution.py:136
  263.7 1.1 dynamic-slice_bitcast_fusion
  264.8 0.1 collective-permute-start.5
  264.9 1.8 collective-permute-done.5
  266.7 1.1 bitcast_select_fusion.1
  267.8 1.5 maximum_convert_fusion
  (30 shorter events, 0.6 us)
Async XLA Ops:
  7.2 14.9 %copy-start = (bf16[256,1920]{1,0:T(8,128)(2,1)S(1)}, bf16[256,1920]{1,0:T(8,128)(2,1)}, u32[]{:S(2)}) copy-start(bf16[256,1920]{1,0:T(8,128)(2,1)} %param.8) | copy-start | bytes 2949124
  13.8 15.7 %all-to-all-start = ((bf16[32,2,390]{2,1,0:T(2,128)(2,1)}), bf16[32,2,390]{2,1,0:T(2,128)(2,1)S(1)}, u32[]{:S(2)}, u32[]{:S(2)}) async-start(bf16[32,2,390]{2,1,0:T(2,128)(2,1)} %reshape.169), calls=%async_computation | async-start | bytes 131072 | tf_op jit(solution)/shard_map/all_to_all | solution.py:75
  22.0 3.6 %copy-start.2 = (f32[32]{0:T(128)S(1)}, f32[32]{0:T(128)}, u32[]{:S(2)}) copy-start(f32[32]{0:T(128)} %param.13) | copy-start | bytes 388
  22.0 4.2 %copy-start.3 = (f32[32]{0:T(128)S(1)}, f32[32]{0:T(128)}, u32[]{:S(2)}) copy-start(f32[32]{0:T(128)} %param.12) | copy-start | bytes 388
  30.7 34.4 %all-to-all-start.1 = ((bf16[32,12,1920]{2,1,0:T(8,128)(2,1)}), bf16[32,12,1920]{2,1,0:T(8,128)(2,1)S(1)}, u32[]{:S(2)}, u32[]{:S(2)}) async-start(bf16[32,12,1920]{2,1,0:T(8,128)(2,1)} %reshape.138), calls=%async_computation.1 | async-start | bytes 3932160 | tf_op jit(solution)/shard_map/all_to_all | solution.py:77
  37.7 80.8 %all-gather.2.cloned.1.call-start = ((), (), s32[]{:S(2)}) async-start(), calls=%async_computation.3 | async-start | bytes 5222400 | tf_op jit(solution)/shard_map/all_gather | solution.py:102
  50.3 23.3 %collective-permute-start.1 = (bf16[64,384]{1,0:T(8,128)(2,1)S(1)}, bf16[64,384]{1,0:T(8,128)(2,1)S(1)}, u32[]{:S(2)}, u32[]{:S(2)}) collective-permute-start(bf16[64,384]{1,0:T(8,128)(2,1)S(1)} %get-tuple-element.37), channel_id=1, source_target_pairs={{0,4},{4,0},{1,5},{5,1},{2,6},{6,2},{3,7},{7,3},{8,12},{12,8},{9,1... | collective-permute-start | bytes 147464 | tf_op jit(solution)/shard_map/ppermute | solution.py:100
  71.2 2.4 collective-permute-start
  73.7 1.0 copy-start.1
  74.6 189.1 %reduce-scatter.2.cloned.1.call-start = ((), (), s32[]{:S(2)}) async-start(), calls=%async_computation.4 | async-start | bytes 16711680 | tf_op jit(solution)/shard_map/reduce_scatter | solution.py:136
  74.7 1.4 collective-permute-start.2
  123.7 7.1 %collective-permute-start.4 = (f32[128,7680]{1,0:T(8,128)}, f32[128,7680]{1,0:T(8,128)}, u32[]{:S(2)}, u32[]{:S(2)}) collective-permute-start(f32[128,7680]{1,0:T(8,128)} %fusion.45), channel_id=1, source_target_pairs={{0,4},{4,0},{1,5},{5,1},{2,6},{6,2},{3,7},{7,3},{8,12},{12,8},{9,1... | collective-permute-start | bytes 11796488 | tf_op jit(solution)/shard_map/ppermute | solution.py:125
  123.7 13.1 %collective-permute-start.3 = (bf16[272,7680]{1,0:T(8,128)(2,1)}, bf16[272,7680]{1,0:T(8,128)(2,1)}, u32[]{:S(2)}, u32[]{:S(2)}) collective-permute-start(bf16[272,7680]{1,0:T(8,128)(2,1)} %all-gather.2.cloned.1.call-done), channel_id=1, source_target_pairs={{0,4},{4,0},{1,5},{5,1},{2,6},{6,2},{3,7},{7,3},{8,12},{12,8},{9,1... | collective-permute-start | bytes 12533768 | tf_op jit(solution)/shard_map/ppermute | solution.py:106
  264.8 1.9 collective-permute-start.5
Sparse Core Ops, SparseCore 0:
  74.8 43.6 all-gather.1
  155.8 107.8 reduce-scatter.1

commit v18 on v15

--- a/solution.py
+++ b/solution.py
@@ -55,11 +55,9 @@
     arc_ids = arc_of_row[:, 0]
     epoch_table = arc_ids.reshape(rows_dev, tile_count)
     local_arcs = lax.dynamic_slice_in_dim(epoch_table, device_index, 1, 1)[:, 0]
-    onehot = (local_arcs[:, None] == jnp.arange(tile_count, dtype=jnp.int32)[None, :]).astype(
-        jnp.int32
-    )
-    earlier = jnp.cumsum(onehot, axis=0) - onehot
-    within = jnp.sum(earlier * onehot, axis=1)
+    row_id = jnp.arange(rows_dev, dtype=jnp.int32)
+    same_arc = local_arcs[:, None] == local_arcs[None, :]
+    within = jnp.sum((same_arc & (row_id[None, :] < row_id[:, None])).astype(jnp.int32), axis=1)
     target_slot = local_arcs * capacity + within
     chooser = (
         target_slot[None, :] == jnp.arange(slot_count, dtype=jnp.int32)[:, None]

time: 270 us -> 269 us (level)
  no operation moved by 1% of the time
where the time goes in v18:
time: 269 us; the launch traced here: 267 us
  waiting for transfers between devices  133 us (49%)
  blocking collectives  38 us (14%)
  matrix products  35.2 us (13%)
  other arithmetic  18.9 us (7%)
  starting transfers between devices  16.5 us (6%)
  between operations  16.3 us (6%)
  local copies, waits for them, and re-layouts  9.39 us (3%)
    reduce_scatter x1, waiting for transfers between devices, body(): lax.psum_scatter((product * scale).astype(jnp.bfloat16), 'tmc', scatter_d...  108 us
    psum x1, blocking collectives, body(): lax.psum(right_part + lax.ppermute(right_part, 'core', swap), 'tmc')  38 us
    dot_general x1, matrix products, body(): lax.dot_general(row_side, col_side, (((0,), (0,)), ((), ())), preferred_e...  18.1 us
    all_to_all x1, waiting for transfers between devices, body(): lax.all_to_all(send_design, TM, split_axis=0, concat_axis=0, tiled=True)  13.6 us
    all_to_all x1, starting transfers between devices, body(): lax.all_to_all(send_params, TM, split_axis=0, concat_axis=0, tiled=True)  8.17 us
    all_to_all x1, starting transfers between devices, body(): lax.all_to_all(send_design, TM, split_axis=0, concat_axis=0, tiled=True)  6.94 us
    another operation x3, other arithmetic, eliminate(): factor = jnp.linalg.cholesky(param_gram)  6.52 us
    another operation x2, other arithmetic, eliminate(): lax.linalg.triangular_solve(factor, white_params.T, left_side=True, lower...  5.55 us
  transfers between devices with their start and end apart: 9, of which 7 were waited for; matrix products, arithmetic and copies ran while one was open for 11% of the time, Pallas kernels for 0%

profile of v18, /device:TPU:24, one launch (start us, length us, event | category | flops | bytes accessed | tf_op | source)
XLA Modules:
  0.0 267.2 jit_solution(6713833910988469327)
XLA Ops:
  7.2 0.5 broadcast.170
  7.7 2.3 fusion.53
  10.0 0.1 reshape_squeeze.3
  10.0 0.2 dynamic-slice_reduce_fusion
  10.2 0.2 convert_reduce_fusion
  10.4 0.7 broadcast_in_dim.12
  11.1 1.0 convolution_convert_fusion.1
  12.1 0.1 copy.13
  12.2 0.8 reshape.151
  13.0 8.2 %all-to-all-start = ((bf16[32,2,390]{2,1,0:T(2,128)(2,1)}), bf16[32,2,390]{2,1,0:T(2,128)(2,1)S(1)}, u32[]{:S(2)}, u32[]{:S(2)}) async-start(bf16[32,2,390]{2,1,0:T(2,128)(2,1)} %reshape.151), calls=%async_computation | async-start | bytes 131072 | tf_op jit(solution)/shard_map/all_to_all | solution.py:73
  21.2 0.1 convert_reduce_fusion.1
  21.3 0.6 convolution_convert_fusion
  21.9 0.1 iota_compare_fusion.11
  22.0 0.7 and_select_fusion
  22.7 0.1 broadcast_add_fusion
  22.7 0.7 iota_compare_fusion.12
  23.4 1.5 reshape.122
  24.9 0.6 dynamic_slice.20
  25.4 0.6 dynamic_slice.19
  28.0 0.1 lt.80
  28.2 0.1 add.113
  28.3 0.5 all-to-all-done
  28.7 0.2 reshape.152
  29.0 0.7 fusion.34
  29.6 0.2 fusion.87
  29.9 0.1 copy.14
  30.0 6.9 %all-to-all-start.1 = ((bf16[32,12,1920]{2,1,0:T(8,128)(2,1)}), bf16[32,12,1920]{2,1,0:T(8,128)(2,1)S(1)}, u32[]{:S(2)}, u32[]{:S(2)}) async-start(bf16[32,12,1920]{2,1,0:T(8,128)(2,1)} %reshape.122), calls=%async_computation.1 | async-start | bytes 3932160 | tf_op jit(solution)/shard_map/all_to_all | solution.py:75
  37.0 5.8 %cholesky.17 = f32[64,64]{1,0:T(8,128)S(1)} custom-call(f32[64,64]{1,0:T(8,128)S(1)} %fusion.58), custom_call_target="Cholesky" | custom-call | tf_op jit(solution)/shard_map/jit(cholesky)/cholesky | solution.py:32
  42.9 0.6 compare_reduce_fusion
  43.5 0.7 fusion.52
  44.2 4.9 %custom-call.6 = f32[1,64,64]{1,2,0:T(8,128)S(1)} custom-call(f32[1,64,64]{2,1,0:T(8,128)S(1)} %fusion.52), custom_call_target="InvertDiagBlocksLowerTriangular" | custom-call | tf_op jit(solution)/shard_map/triangular_solve | solution.py:33
  49.1 0.2 slice_reduce_fusion
  49.3 0.3 fusion.84
  49.6 0.4 collective-permute-start.1
  49.9 0.6 convolution_bitcast_fusion
  50.6 0.2 convolution_bitcast_fusion.1
  50.8 13.6 %all-to-all-done.1 = bf16[32,12,1920]{2,1,0:T(8,128)(2,1)S(1)} async-done(((bf16[32,12,1920]{2,1,0:T(8,128)(2,1)}), bf16[32,12,1920]{2,1,0:T(8,128)(2,1)S(1)}, u32[]{:S(2)}, u32[]{:S(2)}) %all-to-all-start.1) | async-done | bytes 1474592 | tf_op jit(solution)/shard_map/all_to_all | solution.py:75
  64.4 1.3 reshape.124
  65.7 2.8 %fusion.85 = (bf16[384,1920]{1,0:T(8,128)(2,1)S(1)}, f32[384,1920]{1,0:T(8,128)S(1)}) fusion(bf16[384,1920]{1,0:T(8,128)(2,1)} %reshape.124, f32[]{:T(128)} %bitcast.1, f32[]{:T(128)} %bitcast, s32[384]{0:T(512)S(1)} %add.113, pred[384]{0:T(512)(128)(4,1)S(1)} %lt.80, pred[384]{0:T(512)(128)(4,1)S(1)} %iota_compare_fusion.12), kind=kOutput, calls=%fused_computation.125 | convolution fusion | flops 570359808 | bytes 5900552 | tf_op jit(solution)/shard_map/dot_general | solution.py:25
  68.4 0.1 slice.75
  68.6 1.8 fusion.88
  70.4 0.3 collective-permute-start
  70.7 0.4 convolution_reduce_fusion
  71.1 1.7 fusion.9
  72.8 0.1 fusion.27
  72.9 0.9 copy-done.2
  73.9 0.0 reduce-scatter.2.cloned.1.call-start
  73.9 0.6 collective-permute-start.2
  74.5 0.8 collective-permute-done.2
  75.4 38.0 %psum.7 = f32[1920]{0:T(1024)} all-reduce(f32[1920]{0:T(1024)S(1)} %add.122), channel_id=1, replica_groups=mesh['tmc'=16,'core'=2,'panel'=4] {'tmc'}, use_global_device_ids=true, to_apply=%region_6.7 | all-reduce | flops 1920 | bytes 15360 | tf_op jit(solution)/shard_map/psum | solution.py:101
  113.4 4.3 %all-gather.2.cloned.1.call-done = bf16[272,7680]{1,0:T(8,128)(2,1)} async-done(((bf16[272,1920]{1,0:T(8,128)(2,1)}), bf16[272,7680]{1,0:T(8,128)(2,1)}) %all-gather.2.cloned.1.call-update) | async-done | bytes 4177936 | tf_op jit(solution)/shard_map/all_gather | solution.py:100
  117.7 0.1 slice.81
  117.7 0.1 slice.82
  117.8 0.1 fusion.43
  117.9 3.4 %fusion.46 = f32[128,7680]{1,0:T(8,128)S(1)} fusion(bf16[272,7680]{1,0:T(8,128)(2,1)} %all-gather.2.cloned.1.call-done, bf16[128,544]{1,0:T(8,128)(2,1)S(1)} %fusion.43), kind=kOutput, calls=%fused_computation.69 | convolution fusion | flops 534773760 | bytes 8208384 | tf_op jit(solution)/shard_map/dot_general | solution.py:122
  121.3 3.8 %collective-permute-done.3 = bf16[272,7680]{1,0:T(8,128)(2,1)} collective-permute-done((bf16[272,7680]{1,0:T(8,128)(2,1)}, bf16[272,7680]{1,0:T(8,128)(2,1)}, u32[]{:S(2)}, u32[]{:S(2)}) %collective-permute-start.3) | collective-permute-done | bytes 4177952 | tf_op jit(solution)/shard_map/ppermute | solution.py:104
  125.1 3.4 %fusion.86 = (bf16[128,7680]{1,0:T(8,128)(2,1)S(1)}, bf16[128,7680]{1,0:T(8,128)(2,1)S(1)}) fusion(f32[128,7680]{1,0:T(8,128)S(1)} %fusion.46, bf16[272,7680]{1,0:T(8,128)(2,1)} %collective-permute-done.3, bf16[128,544]{1,0:T(8,128)(2,1)S(1)} %fusion.43), kind=kOutput, calls=%fused_computation.126 | convolution fusion | flops 537722880 | bytes 12140544 | tf_op jit(solution)/shard_map/dot_general | solution.py:123
  128.6 18.1 %multiply_convert_fusion = bf16[7680,960]{1,0:T(8,128)(2,1)} fusion(bf16[272,7680]{1,0:T(8,128)(2,1)} %collective-permute-done.3, bf16[272,7680]{1,0:T(8,128)(2,1)S(1)} %copy-done.1, bf16[128,7680]{1,0:T(8,128)(2,1)S(1)} %get-tuple-element.38, s32[]{:T(128)S(6)} %select_n.63, bf16[128,7680]{1,0:T(8,128)(2,1)S(1)} %get-tuple-element.39), kind=kOutput, calls=%fused_computation | convolution fusion | flops 9958625280 | bytes 35389444 | tf_op jit(solution)/shard_map/dot_general | solution.py:130
  146.7 108.0 %reduce-scatter.2.cloned.1.call-done = bf16[480,960]{1,0:T(8,128)(2,1)} async-done(((bf16[7680,960]{1,0:T(8,128)(2,1)}), bf16[480,960]{1,0:T(8,128)(2,1)}) %reduce-scatter.2.cloned.1.call-update) | async-done | bytes 921616 | tf_op jit(solution)/shard_map/reduce_scatter | solution.py:133
  254.7 1.1 dynamic-slice_bitcast_fusion
  255.8 0.1 collective-permute-start.4
  255.9 1.8 collective-permute-done.4
  257.8 1.1 bitcast_select_fusion.1
  258.9 1.5 maximum_convert_fusion
  (25 shorter events, 0.3 us)
Async XLA Ops:
  7.2 14.1 %copy-start = (bf16[256,1920]{1,0:T(8,128)(2,1)S(1)}, bf16[256,1920]{1,0:T(8,128)(2,1)}, u32[]{:S(2)}) copy-start(bf16[256,1920]{1,0:T(8,128)(2,1)} %param.8) | copy-start | bytes 2949124
  13.0 15.7 %all-to-all-start = ((bf16[32,2,390]{2,1,0:T(2,128)(2,1)}), bf16[32,2,390]{2,1,0:T(2,128)(2,1)S(1)}, u32[]{:S(2)}, u32[]{:S(2)}) async-start(bf16[32,2,390]{2,1,0:T(2,128)(2,1)} %reshape.151), calls=%async_computation | async-start | bytes 131072 | tf_op jit(solution)/shard_map/all_to_all | solution.py:73
  21.3 3.6 %copy-start.3 = (f32[32]{0:T(128)S(1)}, f32[32]{0:T(128)}, u32[]{:S(2)}) copy-start(f32[32]{0:T(128)} %param.13) | copy-start | bytes 388
  21.3 4.2 %copy-start.4 = (f32[32]{0:T(128)S(1)}, f32[32]{0:T(128)}, u32[]{:S(2)}) copy-start(f32[32]{0:T(128)} %param.12) | copy-start | bytes 388
  30.0 34.4 %all-to-all-start.1 = ((bf16[32,12,1920]{2,1,0:T(8,128)(2,1)}), bf16[32,12,1920]{2,1,0:T(8,128)(2,1)S(1)}, u32[]{:S(2)}, u32[]{:S(2)}) async-start(bf16[32,12,1920]{2,1,0:T(8,128)(2,1)} %reshape.122), calls=%async_computation.1 | async-start | bytes 3932160 | tf_op jit(solution)/shard_map/all_to_all | solution.py:75
  36.9 80.8 %all-gather.2.cloned.1.call-start = ((), (), s32[]{:S(2)}) async-start(), calls=%async_computation.3 | async-start | bytes 5222400 | tf_op jit(solution)/shard_map/all_gather | solution.py:100
  49.6 23.4 %collective-permute-start.1 = (bf16[64,384]{1,0:T(8,128)(2,1)S(1)}, bf16[64,384]{1,0:T(8,128)(2,1)S(1)}, u32[]{:S(2)}, u32[]{:S(2)}) collective-permute-start(bf16[64,384]{1,0:T(8,128)(2,1)S(1)} %get-tuple-element.33), channel_id=1, source_target_pairs={{0,4},{4,0},{1,5},{5,1},{2,6},{6,2},{3,7},{7,3},{8,12},{12,8},{9,1... | collective-permute-start | bytes 147464 | tf_op jit(solution)/shard_map/ppermute | solution.py:98
  70.4 2.4 collective-permute-start
  72.9 1.0 copy-start.2
  73.9 180.8 %reduce-scatter.2.cloned.1.call-start = ((), (), s32[]{:S(2)}) async-start(), calls=%async_computation.4 | async-start | bytes 16711680 | tf_op jit(solution)/shard_map/reduce_scatter | solution.py:133
  73.9 1.4 collective-permute-start.2
  117.7 7.5 %collective-permute-start.3 = (bf16[272,7680]{1,0:T(8,128)(2,1)}, bf16[272,7680]{1,0:T(8,128)(2,1)}, u32[]{:S(2)}, u32[]{:S(2)}) collective-permute-start(bf16[272,7680]{1,0:T(8,128)(2,1)} %all-gather.2.cloned.1.call-done), channel_id=1, source_target_pairs={{0,4},{4,0},{1,5},{5,1},{2,6},{6,2},{3,7},{7,3},{8,12},{12,8},{9,1... | collective-permute-start | bytes 12533768 | tf_op jit(solution)/shard_map/ppermute | solution.py:104
  121.3 7.3 %copy-start.1 = (bf16[272,7680]{1,0:T(8,128)(2,1)S(1)}, bf16[272,7680]{1,0:T(8,128)(2,1)}, u32[]{:S(2)}) copy-start(bf16[272,7680]{1,0:T(8,128)(2,1)} %all-gather.2.cloned.1.call-done) | copy-start | bytes 12533764
  255.8 1.9 collective-permute-start.4
Sparse Core Ops, SparseCore 0:
  74.0 43.5 all-gather.1
  146.9 107.8 reduce-scatter.1

commit v19 on v18

--- a/solution.py
+++ b/solution.py
@@ -135,8 +135,8 @@
     )
     block_rows = pair.shape[0] // core_count
     by_core = pair.reshape(core_count, block_rows, half)
-    mine = lax.dynamic_index_in_dim(by_core, core_index, 0, keepdims=False)
-    given = lax.dynamic_index_in_dim(by_core, 1 - core_index, 0, keepdims=False)
+    mine = jnp.where(core_index == 0, by_core[0], by_core[1])
+    given = jnp.where(core_index == 0, by_core[1], by_core[0])
     got = lax.ppermute(given, "core", swap)
     first = jnp.where(core_index == 0, mine, got)
     second = jnp.where(core_index == 0, got, mine)

time: 269 us -> 269 us (level)
  transfers between devices with their start and end apart: 9 -> 9, of which waited for: 7 -> 7; matrix products, arithmetic and copies ran while one was open for 11% -> 12% of each run, Pallas kernels for 0% -> 0%
where the time goes in v19:
time: 269 us; the launch traced here: 267 us
  waiting for transfers between devices  132 us (49%)
  blocking collectives  38 us (14%)
  matrix products  35.2 us (13%)
  other arithmetic  20.3 us (8%)
  starting transfers between devices  16.6 us (6%)
  between operations  16.4 us (6%)
  local copies, waits for them, and re-layouts  8.41 us (3%)
    reduce_scatter x1, waiting for transfers between devices, body(): lax.psum_scatter((product * scale).astype(jnp.bfloat16), 'tmc', scatter_d...  108 us
    psum x1, blocking collectives, body(): lax.psum(right_part + lax.ppermute(right_part, 'core', swap), 'tmc')  38 us
    dot_general x1, matrix products, body(): lax.dot_general(row_side, col_side, (((0,), (0,)), ((), ())), preferred_e...  18.1 us
    all_to_all x1, waiting for transfers between devices, body(): lax.all_to_all(send_design, TM, split_axis=0, concat_axis=0, tiled=True)  12.6 us
    all_to_all x1, starting transfers between devices, body(): lax.all_to_all(send_params, TM, split_axis=0, concat_axis=0, tiled=True)  8.16 us
    all_to_all x1, starting transfers between devices, body(): lax.all_to_all(send_design, TM, split_axis=0, concat_axis=0, tiled=True)  7.02 us
    another operation x3, other arithmetic, eliminate(): factor = jnp.linalg.cholesky(param_gram)  6.52 us
    another operation x2, other arithmetic, eliminate(): lax.linalg.triangular_solve(factor, white_params.T, left_side=True, lower...  5.55 us
  transfers between devices with their start and end apart: 9, of which 7 were waited for; matrix products, arithmetic and copies ran while one was open for 12% of the time, Pallas kernels for 0%

profile of v19, /device:TPU:24, one launch (start us, length us, event | category | flops | bytes accessed | tf_op | source)
XLA Modules:
  0.0 266.6 jit_solution(4440556200000650307)
XLA Ops:
  7.2 0.7 broadcast_in_dim.12
  7.9 0.5 broadcast.170
  8.5 2.3 fusion.53
  10.7 0.1 reshape_squeeze.3
  10.8 0.2 dynamic-slice_reduce_fusion
  11.0 0.2 convert_reduce_fusion
  11.2 1.0 convolution_convert_fusion.1
  12.2 0.1 copy.13
  12.3 0.8 reshape.152
  13.1 8.2 %all-to-all-start = ((bf16[32,2,390]{2,1,0:T(2,128)(2,1)}), bf16[32,2,390]{2,1,0:T(2,128)(2,1)S(1)}, u32[]{:S(2)}, u32[]{:S(2)}) async-start(bf16[32,2,390]{2,1,0:T(2,128)(2,1)} %reshape.152), calls=%async_computation | async-start | bytes 131072 | tf_op jit(solution)/shard_map/all_to_all | solution.py:73
  21.3 0.1 convert_reduce_fusion.1
  21.4 0.7 and_select_fusion
  22.1 0.1 iota_compare_fusion.11
  22.2 0.6 convolution_convert_fusion
  22.7 0.1 broadcast_add_fusion
  22.8 0.7 iota_compare_fusion.12
  23.5 0.6 dynamic_slice.13
  24.8 0.7 dynamic_slice.12
  26.8 0.1 add.105
  26.9 0.1 lt.73
  27.0 1.5 reshape.124
  28.5 0.4 all-to-all-done
  28.8 0.2 reshape.153
  29.0 7.0 %all-to-all-start.1 = ((bf16[32,12,1920]{2,1,0:T(8,128)(2,1)}), bf16[32,12,1920]{2,1,0:T(8,128)(2,1)S(1)}, u32[]{:S(2)}, u32[]{:S(2)}) async-start(bf16[32,12,1920]{2,1,0:T(8,128)(2,1)} %reshape.124), calls=%async_computation.1 | async-start | bytes 3932160 | tf_op jit(solution)/shard_map/all_to_all | solution.py:75
  36.1 0.7 fusion.34
  36.8 0.2 fusion.87
  37.1 0.2 slice_reduce_fusion
  37.3 0.1 copy.14
  37.4 5.8 %cholesky.17 = f32[64,64]{1,0:T(8,128)S(1)} custom-call(f32[64,64]{1,0:T(8,128)S(1)} %fusion.58), custom_call_target="Cholesky" | custom-call | tf_op jit(solution)/shard_map/jit(cholesky)/cholesky | solution.py:32
  43.3 0.6 compare_reduce_fusion
  43.9 0.7 fusion.52
  44.6 4.9 %custom-call.6 = f32[1,64,64]{1,2,0:T(8,128)S(1)} custom-call(f32[1,64,64]{2,1,0:T(8,128)S(1)} %fusion.52), custom_call_target="InvertDiagBlocksLowerTriangular" | custom-call | tf_op jit(solution)/shard_map/triangular_solve | solution.py:33
  49.5 0.3 fusion.84
  49.8 0.4 collective-permute-start.1
  50.1 0.6 convolution_bitcast_fusion
  50.8 0.2 convolution_bitcast_fusion.1
  51.0 12.6 %all-to-all-done.1 = bf16[32,12,1920]{2,1,0:T(8,128)(2,1)S(1)} async-done(((bf16[32,12,1920]{2,1,0:T(8,128)(2,1)}), bf16[32,12,1920]{2,1,0:T(8,128)(2,1)S(1)}, u32[]{:S(2)}, u32[]{:S(2)}) %all-to-all-start.1) | async-done | bytes 1474592 | tf_op jit(solution)/shard_map/all_to_all | solution.py:75
  63.5 1.3 reshape.126
  64.8 2.8 %fusion.85 = (bf16[384,1920]{1,0:T(8,128)(2,1)S(1)}, f32[384,1920]{1,0:T(8,128)S(1)}) fusion(bf16[384,1920]{1,0:T(8,128)(2,1)} %reshape.126, f32[]{:T(128)} %bitcast.1, f32[]{:T(128)} %bitcast, s32[384]{0:T(512)S(1)} %add.105, pred[384]{0:T(512)(128)(4,1)S(1)} %lt.73, pred[384]{0:T(512)(128)(4,1)S(1)} %iota_compare_fusion.12), kind=kOutput, calls=%fused_computation.126 | convolution fusion | flops 570359808 | bytes 5900552 | tf_op jit(solution)/shard_map/dot_general | solution.py:25
  67.6 0.1 slice.87
  67.7 1.8 fusion.88
  69.5 0.3 collective-permute-start
  69.8 0.4 convolution_reduce_fusion
  70.2 1.7 fusion.9
  71.9 0.1 fusion.27
  72.1 0.9 copy-done.2
  73.0 0.0 reduce-scatter.2.cloned.1.call-start
  73.1 0.6 collective-permute-start.2
  73.7 0.8 collective-permute-done.2
  74.5 38.0 %psum.7 = f32[1920]{0:T(1024)} all-reduce(f32[1920]{0:T(1024)S(1)} %add.114), channel_id=1, replica_groups=mesh['tmc'=16,'core'=2,'panel'=4] {'tmc'}, use_global_device_ids=true, to_apply=%region_6.7 | all-reduce | flops 1920 | bytes 15360 | tf_op jit(solution)/shard_map/psum | solution.py:101
  112.5 4.3 %all-gather.2.cloned.1.call-done = bf16[272,7680]{1,0:T(8,128)(2,1)} async-done(((bf16[272,1920]{1,0:T(8,128)(2,1)}), bf16[272,7680]{1,0:T(8,128)(2,1)}) %all-gather.2.cloned.1.call-update) | async-done | bytes 4177936 | tf_op jit(solution)/shard_map/all_gather | solution.py:100
  116.8 0.1 slice.93
  116.9 0.1 slice.94
  117.0 0.1 fusion.43
  117.1 3.4 %fusion.46 = f32[128,7680]{1,0:T(8,128)S(1)} fusion(bf16[272,7680]{1,0:T(8,128)(2,1)} %all-gather.2.cloned.1.call-done, bf16[128,544]{1,0:T(8,128)(2,1)S(1)} %fusion.43), kind=kOutput, calls=%fused_computation.70 | convolution fusion | flops 534773760 | bytes 8208384 | tf_op jit(solution)/shard_map/dot_general | solution.py:122
  120.4 3.8 %collective-permute-done.3 = bf16[272,7680]{1,0:T(8,128)(2,1)} collective-permute-done((bf16[272,7680]{1,0:T(8,128)(2,1)}, bf16[272,7680]{1,0:T(8,128)(2,1)}, u32[]{:S(2)}, u32[]{:S(2)}) %collective-permute-start.3) | collective-permute-done | bytes 4177952 | tf_op jit(solution)/shard_map/ppermute | solution.py:104
  124.3 3.4 %fusion.86 = (bf16[128,7680]{1,0:T(8,128)(2,1)S(1)}, bf16[128,7680]{1,0:T(8,128)(2,1)S(1)}) fusion(f32[128,7680]{1,0:T(8,128)S(1)} %fusion.46, bf16[272,7680]{1,0:T(8,128)(2,1)} %collective-permute-done.3, bf16[128,544]{1,0:T(8,128)(2,1)S(1)} %fusion.43), kind=kOutput, calls=%fused_computation.127 | convolution fusion | flops 537722880 | bytes 12140544 | tf_op jit(solution)/shard_map/dot_general | solution.py:123
  127.7 18.1 %multiply_convert_fusion = bf16[7680,960]{1,0:T(8,128)(2,1)} fusion(bf16[272,7680]{1,0:T(8,128)(2,1)} %collective-permute-done.3, bf16[272,7680]{1,0:T(8,128)(2,1)S(1)} %copy-done.1, bf16[128,7680]{1,0:T(8,128)(2,1)S(1)} %get-tuple-element.38, s32[]{:T(128)S(6)} %select_n.64, bf16[128,7680]{1,0:T(8,128)(2,1)S(1)} %get-tuple-element.39), kind=kOutput, calls=%fused_computation | convolution fusion | flops 9958625280 | bytes 35389444 | tf_op jit(solution)/shard_map/dot_general | solution.py:130
  145.9 108.0 %reduce-scatter.2.cloned.1.call-done = bf16[480,960]{1,0:T(8,128)(2,1)} async-done(((bf16[7680,960]{1,0:T(8,128)(2,1)}), bf16[480,960]{1,0:T(8,128)(2,1)}) %reduce-scatter.2.cloned.1.call-update) | async-done | bytes 921616 | tf_op jit(solution)/shard_map/reduce_scatter | solution.py:133
  253.8 1.2 broadcast_select_fusion.2
  255.1 0.1 collective-permute-start.4
  255.2 1.9 collective-permute-done.4
  257.0 1.3 broadcast_select_fusion.1
  258.3 1.5 maximum_convert_fusion
  (25 shorter events, 0.3 us)
Async XLA Ops:
  7.2 15.0 %copy-start = (bf16[256,1920]{1,0:T(8,128)(2,1)S(1)}, bf16[256,1920]{1,0:T(8,128)(2,1)}, u32[]{:S(2)}) copy-start(bf16[256,1920]{1,0:T(8,128)(2,1)} %param.8) | copy-start | bytes 2949124
  7.2 16.3 %copy-start.3 = (f32[32]{0:T(128)S(1)}, f32[32]{0:T(128)}, u32[]{:S(2)}) copy-start(f32[32]{0:T(128)} %param.13) | copy-start | bytes 388
  7.2 17.6 %copy-start.4 = (f32[32]{0:T(128)S(1)}, f32[32]{0:T(128)}, u32[]{:S(2)}) copy-start(f32[32]{0:T(128)} %param.12) | copy-start | bytes 388
  13.1 15.7 %all-to-all-start = ((bf16[32,2,390]{2,1,0:T(2,128)(2,1)}), bf16[32,2,390]{2,1,0:T(2,128)(2,1)S(1)}, u32[]{:S(2)}, u32[]{:S(2)}) async-start(bf16[32,2,390]{2,1,0:T(2,128)(2,1)} %reshape.152), calls=%async_computation | async-start | bytes 131072 | tf_op jit(solution)/shard_map/all_to_all | solution.py:73
  29.0 34.5 %all-to-all-start.1 = ((bf16[32,12,1920]{2,1,0:T(8,128)(2,1)}), bf16[32,12,1920]{2,1,0:T(8,128)(2,1)S(1)}, u32[]{:S(2)}, u32[]{:S(2)}) async-start(bf16[32,12,1920]{2,1,0:T(8,128)(2,1)} %reshape.124), calls=%async_computation.1 | async-start | bytes 3932160 | tf_op jit(solution)/shard_map/all_to_all | solution.py:75
  36.0 80.8 %all-gather.2.cloned.1.call-start = ((), (), s32[]{:S(2)}) async-start(), calls=%async_computation.3 | async-start | bytes 5222400 | tf_op jit(solution)/shard_map/all_gather | solution.py:100
  49.8 22.3 %collective-permute-start.1 = (bf16[64,384]{1,0:T(8,128)(2,1)S(1)}, bf16[64,384]{1,0:T(8,128)(2,1)S(1)}, u32[]{:S(2)}, u32[]{:S(2)}) collective-permute-start(bf16[64,384]{1,0:T(8,128)(2,1)S(1)} %get-tuple-element.33), channel_id=1, source_target_pairs={{0,4},{4,0},{1,5},{5,1},{2,6},{6,2},{3,7},{7,3},{8,12},{12,8},{9,1... | collective-permute-start | bytes 147464 | tf_op jit(solution)/shard_map/ppermute | solution.py:98
  69.5 2.4 collective-permute-start
  72.0 1.0 copy-start.2
  73.0 180.8 %reduce-scatter.2.cloned.1.call-start = ((), (), s32[]{:S(2)}) async-start(), calls=%async_computation.4 | async-start | bytes 16711680 | tf_op jit(solution)/shard_map/reduce_scatter | solution.py:133
  73.1 1.4 collective-permute-start.2
  116.8 7.5 %collective-permute-start.3 = (bf16[272,7680]{1,0:T(8,128)(2,1)}, bf16[272,7680]{1,0:T(8,128)(2,1)}, u32[]{:S(2)}, u32[]{:S(2)}) collective-permute-start(bf16[272,7680]{1,0:T(8,128)(2,1)} %all-gather.2.cloned.1.call-done), channel_id=1, source_target_pairs={{0,4},{4,0},{1,5},{5,1},{2,6},{6,2},{3,7},{7,3},{8,12},{12,8},{9,1... | collective-permute-start | bytes 12533768 | tf_op jit(solution)/shard_map/ppermute | solution.py:104
  120.4 7.3 %copy-start.1 = (bf16[272,7680]{1,0:T(8,128)(2,1)S(1)}, bf16[272,7680]{1,0:T(8,128)(2,1)}, u32[]{:S(2)}) copy-start(bf16[272,7680]{1,0:T(8,128)(2,1)} %all-gather.2.cloned.1.call-done) | copy-start | bytes 12533764
  255.1 1.9 collective-permute-start.4
Sparse Core Ops, SparseCore 0:
  73.2 43.6 all-gather.1
  146.0 107.8 reduce-scatter.1

commit v20 on v19

--- a/solution.py
+++ b/solution.py
@@ -68,13 +68,17 @@
         return picked.astype(values.dtype)
 
     send_design = pick_rows(design).reshape(tile_count, capacity, panel_width)
-    with_obs = jnp.concatenate([partials, observed[:, None]], axis=1)
-    send_params = pick_rows(with_obs).reshape(tile_count, capacity, param_count + 1)
+    lane_width = -(-(param_count + 1) // 128) * 128
+    with_obs = jnp.concatenate(
+        [partials, observed[:, None], jnp.zeros((rows_dev, lane_width - param_count - 1), partials.dtype)],
+        axis=1,
+    )
+    send_params = pick_rows(with_obs).reshape(tile_count, capacity, lane_width)
     got_params = lax.all_to_all(send_params, TM, split_axis=0, concat_axis=0, tiled=True)
     send_design, got_params = lax.optimization_barrier((send_design, got_params))
     got_design = lax.all_to_all(send_design, TM, split_axis=0, concat_axis=0, tiled=True)
     got_design = got_design.reshape(slot_count, panel_width)
-    got_params = got_params.reshape(slot_count, param_count + 1)
+    got_params = got_params.reshape(slot_count, lane_width)
     got_obs = got_params[:, param_count]
     got_params = got_params[:, :param_count]
     per_source = jnp.sum((epoch_table == device_index).astype(jnp.int32), axis=0)

time: 269 us -> 269 us (level)
  transfers between devices with their start and end apart: 9 -> 9, of which waited for: 7 -> 6; matrix products, arithmetic and copies ran while one was open for 12% -> 12% of each run, Pallas kernels for 0% -> 0%
where the time goes in v20:
time: 269 us; the launch traced here: 267 us
  waiting for transfers between devices  131 us (49%)
  blocking collectives  38 us (14%)
  matrix products  35.3 us (13%)
  other arithmetic  20.3 us (8%)
  starting transfers between devices  16.9 us (6%)
  between operations  16.1 us (6%)
  local copies, waits for them, and re-layouts  9.26 us (3%)
    reduce_scatter x1, waiting for transfers between devices, body(): lax.psum_scatter((product * scale).astype(jnp.bfloat16), 'tmc', scatter_d...  108 us
    psum x1, blocking collectives, body(): lax.psum(right_part + lax.ppermute(right_part, 'core', swap), 'tmc')  38 us
    dot_general x1, matrix products, body(): lax.dot_general(row_side, col_side, (((0,), (0,)), ((), ())), preferred_e...  18.1 us
    all_to_all x1, waiting for transfers between devices, body(): lax.all_to_all(send_design, TM, split_axis=0, concat_axis=0, tiled=True)  12.6 us
    all_to_all x1, starting transfers between devices, body(): lax.all_to_all(send_params, TM, split_axis=0, concat_axis=0, tiled=True)  8.16 us
    all_to_all x1, starting transfers between devices, body(): lax.all_to_all(send_design, TM, split_axis=0, concat_axis=0, tiled=True)  7.4 us
    another operation x3, other arithmetic, eliminate(): factor = jnp.linalg.cholesky(param_gram)  6.52 us
    another operation x2, other arithmetic, eliminate(): lax.linalg.triangular_solve(factor, white_params.T, left_side=True, lower...  5.55 us
  transfers between devices with their start and end apart: 9, of which 6 were waited for; matrix products, arithmetic and copies ran while one was open for 12% of the time, Pallas kernels for 0%

profile of v20, /device:TPU:24, one launch (start us, length us, event | category | flops | bytes accessed | tf_op | source)
XLA Modules:
  0.0 267.3 jit_solution(6818571111994419504)
XLA Ops:
  7.2 0.7 broadcast_in_dim.14
  7.9 0.5 broadcast.175
  8.4 2.3 fusion.54
  10.7 0.1 reshape_squeeze.3
  10.8 0.2 dynamic-slice_reduce_fusion
  11.0 0.2 convert_reduce_fusion
  11.2 0.1 pad.27.clone
  11.3 1.0 convolution_convert_fusion.1
  12.3 0.7 reshape.125
  13.0 8.2 %all-to-all-start = ((bf16[32,12,128]{2,1,0:T(8,128)(2,1)}), bf16[32,12,128]{2,1,0:T(8,128)(2,1)S(1)}, u32[]{:S(2)}, u32[]{:S(2)}) async-start(bf16[32,12,128]{2,1,0:T(8,128)(2,1)} %reshape.125), calls=%async_computation | async-start | bytes 262144 | tf_op jit(solution)/shard_map/all_to_all | solution.py:77
  21.2 0.1 convert_reduce_fusion.1
  21.2 1.2 dynamic_slice.13
  23.1 1.3 dynamic_slice.12
  25.5 0.7 and_select_fusion
  26.2 0.1 broadcast_add_fusion
  26.3 0.1 add.105
  26.4 0.1 iota_compare_fusion.11
  26.5 0.1 lt.73
  26.6 0.6 convolution_convert_fusion
  27.2 1.5 reshape.124
  28.7 0.6 iota_compare_fusion.12
  29.3 7.4 %all-to-all-start.1 = ((bf16[32,12,1920]{2,1,0:T(8,128)(2,1)}), bf16[32,12,1920]{2,1,0:T(8,128)(2,1)S(1)}, u32[]{:S(2)}, u32[]{:S(2)}) async-start(bf16[32,12,1920]{2,1,0:T(8,128)(2,1)} %reshape.124), calls=%async_computation.1 | async-start | bytes 3932160 | tf_op jit(solution)/shard_map/all_to_all | solution.py:79
  36.7 0.0 all-gather.2.cloned.1.call-start
  36.8 0.7 fusion.34
  37.5 0.2 fusion.89
  37.7 0.2 slice_reduce_fusion
  37.9 0.1 copy.10
  38.0 5.8 %cholesky.17 = f32[64,64]{1,0:T(8,128)S(1)} custom-call(f32[64,64]{1,0:T(8,128)S(1)} %fusion.60), custom_call_target="Cholesky" | custom-call | tf_op jit(solution)/shard_map/jit(cholesky)/cholesky | solution.py:32
  43.9 0.6 compare_reduce_fusion
  44.6 0.7 fusion.53
  45.2 4.9 %custom-call.6 = f32[1,64,64]{1,2,0:T(8,128)S(1)} custom-call(f32[1,64,64]{2,1,0:T(8,128)S(1)} %fusion.53), custom_call_target="InvertDiagBlocksLowerTriangular" | custom-call | tf_op jit(solution)/shard_map/triangular_solve | solution.py:33
  50.1 0.3 fusion.86
  50.4 0.4 collective-permute-start.1
  50.8 0.6 convolution_bitcast_fusion
  51.4 0.2 convolution_bitcast_fusion.1
  51.6 12.6 %all-to-all-done.1 = bf16[32,12,1920]{2,1,0:T(8,128)(2,1)S(1)} async-done(((bf16[32,12,1920]{2,1,0:T(8,128)(2,1)}), bf16[32,12,1920]{2,1,0:T(8,128)(2,1)S(1)}, u32[]{:S(2)}, u32[]{:S(2)}) %all-to-all-start.1) | async-done | bytes 1474592 | tf_op jit(solution)/shard_map/all_to_all | solution.py:79
  64.2 1.3 reshape.126
  65.5 2.8 %fusion.87 = (bf16[384,1920]{1,0:T(8,128)(2,1)S(1)}, f32[384,1920]{1,0:T(8,128)S(1)}) fusion(bf16[384,1920]{1,0:T(8,128)(2,1)} %reshape.126, f32[]{:T(128)} %bitcast.1, f32[]{:T(128)} %bitcast, s32[384]{0:T(512)S(1)} %add.105, pred[384]{0:T(512)(128)(4,1)S(1)} %lt.73, pred[384]{0:T(512)(128)(4,1)S(1)} %iota_compare_fusion.12), kind=kOutput, calls=%fused_computation.128 | convolution fusion | flops 570359808 | bytes 5900552 | tf_op jit(solution)/shard_map/dot_general | solution.py:25
  68.3 0.1 slice.87
  68.4 1.8 fusion.90
  70.2 0.3 collective-permute-start
  70.5 0.4 convolution_reduce_fusion
  70.9 1.7 fusion.9
  72.6 0.1 fusion.27
  72.8 0.9 copy-done.2
  73.7 0.0 all-gather.2.cloned.1.call-update
  73.7 0.0 reduce-scatter.2.cloned.1.call-start
  73.8 0.6 collective-permute-start.2
  74.3 0.8 collective-permute-done.2
  75.2 38.0 %psum.7 = f32[1920]{0:T(1024)} all-reduce(f32[1920]{0:T(1024)S(1)} %add.114), channel_id=1, replica_groups=mesh['tmc'=16,'core'=2,'panel'=4] {'tmc'}, use_global_device_ids=true, to_apply=%region_6.7 | all-reduce | flops 1920 | bytes 15360 | tf_op jit(solution)/shard_map/psum | solution.py:105
  113.2 4.3 %all-gather.2.cloned.1.call-done = bf16[272,7680]{1,0:T(8,128)(2,1)} async-done(((bf16[272,1920]{1,0:T(8,128)(2,1)}), bf16[272,7680]{1,0:T(8,128)(2,1)}) %all-gather.2.cloned.1.call-update) | async-done | bytes 4177936 | tf_op jit(solution)/shard_map/all_gather | solution.py:104
  117.5 0.1 slice.93
  117.6 0.1 slice.94
  117.6 0.1 fusion.43
  117.8 3.4 %fusion.46 = f32[128,7680]{1,0:T(8,128)S(1)} fusion(bf16[272,7680]{1,0:T(8,128)(2,1)} %all-gather.2.cloned.1.call-done, bf16[128,544]{1,0:T(8,128)(2,1)S(1)} %fusion.43), kind=kOutput, calls=%fused_computation.70 | convolution fusion | flops 534773760 | bytes 8208384 | tf_op jit(solution)/shard_map/dot_general | solution.py:126
  121.1 3.8 %collective-permute-done.3 = bf16[272,7680]{1,0:T(8,128)(2,1)} collective-permute-done((bf16[272,7680]{1,0:T(8,128)(2,1)}, bf16[272,7680]{1,0:T(8,128)(2,1)}, u32[]{:S(2)}, u32[]{:S(2)}) %collective-permute-start.3) | collective-permute-done | bytes 4177952 | tf_op jit(solution)/shard_map/ppermute | solution.py:108
  125.0 3.4 %fusion.88 = (bf16[128,7680]{1,0:T(8,128)(2,1)S(1)}, bf16[128,7680]{1,0:T(8,128)(2,1)S(1)}) fusion(f32[128,7680]{1,0:T(8,128)S(1)} %fusion.46, bf16[272,7680]{1,0:T(8,128)(2,1)} %collective-permute-done.3, bf16[128,544]{1,0:T(8,128)(2,1)S(1)} %fusion.43), kind=kOutput, calls=%fused_computation.129 | convolution fusion | flops 537722880 | bytes 12140544 | tf_op jit(solution)/shard_map/dot_general | solution.py:127
  128.4 18.1 %multiply_convert_fusion = bf16[7680,960]{1,0:T(8,128)(2,1)} fusion(bf16[272,7680]{1,0:T(8,128)(2,1)} %collective-permute-done.3, bf16[272,7680]{1,0:T(8,128)(2,1)S(1)} %copy-done.1, bf16[128,7680]{1,0:T(8,128)(2,1)S(1)} %get-tuple-element.38, s32[]{:T(128)S(6)} %select_n.64, bf16[128,7680]{1,0:T(8,128)(2,1)S(1)} %get-tuple-element.39), kind=kOutput, calls=%fused_computation | convolution fusion | flops 9958625280 | bytes 35389444 | tf_op jit(solution)/shard_map/dot_general | solution.py:134
  146.6 108.0 %reduce-scatter.2.cloned.1.call-done = bf16[480,960]{1,0:T(8,128)(2,1)} async-done(((bf16[7680,960]{1,0:T(8,128)(2,1)}), bf16[480,960]{1,0:T(8,128)(2,1)}) %reduce-scatter.2.cloned.1.call-update) | async-done | bytes 921616 | tf_op jit(solution)/shard_map/reduce_scatter | solution.py:137
  254.6 1.2 broadcast_select_fusion.2
  255.8 0.1 collective-permute-start.4
  255.9 1.9 collective-permute-done.4
  257.7 1.3 broadcast_select_fusion.1
  259.0 1.5 maximum_convert_fusion
  (20 shorter events, 0.2 us)
Async XLA Ops:
  7.2 19.4 %copy-start = (bf16[256,1920]{1,0:T(8,128)(2,1)S(1)}, bf16[256,1920]{1,0:T(8,128)(2,1)}, u32[]{:S(2)}) copy-start(bf16[256,1920]{1,0:T(8,128)(2,1)} %param.8) | copy-start | bytes 2949124
  13.0 16.3 %all-to-all-start = ((bf16[32,12,128]{2,1,0:T(8,128)(2,1)}), bf16[32,12,128]{2,1,0:T(8,128)(2,1)S(1)}, u32[]{:S(2)}, u32[]{:S(2)}) async-start(bf16[32,12,128]{2,1,0:T(8,128)(2,1)} %reshape.125), calls=%async_computation | async-start | bytes 262144 | tf_op jit(solution)/shard_map/all_to_all | solution.py:77
  29.3 34.9 %all-to-all-start.1 = ((bf16[32,12,1920]{2,1,0:T(8,128)(2,1)}), bf16[32,12,1920]{2,1,0:T(8,128)(2,1)S(1)}, u32[]{:S(2)}, u32[]{:S(2)}) async-start(bf16[32,12,1920]{2,1,0:T(8,128)(2,1)} %reshape.124), calls=%async_computation.1 | async-start | bytes 3932160 | tf_op jit(solution)/shard_map/all_to_all | solution.py:79
  36.7 80.8 %all-gather.2.cloned.1.call-start = ((), (), s32[]{:S(2)}) async-start(), calls=%async_computation.3 | async-start | bytes 5222400 | tf_op jit(solution)/shard_map/all_gather | solution.py:104
  50.4 22.3 %collective-permute-start.1 = (bf16[64,384]{1,0:T(8,128)(2,1)S(1)}, bf16[64,384]{1,0:T(8,128)(2,1)S(1)}, u32[]{:S(2)}, u32[]{:S(2)}) collective-permute-start(bf16[64,384]{1,0:T(8,128)(2,1)S(1)} %get-tuple-element.33), channel_id=1, source_target_pairs={{0,4},{4,0},{1,5},{5,1},{2,6},{6,2},{3,7},{7,3},{8,12},{12,8},{9,1... | collective-permute-start | bytes 147464 | tf_op jit(solution)/shard_map/ppermute | solution.py:102
  70.2 2.4 collective-permute-start
  72.7 1.0 copy-start.2
  73.7 180.8 %reduce-scatter.2.cloned.1.call-start = ((), (), s32[]{:S(2)}) async-start(), calls=%async_computation.4 | async-start | bytes 16711680 | tf_op jit(solution)/shard_map/reduce_scatter | solution.py:137
  73.8 1.4 collective-permute-start.2
  117.5 7.5 %collective-permute-start.3 = (bf16[272,7680]{1,0:T(8,128)(2,1)}, bf16[272,7680]{1,0:T(8,128)(2,1)}, u32[]{:S(2)}, u32[]{:S(2)}) collective-permute-start(bf16[272,7680]{1,0:T(8,128)(2,1)} %all-gather.2.cloned.1.call-done), channel_id=1, source_target_pairs={{0,4},{4,0},{1,5},{5,1},{2,6},{6,2},{3,7},{7,3},{8,12},{12,8},{9,1... | collective-permute-start | bytes 12533768 | tf_op jit(solution)/shard_map/ppermute | solution.py:108
  121.1 7.3 %copy-start.1 = (bf16[272,7680]{1,0:T(8,128)(2,1)S(1)}, bf16[272,7680]{1,0:T(8,128)(2,1)}, u32[]{:S(2)}) copy-start(bf16[272,7680]{1,0:T(8,128)(2,1)} %all-gather.2.cloned.1.call-done) | copy-start | bytes 12533764
  255.8 1.9 collective-permute-start.4
Sparse Core Ops, SparseCore 0:
  73.8 43.6 all-gather.1
  146.7 107.8 reduce-scatter.1
